TPU v7x, 32 devices: a whole 2x2x4 slice. The times are simulated.
32 devices in a mesh: fsdp: 8 (over z, y), rep: 4 (over x, core).
Axes of the slice: x: 2, y: 2, z: 4, core: 2. Of those that a mesh axis runs over, the one named last changes fastest.
Arguments:
- layer_input: bfloat16 [64, 512, 768], P(('fsdp', 'rep')), may hold values from -6 to 6
- segment_ids: int32 [64, 512], P(('fsdp', 'rep')), may hold values from 0 to 511, as said below
- joint_weight: bfloat16 [768, 2304], P('fsdp'), may hold values from -0.21875 to 0.21875
- query_bias: bfloat16 [768], replicated, may hold values from -3 to 3
- value_bias: bfloat16 [768], replicated, may hold values from -3 to 3
- close_weight: bfloat16 [768, 768], P('fsdp'), may hold values from -0.875 to 0.875
- close_bias: bfloat16 [768], replicated, may hold values from -3 to 3
- first_gain: bfloat16 [768], replicated, may hold values from 0.099609375 to 1.8984375
- first_shift: bfloat16 [768], replicated, may hold values from -3 to 3
- expand_weight: bfloat16 [768, 3072], P('fsdp'), may hold values from -0.21875 to 0.21875
- expand_bias: bfloat16 [3072], replicated, may hold values from -3 to 3
- shrink_weight: bfloat16 [3072, 768], P('fsdp'), may hold values from -0.109375 to 0.109375
- shrink_bias: bfloat16 [768], replicated, may hold values from -3 to 3
- second_gain: bfloat16 [768], replicated, may hold values from 0.099609375 to 1.8984375
- second_shift: bfloat16 [768], replicated, may hold values from -3 to 3
- cotangent: bfloat16 [64, 512, 768], P(('fsdp', 'rep')), may hold values from -6 to 6
Outputs:
- layer_output: bfloat16 [64, 512, 768], P(('fsdp', 'rep'))
- input_grad: float32 [64, 512, 768], P(('fsdp', 'rep'))
- joint_grad: float32 [768, 2304], P('fsdp')
- query_bias_grad: float32 [768], replicated
- value_bias_grad: float32 [768], replicated
- close_grad: float32 [768, 768], P('fsdp')
- close_bias_grad: float32 [768], replicated
- first_gain_grad: float32 [768], replicated
- first_shift_grad: float32 [768], replicated
- expand_grad: float32 [768, 3072], P('fsdp')
- expand_bias_grad: float32 [3072], replicated
- shrink_grad: float32 [3072, 768], P('fsdp')
- shrink_bias_grad: float32 [768], replicated
- second_gain_grad: float32 [768], replicated
- second_shift_grad: float32 [768], replicated
Inputs may be any that keep to these rules, and one draw needn't show every extreme that they name: `segment_ids`: along each packed row of 512 positions the document numbers start at 0, never fall and rise by at most one from a position to the next; every position belongs to a document. Some row holds 512 documents of one position.
All inputs are finite; a program needn't handle non-finite values.
Results may differ from a plain program's by a relative error of at most 0.015.
Values may be sent and summed in bfloat16 or wider, within the bound.
No kernel may reach another device: no remote copies, remote signals or barrier semaphores. Data moves between devices by JAX's collectives and lax.ppermute only.
A program may use at most 192 MiB of HBM per device.

v0:
```python
import math

import jax
import jax.numpy as jnp
from jax import lax
from jax.sharding import PartitionSpec as P

HEADS = 12


EPS = 1e-12


def layer_norm(values, gain, shift):
    average = jnp.mean(values, axis=-1, keepdims=True)
    centred = values - average
    variance = jnp.mean(centred * centred, axis=-1, keepdims=True)
    return centred * lax.rsqrt(variance + EPS) * gain + shift


def gelu_exact(values):
    return jax.nn.gelu(values, approximate=False)


def split_heads(packed):
    pos_count = packed.shape[0]
    model_width = packed.shape[1] // 3
    head_size = model_width // HEADS
    queries = packed[:, :model_width].reshape(pos_count, HEADS, head_size)
    keys_part = packed[:, model_width : 2 * model_width].reshape(pos_count, HEADS, head_size)
    values_part = packed[:, 2 * model_width :].reshape(pos_count, HEADS, head_size)
    return (queries, keys_part, values_part, 1.0 / math.sqrt(head_size))


def masked_scores(queries, keys_part, segments, score_scale):
    scores = (
        jnp.einsum("qhd,khd->hqk", queries, keys_part, preferred_element_type=jnp.float32)
        * score_scale
    )
    same_doc = segments[:, None] == segments[None, :]
    return jnp.where(same_doc[None], scores, -jnp.inf)


def attend_row(packed, segments):
    queries, keys_part, values_part, score_scale = split_heads(packed)
    scores = masked_scores(queries, keys_part, segments, score_scale)
    top_score = jnp.max(scores, axis=-1, keepdims=True)
    raised = jnp.exp(scores - top_score)
    denominator = jnp.sum(raised, axis=-1, keepdims=True)
    attn_low = (raised / denominator).astype(jnp.bfloat16)
    context = jnp.einsum("hqk,khd->qhd", attn_low, values_part, preferred_element_type=jnp.float32)
    return (
        context.reshape(packed.shape[0], packed.shape[1] // 3),
        top_score + jnp.log(denominator),
    )


def attend_back(packed, segments, log_total, grad_context):
    pos_count = packed.shape[0]
    model_width = packed.shape[1] // 3
    queries, keys_part, values_part, score_scale = split_heads(packed)
    scores = masked_scores(queries, keys_part, segments, score_scale)
    attn_weights = jnp.exp(scores - log_total)
    grad_heads = grad_context.reshape(pos_count, HEADS, model_width // HEADS)
    grad_attn = jnp.einsum(
        "qhd,khd->hqk", grad_heads, values_part, preferred_element_type=jnp.float32
    )
    inner_sum = jnp.sum(grad_attn * attn_weights, axis=-1, keepdims=True)
    grad_scores = (attn_weights * (grad_attn - inner_sum)).astype(jnp.bfloat16)
    grad_queries = (
        jnp.einsum("hqk,khd->qhd", grad_scores, keys_part, preferred_element_type=jnp.float32)
        * score_scale
    )
    grad_keys = (
        jnp.einsum("hqk,qhd->khd", grad_scores, queries, preferred_element_type=jnp.float32)
        * score_scale
    )
    grad_values = jnp.einsum(
        "hqk,qhd->khd",
        attn_weights.astype(jnp.bfloat16),
        grad_heads,
        preferred_element_type=jnp.float32,
    )
    return jnp.concatenate(
        [
            grad_queries.reshape(pos_count, model_width),
            grad_keys.reshape(pos_count, model_width),
            grad_values.reshape(pos_count, model_width),
        ],
        axis=1,
    )


def body(
    layer_input,
    segment_ids,
    joint_weight,
    query_bias,
    value_bias,
    close_weight,
    close_bias,
    first_gain,
    first_shift,
    expand_weight,
    expand_bias,
    shrink_weight,
    shrink_bias,
    second_gain,
    second_shift,
    cotangent,
):
    row_count, pos_count, model_width = layer_input.shape
    tok_count = row_count * pos_count
    flat_input = layer_input.reshape(tok_count, model_width)
    joint_full, close_full = (
        lax.all_gather(joint_weight, "fsdp", axis=0, tiled=True),
        lax.all_gather(close_weight, "fsdp", axis=0, tiled=True),
    )
    joint_bias = jnp.concatenate([query_bias, jnp.zeros_like(query_bias), value_bias]).astype(
        jnp.float32
    )
    mixed = jnp.dot(flat_input, joint_full, preferred_element_type=jnp.float32) + joint_bias
    joint_low = mixed.astype(jnp.bfloat16).reshape(row_count, pos_count, 3 * model_width)
    context, log_total = lax.map(
        lambda packet: attend_row(packet[0], packet[1]), (joint_low, segment_ids)
    )
    context_low = context.reshape(tok_count, model_width).astype(jnp.bfloat16)
    expand_full, shrink_full = (
        lax.all_gather(expand_weight, "fsdp", axis=0, tiled=True),
        lax.all_gather(shrink_weight, "fsdp", axis=0, tiled=True),
    )
    branch = jnp.dot(
        context_low, close_full, preferred_element_type=jnp.float32
    ) + close_bias.astype(jnp.float32)
    first_sum = flat_input.astype(jnp.float32) + branch
    hidden, first_pull = jax.vjp(
        layer_norm, first_sum, first_gain.astype(jnp.float32), first_shift.astype(jnp.float32)
    )
    hidden_low = hidden.astype(jnp.bfloat16)
    inner = jnp.dot(
        hidden_low, expand_full, preferred_element_type=jnp.float32
    ) + expand_bias.astype(jnp.float32)
    active, gelu_pull = jax.vjp(gelu_exact, inner)
    active_low = active.astype(jnp.bfloat16)
    ffn_out = jnp.dot(
        active_low, shrink_full, preferred_element_type=jnp.float32
    ) + shrink_bias.astype(jnp.float32)
    output, second_pull = jax.vjp(
        layer_norm,
        hidden + ffn_out,
        second_gain.astype(jnp.float32),
        second_shift.astype(jnp.float32),
    )
    layer_output = output.astype(jnp.bfloat16).reshape(row_count, pos_count, model_width)
    expand_back, shrink_back = (
        lax.all_gather(expand_weight, "fsdp", axis=0, tiled=True),
        lax.all_gather(shrink_weight, "fsdp", axis=0, tiled=True),
    )
    grad_second, second_gain_part, second_shift_part = second_pull(
        cotangent.reshape(tok_count, model_width).astype(jnp.float32)
    )
    grad_ffn = grad_second.astype(jnp.bfloat16)
    shrink_term = jnp.einsum("tf,td->fd", active_low, grad_ffn, preferred_element_type=jnp.float32)
    grad_active = jnp.einsum("td,fd->tf", grad_ffn, shrink_back, preferred_element_type=jnp.float32)
    grad_inner = gelu_pull(grad_active)[0].astype(jnp.bfloat16)
    expand_term = jnp.einsum(
        "td,tf->df", hidden_low, grad_inner, preferred_element_type=jnp.float32
    )
    grad_hidden = grad_second + jnp.einsum(
        "tf,df->td", grad_inner, expand_back, preferred_element_type=jnp.float32
    )
    expand_part, shrink_part = (
        lax.psum_scatter(expand_term, "fsdp", scatter_dimension=0, tiled=True),
        lax.psum_scatter(shrink_term, "fsdp", scatter_dimension=0, tiled=True),
    )
    grad_first, first_gain_part, first_shift_part = first_pull(grad_hidden)
    grad_branch = grad_first.astype(jnp.bfloat16)
    joint_back, close_back = (
        lax.all_gather(joint_weight, "fsdp", axis=0, tiled=True),
        lax.all_gather(close_weight, "fsdp", axis=0, tiled=True),
    )
    close_term = jnp.einsum(
        "td,te->de", context_low, grad_branch, preferred_element_type=jnp.float32
    )
    grad_context = jnp.einsum(
        "te,de->td", grad_branch, close_back, preferred_element_type=jnp.float32
    ).astype(jnp.bfloat16)
    grad_mixed = lax.map(
        lambda packet: attend_back(packet[0], packet[1], packet[2], packet[3]),
        (
            joint_low,
            segment_ids,
            log_total,
            grad_context.reshape(row_count, pos_count, model_width),
        ),
    )
    grad_mixed_low = grad_mixed.reshape(tok_count, 3 * model_width).astype(jnp.bfloat16)
    joint_term = jnp.einsum(
        "td,te->de", flat_input, grad_mixed_low, preferred_element_type=jnp.float32
    )
    input_grad = grad_first + jnp.einsum(
        "te,de->td", grad_mixed_low, joint_back, preferred_element_type=jnp.float32
    )
    joint_part, close_part = (
        lax.psum_scatter(joint_term, "fsdp", scatter_dimension=0, tiled=True),
        lax.psum_scatter(close_term, "fsdp", scatter_dimension=0, tiled=True),
    )
    joint_grad, close_grad, expand_grad, shrink_grad = (
        lax.psum(joint_part.astype(jnp.bfloat16), "rep").astype(jnp.float32),
        lax.psum(close_part.astype(jnp.bfloat16), "rep").astype(jnp.float32),
        lax.psum(expand_part.astype(jnp.bfloat16), "rep").astype(jnp.float32),
        lax.psum(shrink_part.astype(jnp.bfloat16), "rep").astype(jnp.float32),
    )
    grad_mixed_wide = grad_mixed_low.astype(jnp.float32)
    vector_terms = (
        jnp.sum(grad_mixed_wide[:, :model_width], axis=0),
        jnp.sum(grad_mixed_wide[:, 2 * model_width :], axis=0),
        jnp.sum(grad_branch.astype(jnp.float32), axis=0),
        first_gain_part,
        first_shift_part,
        jnp.sum(grad_inner.astype(jnp.float32), axis=0),
        jnp.sum(grad_ffn.astype(jnp.float32), axis=0),
        second_gain_part,
        second_shift_part,
    )
    (
        query_bias_grad,
        value_bias_grad,
        close_bias_grad,
        first_gain_grad,
        first_shift_grad,
        expand_bias_grad,
        shrink_bias_grad,
        second_gain_grad,
        second_shift_grad,
    ) = lax.psum(
        (
            vector_terms[0],
            vector_terms[1],
            vector_terms[2],
            vector_terms[3],
            vector_terms[4],
            vector_terms[5],
            vector_terms[6],
            vector_terms[7],
            vector_terms[8],
        ),
        ("fsdp", "rep"),
    )
    return (
        layer_output,
        input_grad.reshape(row_count, pos_count, model_width),
        joint_grad,
        query_bias_grad,
        value_bias_grad,
        close_grad,
        close_bias_grad,
        first_gain_grad,
        first_shift_grad,
        expand_grad,
        expand_bias_grad,
        shrink_grad,
        shrink_bias_grad,
        second_gain_grad,
        second_shift_grad,
    )


def solution(mesh):
    placed = (
        P(("fsdp", "rep"), None, None),
        P(("fsdp", "rep"), None),
        P("fsdp", None),
        P(),
        P(),
        P("fsdp", None),
        P(),
        P(),
        P(),
        P("fsdp", None),
        P(),
        P("fsdp", None),
        P(),
        P(),
        P(),
        P(("fsdp", "rep"), None, None),
    )
    return jax.shard_map(
        body,
        mesh=mesh,
        in_specs=placed,
        out_specs=(
            P(("fsdp", "rep"), None, None),
            P(("fsdp", "rep"), None, None),
            P("fsdp", None),
            P(),
            P(),
            P("fsdp", None),
            P(),
            P(),
            P(),
            P("fsdp", None),
            P(),
            P("fsdp", None),
            P(),
            P(),
            P(),
        ),
        check_vma=False,
    )
```

profile of v0, /device:TPU:0, one launch (start us, length us, event | category | flops | bytes accessed | tf_op | source)
XLA Modules:
  0.0 939.9 jit_solution(8562727655183991149)
XLA Ops:
  19.7 57.8 %all-gather.5.cloned.1.call-done = bf16[768,2304]{1,0:T(8,128)(2,1)} async-done(((bf16[96,2304]{1,0:T(8,128)(2,1)}), bf16[768,2304]{1,0:T(8,128)(2,1)}) %all-gather.5.cloned.1.call-update) | async-done | bytes 3538960 | tf_op jit(solution)/shard_map/all_gather | solution.py:116
  77.5 8.4 add_convert_fusion.1
  86.0 6.8 copy.54
  92.8 23.4 %while.22 = (s32[]{:T(128)}, bf16[2,512,768]{2,1,0:T(8,128)(2,1)}, f32[2,12,512,1]{2,1,3,0:T(8,128)S(1)}, bf16[2,512,2304]{1,2,0:T(8,128)(2,1)}, s32[2,512]{1,0:T(2,128)S(1)}, /*index=5*/s32[]{:T(128)}) while((s32[]{:T(128)}, bf16[2,512,768]{2,1,0:T(8,128)(2,1)}, f32[2,12,512,1]{2,1,3,0:T(8,128)S(1)}, bf16[2,512,2304]{1,2,0:T(8,128)(2,1)}, ...), condition=%wide.region_3.4_spmd, body=%wide.region_0.3_spmd.sunk | while | flops 843311104 | bytes 54753372 | solution.py:124
  99.6 3.6 fusion.98
  111.3 3.6 fusion.98
  116.2 3.4 all-gather.7.cloned.1.call-done
  119.6 3.8 fusion.33
  124.0 75.9 %all-gather.9.cloned.1.call-done = bf16[768,3072]{1,0:T(8,128)(2,1)} async-done(((bf16[96,3072]{1,0:T(8,128)(2,1)}), bf16[768,3072]{1,0:T(8,128)(2,1)}) %all-gather.9.cloned.1.call-update) | async-done | bytes 4718608 | tf_op jit(solution)/shard_map/all_gather | solution.py:129
  199.8 36.0 %multiply_convert_fusion.1 = (bf16[1024,3072]{1,0:T(8,128)(2,1)}, f32[1024,3072]{1,0:T(8,128)}, f32[1024,3072]{1,0:T(8,128)}) fusion(f32[3072]{0:T(1024)S(1)} %copy-done.28, bf16[768,3072]{1,0:T(8,128)(2,1)} %all-gather.9.cloned.1.call-done, f32[1024,768]{1,0:T(8,128)S(1)} %get-tuple-element.220, f32[768]{0:T(1024)S(1)} %copy-done.19, ...), kind=kOutput, calls=%fused_computation.34 | convolution fusion | flops 5043388416 | bytes 39348224 | tf_op jit(solution)/shard_map/dot_general | solution.py:140
  235.8 43.8 %all-gather.11.cloned.1.call-done = bf16[3072,768]{1,0:T(8,128)(2,1)} async-done(((bf16[384,768]{1,0:T(8,128)(2,1)}), bf16[3072,768]{1,0:T(8,128)(2,1)}) %all-gather.11.cloned.1.call-update) | async-done | bytes 4718608 | tf_op jit(solution)/shard_map/all_gather | solution.py:130
  279.6 8.9 fusion.34
  295.5 19.4 %convert_reduce_fusion = (f32[3072]{0:T(1024)}, bf16[1024,3072]{1,0:T(8,128)(2,1)}) fusion(f32[1024,3072]{1,0:T(8,128)} %get-tuple-element.207, bf16[1024,768]{1,0:T(8,128)(2,1)} %get-tuple-element.199, bf16[3072,768]{1,0:T(8,128)(2,1)} %all-gather.11.cloned.1.call-done, f32[1024,3072]{1,0:T(8,128)} %get-tuple-element.221, f32[3072]{0:T(1024)S(1)} %copy-done.28), kind=kOutput, calls=%fused_computation.32 | convolution fusion | flops 4885312512 | bytes 37773312 | tf_op jit(solution)/shard_map/td,fd->tf/dot_general | solution.py:164
  315.0 10.1 %multiply_reduce_fusion.1 = (f32[768]{0:T(1024)}, f32[1024]{0:T(1024)S(1)}, f32[768]{0:T(1024)}, f32[1024,768]{1,0:T(8,128)S(1)}) fusion(f32[1024,768]{1,0:T(8,128)S(1)} %get-tuple-element.220, f32[1024]{0:T(1024)S(1)} %fusion.22, f32[1024]{0:T(1024)S(1)} %broadcast_multiply_fusion.1, f32[768]{0:T(1024)S(1)} %copy-done.15, ...), kind=kOutput, calls=%fused_computation.62 | convolution fusion | flops 4839699456 | bytes 20472832 | tf_op jit(solution)/shard_map/tf,df->td/dot_general | solution.py:169
  334.9 62.1 %while.23 = (s32[]{:T(128)}, bf16[2,512,2304]{2,1,0:T(8,128)(2,1)}, bf16[2,512,2304]{1,2,0:T(8,128)(2,1)}, s32[2,512]{1,0:T(2,128)S(1)}, f32[2,12,512,1]{2,1,3,0...) while((s32[]{:T(128)}, bf16[2,512,2304]{2,1,0:T(8,128)(2,1)}, ...), condition=%wide.region_14.15_spmd, body=%wide.region_12.14_spmd.sunk | while | flops 2069358592 | bytes 142784688 | solution.py:188
  339.5 3.2 fusion.111
  342.7 6.9 multiply_reduce_fusion.6
  349.5 7.1 multiply_convert_fusion.3
  362.5 3.3 constant_dynamic-update-slice_fusion.5
  373.4 6.9 multiply_reduce_fusion.6
  380.3 7.2 multiply_convert_fusion.3
  393.4 3.4 constant_dynamic-update-slice_fusion.5
  397.0 9.7 %convolution_bitcast_fusion = f32[768,2304]{0,1:T(8,128)} fusion(bf16[2,512,2304]{2,1,0:T(8,128)(2,1)} %get-tuple-element.77, bf16[2,512,768]{2,1,0:T(8,128)(2,1)} %param.20), kind=kOutput, calls=%fused_computation.49 | convolution fusion | flops 3623878656 | bytes 13369344 | tf_op jit(solution)/shard_map/td,te->de/dot_general | solution.py:198
  406.7 8.1 copy.66
  416.6 10.7 %fusion.24 = f32[768,3072]{1,0:T(8,128)} fusion(bf16[1024,3072]{1,0:T(8,128)(2,1)} %get-tuple-element.226, f32[1024,768]{1,0:T(8,128)S(1)} %copy-done.1, f32[768]{0:T(1024)S(1)} %copy-done.20, f32[768]{0:T(1024)S(1)} %copy-done.16, f32[1024]{0:T(1024)S(1)} %copy-done.14, f32[1024]{0:T(1024)S(1)} %copy-done.12), kind=kOutput, calls=%fused_computation.89 | convolution fusion | flops 4835770368 | bytes 18888704 | tf_op jit(solution)/shard_map/td,tf->df/dot_general | solution.py:166
  428.7 10.2 %fusion.37 = f32[3072,768]{1,0:T(8,128)} fusion(bf16[1024,3072]{1,0:T(8,128)(2,1)} %get-tuple-element.206, bf16[1024,768]{1,0:T(8,128)(2,1)S(1)} %copy-done.8), kind=kOutput, calls=%fused_computation.99 | convolution fusion | flops 4831838208 | bytes 17301504 | tf_op jit(solution)/shard_map/tf,td->fd/dot_general | solution.py:163
  444.5 43.5 %all-reduce = (f32[768]{0:T(1024)}, f32[768]{0:T(1024)}, f32[768]{0:T(1024)}, f32[768]{0:T(1024)}, f32[768]{0:T(1024)}, /*index=5*/f32[3072]{0:T(1024)}, f32[768]{0:T(1024)}, f32[768]{0:T(1024)}, f32[768]{0:T(1024)}) all-reduce(f32[768]{0:T(1024)S(1)} %get-tuple-element.157, ...), channel_id=1, replica_groups=mesh['fsdp'=8,'rep'=4] {'fsdp','rep'}, use_global_device_ids=true, to_apply=%region_18.19 | all-reduce | flops 9216 | bytes 73728 | tf_op jit(solution)/shard_map/psum | solution.py:236
  489.6 54.0 %reduce-scatter.13.cloned.1.call-done = f32[96,2304]{1,0:T(8,128)} async-done(((f32[768,2304]{1,0:T(8,128)}), f32[96,2304]{1,0:T(8,128)}) %reduce-scatter.13.cloned.1.call-update) | async-done | bytes 884752
  545.9 162.6 %reduce-scatter.9.cloned.1.call-done = f32[96,3072]{1,0:T(8,128)} async-done(((f32[768,3072]{1,0:T(8,128)}), f32[96,3072]{1,0:T(8,128)}) %reduce-scatter.9.cloned.1.call-update) | async-done | bytes 1179664 | tf_op jit(solution)/shard_map/reduce_scatter | solution.py:173
  710.6 162.7 %reduce-scatter.11.cloned.1.call-done = f32[384,768]{1,0:T(8,128)} async-done(((f32[3072,768]{1,0:T(8,128)}), f32[384,768]{1,0:T(8,128)}) %reduce-scatter.11.cloned.1.call-update) | async-done | bytes 1179664 | tf_op jit(solution)/shard_map/reduce_scatter | solution.py:174
  875.5 8.9 add_add_fusion.4
  884.5 40.4 %all-reduce.4.cloned.1.call-done = (bf16[96,2304]{0,1:T(8,128)(2,1)}, bf16[96,768]{1,0:T(8,128)(2,1)}, bf16[96,3072]{1,0:T(8,128)(2,1)}, bf16[384,768]{1,0:T(8,128)(2,1)}) async-done(((bf16[96,2304]{0,1:T(8,128)(2,1)}, bf16[96,768]{1,0:T(8,128)(2,1)}, bf16[96,3072]{1,0:T(8,128)(2,1)}, bf16[384,768]{1,0:T(8,128)(2,1)}), (bf16[96,2304]{0,1:T(8,128)(2,1)}, bf16[96,768]{1,0:T(8,128)(2,1)}, ...) | async-done | bytes 1769488 | tf_op jit(solution)/shard_map/psum | solution.py:209
  (176 shorter events, 94.5 us)
Async XLA Ops:
  7.2 70.3 %all-gather.5.cloned.1.call-start = ((), (), s32[]{:S(2)}) async-start(), calls=%async_computation.4 | async-start | bytes 3981312 | tf_op jit(solution)/shard_map/all_gather | solution.py:116
  7.9 111.7 %all-gather.7.cloned.1.call-start = ((), (), s32[]{:S(2)}) async-start(), calls=%async_computation.5 | async-start | bytes 1327104 | tf_op jit(solution)/shard_map/all_gather | solution.py:117
  8.7 191.2 %all-gather.9.cloned.1.call-start = ((), (), s32[]{:S(2)}) async-start(), calls=%async_computation.6 | async-start | bytes 5308416 | tf_op jit(solution)/shard_map/all_gather | solution.py:129
  9.4 270.2 %all-gather.11.cloned.1.call-start = ((), (), s32[]{:S(2)}) async-start(), calls=%async_computation.7 | async-start | bytes 5308416 | tf_op jit(solution)/shard_map/all_gather | solution.py:130
  10.0 478.0 %reduce-scatter.7.cloned.1.call-start = ((), (), s32[]{:S(2)}) async-start(), calls=%async_computation.8 | async-start | bytes 2654208 | tf_op jit(solution)/shard_map/reduce_scatter | solution.py:206
  86.0 6.8 copy-start.17
  92.8 26.8 %copy-start.31 = (f32[768]{0:T(1024)S(1)}, f32[768]{0:T(1024)}, u32[]{:S(2)}) copy-start(f32[768]{0:T(1024)} %convert_element_type.127) | copy-start | bytes 9220
  116.2 3.4 copy-start.9
  119.6 80.2 %copy-start.15 = (f32[768]{0:T(1024)S(1)}, f32[768]{0:T(1024)}, u32[]{:S(2)}) copy-start(f32[768]{0:T(1024)} %convert_element_type.128) | copy-start | bytes 9220
  119.6 80.2 %copy-start.19 = (f32[768]{0:T(1024)S(1)}, f32[768]{0:T(1024)}, u32[]{:S(2)}) copy-start(f32[768]{0:T(1024)} %convert_element_type.129) | copy-start | bytes 9220
  119.6 80.2 %copy-start.28 = (f32[3072]{0:T(1024)S(1)}, f32[3072]{0:T(1024)}, u32[]{:S(2)}) copy-start(f32[3072]{0:T(1024)} %convert_element_type.131) | copy-start | bytes 36868
  123.4 201.7 %copy-start = (f32[1024,768]{1,0:T(8,128)}, f32[1024,768]{1,0:T(8,128)S(1)}, u32[]{:S(2)}) copy-start(f32[1024,768]{1,0:T(8,128)S(1)} %get-tuple-element.220) | copy-start | bytes 9437188
  123.4 201.7 %copy-start.11 = (f32[1024]{0:T(1024)}, f32[1024]{0:T(1024)S(1)}, u32[]{:S(2)}) copy-start(f32[1024]{0:T(1024)S(1)} %broadcast_multiply_fusion.1) | copy-start | bytes 12292
  123.9 201.2 %copy-start.13 = (f32[1024]{0:T(1024)}, f32[1024]{0:T(1024)S(1)}, u32[]{:S(2)}) copy-start(f32[1024]{0:T(1024)S(1)} %fusion.22) | copy-start | bytes 12292
  123.9 155.6 %copy-start.30 = (f32[768]{0:T(1024)S(1)}, f32[768]{0:T(1024)}, u32[]{:S(2)}) copy-start(f32[768]{0:T(1024)} %convert_element_type.133) | copy-start | bytes 9220
  279.6 9.5 %copy-start.2 = (bf16[2,512,768]{2,1,0:T(8,128)(2,1)S(1)}, bf16[2,512,768]{2,1,0:T(8,128)(2,1)}, u32[]{:S(2)}) copy-start(bf16[2,512,768]{2,1,0:T(8,128)(2,1)} %param.35) | copy-start | bytes 4718596
  279.6 9.5 %copy-start.21 = (f32[768]{0:T(1024)S(1)}, f32[768]{0:T(1024)}, u32[]{:S(2)}) copy-start(f32[768]{0:T(1024)} %convert_element_type.134) | copy-start | bytes 9220
  288.5 2.3 copy-start.24
  326.6 2.6 copy-start.34
  326.6 2.6 copy-start.22
  332.1 2.8 copy-start.10
  332.1 2.8 copy-start.18
  332.1 211.5 %reduce-scatter.13.cloned.1.call-start = ((), (), s32[]{:S(2)}) async-start(), calls=%async_computation.11 | async-start | bytes 7962624
  335.0 2.6 copy-start.6
  362.5 3.3 copy-start.7
  365.8 2.6 copy-start.6
  393.3 3.4 copy-start.7
  414.8 293.7 %reduce-scatter.9.cloned.1.call-start = ((), (), s32[]{:S(2)}) async-start(), calls=%async_computation.9 | async-start | bytes 10616832 | tf_op jit(solution)/shard_map/reduce_scatter | solution.py:173
  427.3 446.0 %reduce-scatter.11.cloned.1.call-start = ((), (), s32[]{:S(2)}) async-start(), calls=%async_computation.10 | async-start | bytes 10616832 | tf_op jit(solution)/shard_map/reduce_scatter | solution.py:174
  438.9 485.9 %all-reduce.4.cloned.1.call-start = ((), (), s32[]{:S(2)}) async-start(), calls=%async_computation.12 | async-start | bytes 3833856 | tf_op jit(solution)/shard_map/psum | solution.py:209
  444.2 431.3 %copy-start.5 = (f32[1024,768]{1,0:T(8,128)S(1)}, f32[1024,768]{1,0:T(8,128)}, u32[]{:S(2)}) copy-start(f32[1024,768]{1,0:T(8,128)} %copy-done.4) | copy-start | bytes 9437188
  444.2 431.3 %copy-start.23 = (f32[1024]{0:T(1024)S(1)}, f32[1024]{0:T(1024)}, u32[]{:S(2)}) copy-start(f32[1024]{0:T(1024)} %copy-done.22) | copy-start | bytes 12292
  (14 other events, 18.2 us)
Sparse Core Ops, SparseCore 0:
  10.2 67.3 all-gather.4
  79.7 39.8 all-gather.6
  121.8 78.0 all-gather.8
  201.9 77.6 all-gather.10
  332.2 67.9 reduce-scatter.6
  414.9 128.6 reduce-scatter.12
  547.2 161.2 reduce-scatter.8
  712.1 161.1 reduce-scatter.10
  877.1 47.7 all-reduce.3
where the time goes:
time: 944 us; the launch traced here: 940 us
  waiting for transfers between devices  603 us (64%)
  matrix products  173 us (18%)
  other arithmetic  55.7 us (6%)
  local copies, waits for them, and re-layouts  48.9 us (5%)
  blocking collectives  43.5 us (5%)
  between operations  14.5 us (2%)
    reduce_scatter x1, waiting for transfers between devices, body(): lax.psum_scatter(shrink_term, 'fsdp', scatter_dimension=0, tiled=True)  163 us
    reduce_scatter x1, waiting for transfers between devices, body(): lax.psum_scatter(expand_term, 'fsdp', scatter_dimension=0, tiled=True)  163 us
    all_gather x1, waiting for transfers between devices, body(): lax.all_gather(expand_weight, 'fsdp', axis=0, tiled=True)  75.9 us
    all_gather x1, waiting for transfers between devices, body(): lax.all_gather(joint_weight, 'fsdp', axis=0, tiled=True)  57.8 us
    unnamed x10, waiting for transfers between devices  56.7 us
    all_gather x1, waiting for transfers between devices, body(): lax.all_gather(shrink_weight, 'fsdp', axis=0, tiled=True)  43.8 us
    psum x1, blocking collectives, body(): lax.psum((vector_terms[0], vector_terms[1], vector_terms[2], vector_terms...  43.5 us
    psum x1, waiting for transfers between devices, body(): lax.psum(joint_part.astype(jnp.bfloat16), 'rep').astype(jnp.float32)  40.4 us
  transfers between devices with their start and end apart: 9, of which 8 were waited for; matrix products, arithmetic and copies ran while one was open for 22% of the time, Pallas kernels for 0%

commit v1 on v0

--- a/solution.py
+++ b/solution.py
@@ -1,8 +1,11 @@
+import functools
 import math
 
 import jax
 import jax.numpy as jnp
 from jax import lax
+from jax.experimental import pallas as pl
+from jax.experimental.pallas import tpu as pltpu
 from jax.sharding import PartitionSpec as P
 
 HEADS = 12
@@ -91,7 +94,190 @@
     )
 
 
+AXES = ("fsdp", "rep")
+WIDE = 768
+HALF = 384
+
+
+def swap(value, mask, total):
+    return lax.ppermute(value, AXES, [(i, i ^ mask) for i in range(total)])
+
+
+def pick(flag, first, second):
+    return jnp.where(flag, second, first)
+
+
+def assemble_kernel(meta_ref, *refs):
+    out_ref = refs[-1]
+    fsdp_count, piece_rows = refs[0].shape[0], refs[0].shape[1]
+    for place in range(4):
+        x_here = meta_ref[1] ^ (place & 1)
+        c_here = meta_ref[2] ^ (place >> 1)
+        row = pl.multiple_of(x_here * piece_rows, piece_rows)
+        col = pl.multiple_of(c_here * HALF, 128)
+        for j in range(fsdp_count):
+            out_ref[meta_ref[0] ^ rel_shard(j, fsdp_count), pl.ds(row, piece_rows), pl.ds(col, HALF)] = refs[place][j]
+
+
+def rel_shard(j, fsdp_count):
+    bits = fsdp_count.bit_length() - 1
+    return sum(((j >> b) & 1) << (bits - 1 - b) for b in range(bits))
+
+
+def assemble(pieces, meta, by_rows):
+    fsdp_count, planes, piece_rows, _ = pieces[0].shape
+    shard_rows = 2 * piece_rows
+    if by_rows:
+        shape = (fsdp_count, planes * shard_rows, WIDE)
+        out_spec = pl.BlockSpec((fsdp_count, shard_rows, WIDE), lambda p, m: (0, p, 0))
+    else:
+        shape = (fsdp_count, shard_rows, planes * WIDE)
+        out_spec = pl.BlockSpec((fsdp_count, shard_rows, WIDE), lambda p, m: (0, 0, p))
+    full = pl.pallas_call(
+        assemble_kernel,
+        out_shape=jax.ShapeDtypeStruct(shape, jnp.bfloat16),
+        grid_spec=pltpu.PrefetchScalarGridSpec(
+            num_scalar_prefetch=1,
+            grid=(planes,),
+            in_specs=[
+                pl.BlockSpec((fsdp_count, pl.Squeezed(), piece_rows, HALF), lambda p, m: (0, p, 0, 0))
+            ]
+            * 4,
+            out_specs=out_spec,
+        ),
+        cost_estimate=pl.CostEstimate(
+            flops=0, bytes_accessed=4 * math.prod(shape), transcendentals=0
+        ),
+        name="assemble",
+    )(meta, *pieces)
+    return full.reshape(-1, shape[2])
+
+
+def assemble_plain(pieces, meta, by_rows):
+    fsdp_count, planes, piece_rows, _ = pieces[0].shape
+    order = meta[0] ^ jnp.array([rel_shard(j, fsdp_count) for j in range(fsdp_count)])
+    place = jnp.zeros_like(order).at[order].set(jnp.arange(fsdp_count))
+    ordered = [jnp.take(p, place, axis=0) for p in pieces]
+    halves = []
+    for c in range(2):
+        near = [pick(meta[2] != c, ordered[0], ordered[2]), pick(meta[2] != c, ordered[1], ordered[3])]
+        halves.append(
+            jnp.concatenate(
+                [pick(meta[1] == 1, near[0], near[1]), pick(meta[1] == 1, near[1], near[0])], axis=2
+            )
+        )
+    full = jnp.concatenate(halves, axis=3)
+    if by_rows:
+        return full.reshape(fsdp_count * planes * 2 * piece_rows, WIDE)
+    return full.transpose(0, 2, 1, 3).reshape(fsdp_count * 2 * piece_rows, planes * WIDE)
+
+
+def own_piece(shard, meta, by_rows):
+    if by_rows:
+        planes = D_SPLIT
+        rows = shard.shape[0] // planes
+        blocks = [shard[p * rows : (p + 1) * rows] for p in range(planes)]
+    else:
+        planes = shard.shape[1] // WIDE
+        rows = shard.shape[0]
+        blocks = [shard[:, p * WIDE : (p + 1) * WIDE] for p in range(planes)]
+    half = rows // 2
+    out = []
+    for b in blocks:
+        b = pick(meta[2] == 1, b[:, :HALF], b[:, HALF:])
+        out.append(pick(meta[1] == 1, b[:half], b[half:]))
+    return jnp.stack(out)
+
+
+D_SPLIT = 4
+
+
+def gather_pieces(piece, fsdp_count):
+    total = 4 * fsdp_count
+    held = piece[None]
+    mask = total // 2
+    while mask >= 4:
+        held = jnp.concatenate([held, swap(held, mask, total)], axis=0)
+        mask //= 2
+    over_x = swap(held, 2, total)
+    return [held, over_x, swap(held, 1, total), swap(over_x, 1, total)]
+
+
+def gather_weights(shards, meta, fsdp_count):
+    parts = [own_piece(s, meta, r) for s, r in shards]
+    counts = [p.shape[0] for p in parts]
+    pieces = gather_pieces(jnp.concatenate(parts, axis=0), fsdp_count)
+    out, start = [], 0
+    build = assemble if pieces[0].shape[2] % 16 == 0 else assemble_plain
+    for (_, by_rows), n in zip(shards, counts):
+        out.append(build([p[:, start : start + n] for p in pieces], meta, by_rows))
+        start += n
+    return out
+
+
+def reduce_grads(grads, meta, fsdp_count):
+    total = 4 * fsdp_count
+    planes, shapes = [], []
+    for g, by_rows in grads:
+        if by_rows:
+            rows = g.shape[0] // fsdp_count // D_SPLIT
+            g = g.reshape(fsdp_count, D_SPLIT, rows, WIDE)
+            planes += [g[:, p] for p in range(D_SPLIT)]
+            shapes.append((D_SPLIT, rows, True))
+        else:
+            n = g.shape[1] // WIDE
+            rows = g.shape[0] // fsdp_count
+            g = g.reshape(fsdp_count, rows, g.shape[1])
+            planes += [g[:, :, p * WIDE : (p + 1) * WIDE] for p in range(n)]
+            shapes.append((n, rows, False))
+    core = meta[2] == 1
+    keep = jnp.stack([pick(core, p[..., :HALF], p[..., HALF:]) for p in planes], axis=1)
+    send = jnp.stack(
+        [pick(core, p[..., HALF:], p[..., :HALF]).astype(jnp.bfloat16) for p in planes], axis=1
+    )
+    held = (keep + swap(send, 1, total)).astype(jnp.bfloat16)
+    half = held.shape[2] // 2
+    flag = meta[1] == 1
+    send = pick(flag, held[:, :, half:], held[:, :, :half])
+    keep = pick(flag, held[:, :, :half], held[:, :, half:])
+    held = (keep.astype(jnp.float32) + swap(send, 2, total)).astype(jnp.bfloat16)
+    bit = 1
+    while bit < fsdp_count:
+        held = held.reshape((held.shape[0] // 2, 2) + held.shape[1:])
+        flag = (meta[0] & bit) != 0
+        send = pick(flag, held[:, 1], held[:, 0])
+        keep = pick(flag, held[:, 0], held[:, 1])
+        held = (keep.astype(jnp.float32) + swap(send, bit * 4, total)).astype(jnp.bfloat16)
+        bit *= 2
+    mine = held[0]
+    other = swap(mine, 2, total)
+    near = jnp.concatenate([pick(meta[1] == 1, mine, other), pick(meta[1] == 1, other, mine)], axis=1)
+    far = swap(near, 1, total)
+    whole = jnp.concatenate(
+        [pick(core, near, far), pick(core, far, near)], axis=2
+    ).astype(jnp.float32)
+    out, start = [], 0
+    for n, rows, by_rows in shapes:
+        block = whole[start : start + n]
+        if by_rows:
+            out.append(block.reshape(n * rows, WIDE))
+        else:
+            out.append(jnp.concatenate([block[p] for p in range(n)], axis=1))
+        start += n
+    return out
+
+
+def reduce_vector(vector, fsdp_count):
+    total = 4 * fsdp_count
+    mask = 1
+    while mask < total:
+        vector = vector + swap(vector, mask, total)
+        mask *= 2
+    return vector
+
+
 def body(
+    fsdp_count,
     layer_input,
     segment_ids,
     joint_weight,
@@ -112,10 +298,13 @@
     row_count, pos_count, model_width = layer_input.shape
     tok_count = row_count * pos_count
     flat_input = layer_input.reshape(tok_count, model_width)
-    joint_full, close_full = (
-        lax.all_gather(joint_weight, "fsdp", axis=0, tiled=True),
-        lax.all_gather(close_weight, "fsdp", axis=0, tiled=True),
-    )
+    rep_index = lax.axis_index("rep")
+    meta = jnp.stack([lax.axis_index("fsdp"), rep_index >> 1, rep_index & 1]).astype(jnp.int32)
+    (joint_full,) = gather_weights([(joint_weight, False)], meta, fsdp_count)
+    close_full, expand_full = gather_weights(
+        [(close_weight, False), (expand_weight, False)], meta, fsdp_count
+    )
+    (shrink_full,) = gather_weights([(shrink_weight, True)], meta, fsdp_count)
     joint_bias = jnp.concatenate([query_bias, jnp.zeros_like(query_bias), value_bias]).astype(
         jnp.float32
     )
@@ -125,10 +314,6 @@
         lambda packet: attend_row(packet[0], packet[1]), (joint_low, segment_ids)
     )
     context_low = context.reshape(tok_count, model_width).astype(jnp.bfloat16)
-    expand_full, shrink_full = (
-        lax.all_gather(expand_weight, "fsdp", axis=0, tiled=True),
-        lax.all_gather(shrink_weight, "fsdp", axis=0, tiled=True),
-    )
     branch = jnp.dot(
         context_low, close_full, preferred_element_type=jnp.float32
     ) + close_bias.astype(jnp.float32)
@@ -152,38 +337,27 @@
         second_shift.astype(jnp.float32),
     )
     layer_output = output.astype(jnp.bfloat16).reshape(row_count, pos_count, model_width)
-    expand_back, shrink_back = (
-        lax.all_gather(expand_weight, "fsdp", axis=0, tiled=True),
-        lax.all_gather(shrink_weight, "fsdp", axis=0, tiled=True),
-    )
     grad_second, second_gain_part, second_shift_part = second_pull(
         cotangent.reshape(tok_count, model_width).astype(jnp.float32)
     )
     grad_ffn = grad_second.astype(jnp.bfloat16)
     shrink_term = jnp.einsum("tf,td->fd", active_low, grad_ffn, preferred_element_type=jnp.float32)
-    grad_active = jnp.einsum("td,fd->tf", grad_ffn, shrink_back, preferred_element_type=jnp.float32)
+    grad_active = jnp.einsum("td,fd->tf", grad_ffn, shrink_full, preferred_element_type=jnp.float32)
     grad_inner = gelu_pull(grad_active)[0].astype(jnp.bfloat16)
     expand_term = jnp.einsum(
         "td,tf->df", hidden_low, grad_inner, preferred_element_type=jnp.float32
     )
     grad_hidden = grad_second + jnp.einsum(
-        "tf,df->td", grad_inner, expand_back, preferred_element_type=jnp.float32
-    )
-    expand_part, shrink_part = (
-        lax.psum_scatter(expand_term, "fsdp", scatter_dimension=0, tiled=True),
-        lax.psum_scatter(shrink_term, "fsdp", scatter_dimension=0, tiled=True),
-    )
+        "tf,df->td", grad_inner, expand_full, preferred_element_type=jnp.float32
+    )
+    (shrink_grad,) = reduce_grads([(shrink_term, True)], meta, fsdp_count)
     grad_first, first_gain_part, first_shift_part = first_pull(grad_hidden)
     grad_branch = grad_first.astype(jnp.bfloat16)
-    joint_back, close_back = (
-        lax.all_gather(joint_weight, "fsdp", axis=0, tiled=True),
-        lax.all_gather(close_weight, "fsdp", axis=0, tiled=True),
-    )
     close_term = jnp.einsum(
         "td,te->de", context_low, grad_branch, preferred_element_type=jnp.float32
     )
     grad_context = jnp.einsum(
-        "te,de->td", grad_branch, close_back, preferred_element_type=jnp.float32
+        "te,de->td", grad_branch, close_full, preferred_element_type=jnp.float32
     ).astype(jnp.bfloat16)
     grad_mixed = lax.map(
         lambda packet: attend_back(packet[0], packet[1], packet[2], packet[3]),
@@ -199,33 +373,33 @@
         "td,te->de", flat_input, grad_mixed_low, preferred_element_type=jnp.float32
     )
     input_grad = grad_first + jnp.einsum(
-        "te,de->td", grad_mixed_low, joint_back, preferred_element_type=jnp.float32
-    )
-    joint_part, close_part = (
-        lax.psum_scatter(joint_term, "fsdp", scatter_dimension=0, tiled=True),
-        lax.psum_scatter(close_term, "fsdp", scatter_dimension=0, tiled=True),
-    )
-    joint_grad, close_grad, expand_grad, shrink_grad = (
-        lax.psum(joint_part.astype(jnp.bfloat16), "rep").astype(jnp.float32),
-        lax.psum(close_part.astype(jnp.bfloat16), "rep").astype(jnp.float32),
-        lax.psum(expand_part.astype(jnp.bfloat16), "rep").astype(jnp.float32),
-        lax.psum(shrink_part.astype(jnp.bfloat16), "rep").astype(jnp.float32),
-    )
+        "te,de->td", grad_mixed_low, joint_full, preferred_element_type=jnp.float32
+    )
+    close_grad, expand_grad = reduce_grads(
+        [(close_term, False), (expand_term, False)], meta, fsdp_count
+    )
+    (joint_grad,) = reduce_grads([(joint_term, False)], meta, fsdp_count)
     grad_mixed_wide = grad_mixed_low.astype(jnp.float32)
-    vector_terms = (
-        jnp.sum(grad_mixed_wide[:, :model_width], axis=0),
-        jnp.sum(grad_mixed_wide[:, 2 * model_width :], axis=0),
-        jnp.sum(grad_branch.astype(jnp.float32), axis=0),
-        first_gain_part,
-        first_shift_part,
-        jnp.sum(grad_inner.astype(jnp.float32), axis=0),
-        jnp.sum(grad_ffn.astype(jnp.float32), axis=0),
-        second_gain_part,
-        second_shift_part,
-    )
+    early = reduce_vector(
+        jnp.concatenate(
+            [
+                jnp.sum(grad_branch.astype(jnp.float32), axis=0),
+                first_gain_part,
+                first_shift_part,
+                jnp.sum(grad_inner.astype(jnp.float32), axis=0),
+                jnp.sum(grad_ffn.astype(jnp.float32), axis=0),
+                second_gain_part,
+                second_shift_part,
+            ]
+        ),
+        fsdp_count,
+    )
+    hidden_units = expand_bias.shape[0]
+    cuts, place = [], 0
+    for size in (model_width,) * 3 + (hidden_units,) + (model_width,) * 3:
+        cuts.append(early[place : place + size])
+        place += size
     (
-        query_bias_grad,
-        value_bias_grad,
         close_bias_grad,
         first_gain_grad,
         first_shift_grad,
@@ -233,20 +407,17 @@
         shrink_bias_grad,
         second_gain_grad,
         second_shift_grad,
-    ) = lax.psum(
-        (
-            vector_terms[0],
-            vector_terms[1],
-            vector_terms[2],
-            vector_terms[3],
-            vector_terms[4],
-            vector_terms[5],
-            vector_terms[6],
-            vector_terms[7],
-            vector_terms[8],
-        ),
-        ("fsdp", "rep"),
-    )
+    ) = cuts
+    late = reduce_vector(
+        jnp.concatenate(
+            [
+                jnp.sum(grad_mixed_wide[:, :model_width], axis=0),
+                jnp.sum(grad_mixed_wide[:, 2 * model_width :], axis=0),
+            ]
+        ),
+        fsdp_count,
+    )
+    query_bias_grad, value_bias_grad = late[:model_width], late[model_width:]
     return (
         layer_output,
         input_grad.reshape(row_count, pos_count, model_width),
@@ -286,7 +457,7 @@
         P(("fsdp", "rep"), None, None),
     )
     return jax.shard_map(
-        body,
+        functools.partial(body, mesh.shape["fsdp"]),
         mesh=mesh,
         in_specs=placed,
         out_specs=(

time: 944 us -> 531 us (0.56)
  waiting for transfers between devices: 603 us -> 157 us
  starting transfers between devices: 0.36 us -> 46.5 us
  blocking collectives: 43.5 us -> 0 us
  Pallas kernels: 0 us -> 20.8 us
  other arithmetic: 55.7 us -> 70.6 us
  local copies, waits for them, and re-layouts: 48.9 us -> 62.6 us
  between operations: 14.5 us -> 2.1 us
    reduce_scatter x3 -> x0, waiting for transfers between devices: 325 us -> none  [the longest x1 163 us: body(): lax.psum_scatter(shrink_term, 'fsdp', scatter_dimension=0, tiled=True)]
    all_gather x4 -> x0, waiting for transfers between devices: 181 us -> none  [the longest x1 75.9 us: body(): lax.all_gather(expand_weight, 'fsdp', axis=0, tiled=True)]
    ppermute x0 -> x49, waiting for transfers between devices: none -> 157 us  [swap(): return lax.ppermute(value, AXES, [(i, i ^ mask) for i in range(total)])]
    unnamed x10 -> x0, waiting for transfers between devices: 56.7 us -> none
    ppermute x0 -> x49, starting transfers between devices: none -> 46.5 us  [swap(): return lax.ppermute(value, AXES, [(i, i ^ mask) for i in range(total)])]
    psum x1 -> x0, blocking collectives: 43.5 us -> none  [body(): lax.psum((vector_terms[0], vector_terms[1], vector_terms[2], vector_terms...]
    psum x1 -> x0, waiting for transfers between devices: 40.4 us -> none  [body(): lax.psum(joint_part.astype(jnp.bfloat16), 'rep').astype(jnp.float32)]
    pallas_call x0 -> x4, Pallas kernels: none -> 20.8 us  [assemble(): pl.pallas_call(assemble_kernel, out_shape=jax.ShapeDtypeStruct(shape, jnp...]
  transfers between devices with their start and end apart: 9 -> 49, of which waited for: 8 -> 28; matrix products, arithmetic and copies ran while one was open for 22% -> 17% of each run, Pallas kernels for 0% -> 2%
where the time goes in v1:
time: 531 us; the launch traced here: 527 us
  matrix products  166 us (31%)
  waiting for transfers between devices  157 us (30%)
  other arithmetic  70.6 us (13%)
  local copies, waits for them, and re-layouts  62.6 us (12%)
  starting transfers between devices  46.5 us (9%)
  Pallas kernels  20.8 us (4%)
    ppermute x49, waiting for transfers between devices, swap(): return lax.ppermute(value, AXES, [(i, i ^ mask) for i in range(total)])  157 us
    ppermute x49, starting transfers between devices, swap(): return lax.ppermute(value, AXES, [(i, i ^ mask) for i in range(total)])  46.5 us
    dot_general x1, matrix products, body(): jnp.dot(hidden_low, expand_full, preferred_element_type=jnp.float32)  37.5 us
    pallas_call x4, Pallas kernels, assemble(): pl.pallas_call(assemble_kernel, out_shape=jax.ShapeDtypeStruct(shape, jnp...  20.8 us
    dot_general x1, matrix products, body(): jnp.einsum('td,fd->tf', grad_ffn, shrink_full, preferred_element_type=jnp...  18.8 us
    slice x8, local copies, waits for them, and re-layouts, gather_weights(): out.append(build([p[:, start:start + n] for p in pieces], meta, by_rows))  16.4 us
    convert_element_type x2, other arithmetic, attend_back(): grad_scores = (attn_weights * (grad_attn - inner_sum)).astype(jnp.bfloat16)  13.9 us
    dot_general x2, matrix products, attend_back(): jnp.einsum('qhd,khd->hqk', grad_heads, values_part, preferred_element_typ...  13.6 us
  transfers between devices with their start and end apart: 49, of which 28 were waited for; matrix products, arithmetic and copies ran while one was open for 17% of the time, Pallas kernels for 2%

profile of v1, /device:TPU:0, one launch (start us, length us, event | category | flops | bytes accessed | tf_op | source)
XLA Modules:
  0.0 526.6 jit_solution(5317509329941157043)
XLA Ops:
  8.5 7.0 %collective-permute-done = bf16[1,3,48,384]{3,2,1,0:T(8,128)(2,1)S(1)} collective-permute-done((bf16[1,3,48,384]{3,2,1,0:T(8,128)(2,1)S(1)}, bf16[1,3,48,384]{3,2,1,0:T(8,128)(2,1)S(1)}, u32[]{:S(2)}, u32[]{:S(2)}) %collective-permute-start) | collective-permute-done | bytes 110624 | tf_op jit(solution)/shard_map/ppermute | solution.py:103
  19.0 7.5 %collective-permute-done.1 = bf16[2,3,48,384]{3,2,1,0:T(8,128)(2,1)S(1)} collective-permute-done((bf16[2,3,48,384]{3,2,1,0:T(8,128)(2,1)S(1)}, bf16[2,3,48,384]{3,2,1,0:T(8,128)(2,1)S(1)}, u32[]{:S(2)}, u32[]{:S(2)}) %collective-permute-start.1) | collective-permute-done | bytes 221216 | tf_op jit(solution)/shard_map/ppermute | solution.py:103
  30.4 7.7 %collective-permute-done.13 = bf16[2,4,48,384]{3,2,1,0:T(8,128)(2,1)S(1)} collective-permute-done((bf16[2,4,48,384]{3,2,1,0:T(8,128)(2,1)S(1)}, bf16[2,4,48,384]{3,2,1,0:T(8,128)(2,1)S(1)}, u32[]{:S(2)}, u32[]{:S(2)}) %collective-permute-start.13) | collective-permute-done | bytes 294944 | tf_op jit(solution)/shard_map/ppermute | solution.py:103
  44.2 10.3 %collective-permute-done.14 = bf16[4,4,48,384]{3,2,1,0:T(8,128)(2,1)S(1)} collective-permute-done((bf16[4,4,48,384]{3,2,1,0:T(8,128)(2,1)S(1)}, bf16[4,4,48,384]{3,2,1,0:T(8,128)(2,1)S(1)}, u32[]{:S(2)}, u32[]{:S(2)}) %collective-permute-start.14) | collective-permute-done | bytes 589856 | tf_op jit(solution)/shard_map/ppermute | solution.py:103
  78.9 8.6 %collective-permute-done.15.refs_1_ = bf16[8,4,48,384]{3,2,1,0:T(8,128)(2,1)} collective-permute-done((bf16[8,4,48,384]{3,2,1,0:T(8,128)(2,1)}, bf16[8,4,48,384]{3,2,1,0:T(8,128)(2,1)}, u32[]{:S(2)}, u32[]{:S(2)}) %collective-permute-start.15) | collective-permute-done | bytes 1179680 | tf_op jit(solution)/shard_map/ppermute | solution.py:103
  87.5 5.9 %assemble.4 = bf16[8,96,2304]{2,1,0:T(8,128)(2,1)} custom-call(s32[3]{0:T(128)} %pad_add_fusion.meta_ref, bf16[8,3,48,384]{3,2,1,0:T(8,128)(2,1)} %copy-done.12, bf16[8,3,48,384]{3,2,1,0:T(8,128)(2,1)} %copy-done.22, bf16[8,3,48,384]{3,2,1,0:T(8,128)(2,1)} %collective-permute-done.4.refs_2_, bf16[8,3,48,384]{3,2,1,0:T(8,128)(2,1)} %collective-permute-done.5.refs_3_), custom_call_target="tpu_custom_call" | custom-call | bytes 7077888 | tf_op jit(solution)/shard_map/assemble/pallas_call | solution.py:136
  93.4 7.4 %add_convert_fusion.1 = bf16[2304,1024]{0,1:T(8,128)(2,1)} fusion(bf16[1024,768]{1,0:T(8,128)(2,1)S(1)} %bitcast.472, bf16[768,2304]{1,0:T(8,128)(2,1)} %bitcast.453, f32[2304]{0:T(1024)S(1)} %maximum_convert_fusion.3), kind=kOutput, calls=%fused_computation.48 | convolution fusion | flops 3628597248 | bytes 9839616 | tf_op jit(solution)/shard_map/dot_general | solution.py:311
  100.8 6.8 %copy.91 = bf16[2,512,2304]{1,2,0:T(8,128)(2,1)} copy(bf16[2,512,2304]{2,1,0:T(8,128)(2,1)} %bitcast.450) | data formatting | bytes 9437184 | tf_op jit(solution)/shard_map/while | solution.py:313
  107.7 6.5 %collective-permute-done.9 = bf16[8,5,48,384]{3,2,1,0:T(8,128)(2,1)} collective-permute-done((bf16[8,5,48,384]{3,2,1,0:T(8,128)(2,1)}, bf16[8,5,48,384]{3,2,1,0:T(8,128)(2,1)}, u32[]{:S(2)}, u32[]{:S(2)}) %collective-permute-start.9) | collective-permute-done | bytes 1474592 | tf_op jit(solution)/shard_map/ppermute | solution.py:103
  114.2 21.7 %while.22 = (s32[]{:T(128)}, bf16[2,512,768]{2,1,0:T(8,128)(2,1)S(1)}, f32[2,12,512,1]{2,1,3,0:T(8,128)S(1)}, bf16[2,512,2304]{1,2,0:T(8,128)(2,1)}, s32[2,512]{1,0:T(2,128)S(1)}, /*index=5*/s32[]{:T(128)}) while((s32[]{:T(128)}, bf16[2,512,768]{2,1,0:T(8,128)(2,1)S(1)}, f32[2,12,512,1]{2,1,3,0:T(8,128)S(1)}, bf16[2,512,2304]{1,2,0:T(8,128)(2,1)}, ...), condition=%wide.region_3.4_spmd, body=%wide.region_0.3_spmd.sunk | while | flops 843311104 | bytes 54753372 | solution.py:313
  145.9 5.9 %assemble.7 = bf16[8,384,768]{2,1,0:T(8,128)(2,1)} custom-call(s32[3]{0:T(128)} %pad_add_fusion.meta_ref, bf16[8,4,48,384]{3,2,1,0:T(8,128)(2,1)} %pad_maximum_fusion.3.refs_0_, bf16[8,4,48,384]{3,2,1,0:T(8,128)(2,1)} %collective-permute-done.15.refs_1_, bf16[8,4,48,384]{3,2,1,0:T(8,128)(2,1)} %collective-permute-done.16.refs_2_, ...), custom_call_target="tpu_custom_call" | custom-call | bytes 9437184 | tf_op jit(solution)/shard_map/assemble/pallas_call | solution.py:136
  163.8 6.0 %assemble.6 = bf16[8,96,3072]{2,1,0:T(8,128)(2,1)} custom-call(s32[3]{0:T(128)} %pad_add_fusion.meta_ref, bf16[8,4,48,384]{3,2,1,0:T(8,128)(2,1)} %slice.659.refs_0_, bf16[8,4,48,384]{3,2,1,0:T(8,128)(2,1)} %slice.660.refs_1_, bf16[8,4,48,384]{3,2,1,0:T(8,128)(2,1)} %slice.661.refs_2_, bf16[8,4,48,384]{3,2,1,0:T(8,128)(2,1)} %slice.662.refs_3_), custom_call_target="tpu_custom_call" | custom-call | bytes 9437184 | tf_op jit(solution)/shard_map/assemble/pallas_call | solution.py:136
  169.9 37.5 %multiply_convert_fusion.1 = (bf16[1024,3072]{1,0:T(8,128)(2,1)S(1)}, f32[1024,3072]{1,0:T(8,128)}, f32[1024,3072]{1,0:T(8,128)}) fusion(f32[3072]{0:T(1024)S(1)} %copy-done.40, bf16[768,3072]{1,0:T(8,128)(2,1)} %bitcast.448, f32[1024,768]{1,0:T(8,128)S(1)} %get-tuple-element.217, f32[768]{0:T(1024)S(1)} %copy-done.29, f32[768]{0:T(1024)S(1)} %copy-done.26, ...), kind=kOutput, calls=%fused_computation.34 | convolution fusion | flops 5043388416 | bytes 39348224 | tf_op jit(solution)/shard_map/dot_general | solution.py:325
  207.4 10.0 %fusion.99 = (f32[1024]{0:T(1024)S(1)}, f32[1024,768]{1,0:T(8,128)S(1)}) fusion(f32[768]{0:T(1024)S(1)} %copy-done.42, bf16[1024,3072]{1,0:T(8,128)(2,1)S(1)} %get-tuple-element.148, bf16[3072,768]{1,0:T(8,128)(2,1)} %bitcast.446, f32[768]{0:T(1024)S(1)} %copy-done.29, f32[768]{0:T(1024)S(1)} %copy-done.26, f32[1024]{0:T(1024)S(1)} %fusion.81, ...), kind=kOutput, calls=%fused_computation.292 | convolution fusion | flops 4837342208 | bytes 17323008 | tf_op jit(solution)/shard_map/dot_general | solution.py:330
  225.3 18.8 %convert_reduce_fusion = (f32[3072]{0:T(1024)}, bf16[1024,3072]{1,0:T(8,128)(2,1)}) fusion(f32[1024,3072]{1,0:T(8,128)} %get-tuple-element.149, bf16[1024,768]{1,0:T(8,128)(2,1)} %get-tuple-element.141, bf16[3072,768]{1,0:T(8,128)(2,1)} %bitcast.447, f32[1024,3072]{1,0:T(8,128)} %get-tuple-element.218, f32[3072]{0:T(1024)S(1)} %copy-done.40), kind=kOutput, calls=%fused_computation.32 | convolution fusion | flops 4885312512 | bytes 37773312 | tf_op jit(solution)/shard_map/td,fd->tf/dot_general | solution.py:345
  244.1 10.7 %multiply_reduce_fusion.1 = (f32[768]{0:T(1024)}, f32[1024]{0:T(1024)S(1)}, f32[768]{0:T(1024)}, f32[1024,768]{1,0:T(8,128)S(1)}) fusion(f32[1024,768]{1,0:T(8,128)S(1)} %get-tuple-element.217, f32[1024]{0:T(1024)S(1)} %fusion.81, f32[1024]{0:T(1024)S(1)} %broadcast_multiply_fusion.1, f32[768]{0:T(1024)S(1)} %copy-done.26, ...), kind=kOutput, calls=%fused_computation.66 | convolution fusion | flops 4839699456 | bytes 20472832 | tf_op jit(solution)/shard_map/tf,df->td/dot_general | solution.py:350
  254.8 8.4 %fusion.84 = f32[768,3072]{1,0:T(8,128)} fusion(bf16[1024,3072]{1,0:T(8,128)(2,1)S(1)} %copy-done.6, f32[1024,768]{1,0:T(8,128)S(1)} %get-tuple-element.217, f32[768]{0:T(1024)S(1)} %copy-done.29, f32[768]{0:T(1024)S(1)} %copy-done.26, f32[1024]{0:T(1024)S(1)} %fusion.81, f32[1024]{0:T(1024)S(1)} %broadcast_multiply_fusion.1), kind=kOutput, calls=%fused_computation.280 | convolution fusion | flops 4835770368 | bytes 18888704 | tf_op jit(solution)/shard_map/td,tf->df/dot_general | solution.py:347
  263.2 10.3 %fusion.102 = f32[3072,768]{1,0:T(8,128)} fusion(bf16[1024,3072]{1,0:T(8,128)(2,1)} %copy-done.53, bf16[1024,768]{1,0:T(8,128)(2,1)S(1)} %copy-done.20), kind=kOutput, calls=%fused_computation.295 | convolution fusion | flops 4831838208 | bytes 17301504 | tf_op jit(solution)/shard_map/tf,td->fd/dot_general | solution.py:344
  292.8 61.4 %while.23 = (s32[]{:T(128)}, bf16[2,512,2304]{2,1,0:T(8,128)(2,1)}, bf16[2,512,2304]{1,2,0:T(8,128)(2,1)}, s32[2,512]{1,0:T(2,128)S(1)}, f32[2,12,512,1]{2,1,3,0...) while((s32[]{:T(128)}, bf16[2,512,2304]{2,1,0:T(8,128)(2,1)}, ...), condition=%wide.region_14.15_spmd, body=%wide.region_12.14_spmd.sunk | while | flops 2069358592 | bytes 142784688 | solution.py:362
  300.6 6.8 %multiply_reduce_fusion.6 = (f32[12,512]{1,0:T(8,128)S(1)}, f32[12,512,512]{1,2,0:T(8,128)}) fusion(f32[12,512,512]{1,2,0:T(8,128)S(1)} %fusion.174, f32[12,512]{1,0:T(8,128)S(1)} %dynamic-slice_bitcast_fusion.8, pred[512,512]{0,1:T(8,128)(4,1)S(1)} %broadcast_compare_fusion.5, bf16[512,12,64]{0,2,1:T(8,128)(2,1)S(1)} %bitcast.419, ...), kind=kOutput, calls=%fused_computation.14.clone.1 | convolution fusion | flops 418375680 | bytes 27049984 | tf_op jit(solution)/shard_map/while/body/eval_jaxpr/qhd,khd->hqk/dot_general | solution.py:68
  307.4 7.0 %multiply_convert_fusion.3 = bf16[12,512,512]{1,2,0:T(8,128)(2,1)S(1)} fusion(f32[12,512,512]{1,2,0:T(8,128)} %get-tuple-element.318, f32[12,512,512]{1,2,0:T(8,128)S(1)} %fusion.174, f32[12,512]{1,0:T(8,128)S(1)} %get-tuple-element.319, f32[12,512]{1,0:T(8,128)S(1)} %dynamic-slice_bitcast_fusion.8, pred[512,512]{0,1:T(8,128)(4,1)S(1)} %broadcast_compare_fusion.5), kind=kLoop, calls=%fused_computation.13.clone.1 | loop fusion | flops 18874368 | bytes 31768576 | tf_op jit(solution)/shard_map/while/body/eval_jaxpr/convert_element_type | solution.py:72
  331.1 6.8 %multiply_reduce_fusion.6 = (f32[12,512]{1,0:T(8,128)S(1)}, f32[12,512,512]{1,2,0:T(8,128)}) fusion(f32[12,512,512]{1,2,0:T(8,128)S(1)} %fusion.174, f32[12,512]{1,0:T(8,128)S(1)} %dynamic-slice_bitcast_fusion.8, pred[512,512]{0,1:T(8,128)(4,1)S(1)} %broadcast_compare_fusion.5, bf16[512,12,64]{0,2,1:T(8,128)(2,1)S(1)} %bitcast.419, ...), kind=kOutput, calls=%fused_computation.14.clone.1 | convolution fusion | flops 418375680 | bytes 27049984 | tf_op jit(solution)/shard_map/while/body/eval_jaxpr/qhd,khd->hqk/dot_general | solution.py:68
  337.9 7.0 %multiply_convert_fusion.3 = bf16[12,512,512]{1,2,0:T(8,128)(2,1)S(1)} fusion(f32[12,512,512]{1,2,0:T(8,128)} %get-tuple-element.318, f32[12,512,512]{1,2,0:T(8,128)S(1)} %fusion.174, f32[12,512]{1,0:T(8,128)S(1)} %get-tuple-element.319, f32[12,512]{1,0:T(8,128)S(1)} %dynamic-slice_bitcast_fusion.8, pred[512,512]{0,1:T(8,128)(4,1)S(1)} %broadcast_compare_fusion.5), kind=kLoop, calls=%fused_computation.13.clone.1 | loop fusion | flops 18874368 | bytes 31768576 | tf_op jit(solution)/shard_map/while/body/eval_jaxpr/convert_element_type | solution.py:72
  354.3 7.0 %fusion.101 = f32[2304,768,1]{0,1,2:T(8,128)S(1)} fusion(bf16[2,512,2304]{2,1,0:T(8,128)(2,1)} %get-tuple-element.77, bf16[2,512,768]{2,1,0:T(8,128)(2,1)} %param.20), kind=kOutput, calls=%fused_computation.294 | convolution fusion | flops 3623878656 | bytes 13369344 | tf_op jit(solution)/shard_map/td,te->de/dot_general | solution.py:372
  376.1 7.9 %add_add_fusion.4 = f32[1024,768]{1,0:T(8,128)} fusion(f32[1024,768]{1,0:T(8,128)S(1)} %copy-done.3, bf16[1024,2304]{1,0:T(8,128)(2,1)S(1)} %bitcast.445, bf16[768,2304]{1,0:T(8,128)(2,1)} %bitcast.454, f32[1024]{0:T(1024)S(1)} %copy-done.38), kind=kOutput, calls=%fused_computation.75 | convolution fusion | flops 3625451520 | bytes 14553088 | tf_op jit(solution)/shard_map/te,de->td/dot_general | solution.py:375
  415.3 7.5 %collective-permute-done.20 = bf16[4,3,48,384]{3,2,1,0:T(8,128)(2,1)S(1)} collective-permute-done((bf16[4,3,48,384]{3,2,1,0:T(8,128)(2,1)S(1)}, bf16[4,3,48,384]{3,2,1,0:T(8,128)(2,1)S(1)}, u32[]{:S(2)}, u32[]{:S(2)}) %collective-permute-start.20) | collective-permute-done | bytes 442400 | tf_op jit(solution)/shard_map/ppermute | solution.py:103
  423.9 6.2 %collective-permute-done.21 = bf16[2,3,48,384]{3,2,1,0:T(8,128)(2,1)S(1)} collective-permute-done((bf16[2,3,48,384]{3,2,1,0:T(8,128)(2,1)S(1)}, bf16[2,3,48,384]{3,2,1,0:T(8,128)(2,1)S(1)}, u32[]{:S(2)}, u32[]{:S(2)}) %collective-permute-start.21) | collective-permute-done | bytes 221216 | tf_op jit(solution)/shard_map/ppermute | solution.py:103
  438.9 15.7 %collective-permute-done.23 = bf16[3,48,384]{2,1,0:T(8,128)(2,1)S(1)} collective-permute-done((bf16[3,48,384]{2,1,0:T(8,128)(2,1)S(1)}, bf16[3,48,384]{2,1,0:T(8,128)(2,1)S(1)}, u32[]{:S(2)}, u32[]{:S(2)}) %collective-permute-start.23) | collective-permute-done | bytes 110624 | tf_op jit(solution)/shard_map/ppermute | solution.py:103
  457.4 24.8 %collective-permute-done.31 = bf16[8,5,48,384]{3,2,0,1:T(8,128)(2,1)S(1)} collective-permute-done((bf16[8,5,48,384]{3,2,0,1:T(8,128)(2,1)S(1)}, bf16[8,5,48,384]{3,2,0,1:T(8,128)(2,1)S(1)}, u32[]{:S(2)}, u32[]{:S(2)}) %collective-permute-start.31) | collective-permute-done | bytes 1474592 | tf_op jit(solution)/shard_map/ppermute | solution.py:103
  485.8 11.8 %collective-permute-done.32 = bf16[4,5,48,384]{3,2,1,0:T(8,128)(2,1)S(1)} collective-permute-done((bf16[4,5,48,384]{3,2,1,0:T(8,128)(2,1)S(1)}, bf16[4,5,48,384]{3,2,1,0:T(8,128)(2,1)S(1)}, u32[]{:S(2)}, u32[]{:S(2)}) %collective-permute-start.32) | collective-permute-done | bytes 737312 | tf_op jit(solution)/shard_map/ppermute | solution.py:103
  502.0 5.9 %collective-permute-done.33 = bf16[2,5,48,384]{3,2,1,0:T(8,128)(2,1)S(1)} collective-permute-done((bf16[2,5,48,384]{3,2,1,0:T(8,128)(2,1)S(1)}, bf16[2,5,48,384]{3,2,1,0:T(8,128)(2,1)S(1)}, u32[]{:S(2)}, u32[]{:S(2)}) %collective-permute-start.33) | collective-permute-done | bytes 368672 | tf_op jit(solution)/shard_map/ppermute | solution.py:103
  511.6 5.1 collective-permute-done.34
  (415 shorter events, 229.0 us)
Async XLA Ops:
  1.9 13.6 %collective-permute-start = (bf16[1,3,48,384]{3,2,1,0:T(8,128)(2,1)S(1)}, bf16[1,3,48,384]{3,2,1,0:T(8,128)(2,1)S(1)}, u32[]{:S(2)}, u32[]{:S(2)}) collective-permute-start(bf16[1,3,48,384]{3,2,1,0:T(8,128)(2,1)S(1)} %maximum_bitcast_fusion.2), channel_id=1, source_target_pairs={{0,16},{1,17},{2,18},{3,19},{4,20},{5,21},{6,22},{7,23},{8,24},{9,... | collective-permute-start | bytes 331784 | tf_op jit(solution)/shard_map/ppermute | solution.py:103
  7.3 20.9 %collective-permute-start.12 = (bf16[1,4,48,384]{3,2,1,0:T(8,128)(2,1)S(1)}, bf16[1,4,48,384]{3,2,1,0:T(8,128)(2,1)S(1)}, u32[]{:S(2)}, u32[]{:S(2)}) collective-permute-start(bf16[1,4,48,384]{3,2,1,0:T(8,128)(2,1)S(1)} %maximum_bitcast_fusion.1), channel_id=1, source_target_pairs={{0,16},{1,17},{2,18},{3,19},{4,20},{5,21},{6,22},{7,23},{8,24},{9,... | collective-permute-start | bytes 442376 | tf_op jit(solution)/shard_map/ppermute | solution.py:103
  15.5 11.0 %collective-permute-start.1 = (bf16[2,3,48,384]{3,2,1,0:T(8,128)(2,1)S(1)}, bf16[2,3,48,384]{3,2,1,0:T(8,128)(2,1)S(1)}, u32[]{:S(2)}, u32[]{:S(2)}) collective-permute-start(bf16[2,3,48,384]{3,2,1,0:T(8,128)(2,1)S(1)} %pad_maximum_fusion.14), channel_id=1, source_target_pairs={{0,8},{1,9},{2,10},{3,11},{4,12},{5,13},{6,14},{7,15},{8,0},{9,1},... | collective-permute-start | bytes 663560 | tf_op jit(solution)/shard_map/ppermute | solution.py:103
  15.6 12.7 %collective-permute-start.6 = (bf16[1,5,48,384]{3,2,1,0:T(8,128)(2,1)S(1)}, bf16[1,5,48,384]{3,2,1,0:T(8,128)(2,1)S(1)}, u32[]{:S(2)}, u32[]{:S(2)}) collective-permute-start(bf16[1,5,48,384]{3,2,1,0:T(8,128)(2,1)S(1)} %bitcast.457), channel_id=1, source_target_pairs={{0,16},{1,17},{2,18},{3,19},{4,20},{5,21},{6,22},{7,23},{8,24},{9,... | collective-permute-start | bytes 552968 | tf_op jit(solution)/shard_map/ppermute | solution.py:103
  26.5 12.8 %collective-permute-start.2 = (bf16[4,3,48,384]{3,2,1,0:T(8,128)(2,1)S(1)}, bf16[4,3,48,384]{3,2,1,0:T(8,128)(2,1)S(1)}, u32[]{:S(2)}, u32[]{:S(2)}) collective-permute-start(bf16[4,3,48,384]{3,2,1,0:T(8,128)(2,1)S(1)} %pad_maximum_fusion.9), channel_id=1, source_target_pairs={{0,4},{1,5},{2,6},{3,7},{4,0},{5,1},{6,2},{7,3},{8,12},{9,13},{10,... | collective-permute-start | bytes 1327112 | tf_op jit(solution)/shard_map/ppermute | solution.py:103
  28.2 9.9 %collective-permute-start.13 = (bf16[2,4,48,384]{3,2,1,0:T(8,128)(2,1)S(1)}, bf16[2,4,48,384]{3,2,1,0:T(8,128)(2,1)S(1)}, u32[]{:S(2)}, u32[]{:S(2)}) collective-permute-start(bf16[2,4,48,384]{3,2,1,0:T(8,128)(2,1)S(1)} %pad_maximum_fusion.12), channel_id=1, source_target_pairs={{0,8},{1,9},{2,10},{3,11},{4,12},{5,13},{6,14},{7,15},{8,0},{9,1},... | collective-permute-start | bytes 884744 | tf_op jit(solution)/shard_map/ppermute | solution.py:103
  28.4 15.0 %collective-permute-start.7 = (bf16[2,5,48,384]{3,2,1,0:T(8,128)(2,1)S(1)}, bf16[2,5,48,384]{3,2,1,0:T(8,128)(2,1)S(1)}, u32[]{:S(2)}, u32[]{:S(2)}) collective-permute-start(bf16[2,5,48,384]{3,2,1,0:T(8,128)(2,1)S(1)} %pad_maximum_fusion.10), channel_id=1, source_target_pairs={{0,8},{1,9},{2,10},{3,11},{4,12},{5,13},{6,14},{7,15},{8,0},{9,1},... | collective-permute-start | bytes 1105928 | tf_op jit(solution)/shard_map/ppermute | solution.py:103
  38.2 16.3 %collective-permute-start.14 = (bf16[4,4,48,384]{3,2,1,0:T(8,128)(2,1)S(1)}, bf16[4,4,48,384]{3,2,1,0:T(8,128)(2,1)S(1)}, u32[]{:S(2)}, u32[]{:S(2)}) collective-permute-start(bf16[4,4,48,384]{3,2,1,0:T(8,128)(2,1)S(1)} %pad_maximum_fusion.8), channel_id=1, source_target_pairs={{0,4},{1,5},{2,6},{3,7},{4,0},{5,1},{6,2},{7,3},{8,12},{9,13},{10,... | collective-permute-start | bytes 1769480 | tf_op jit(solution)/shard_map/ppermute | solution.py:103
  39.5 22.6 %collective-permute-start.3 = (bf16[8,3,48,384]{3,2,1,0:T(8,128)(2,1)S(1)}, bf16[8,3,48,384]{3,2,1,0:T(8,128)(2,1)S(1)}, u32[]{:S(2)}, u32[]{:S(2)}) collective-permute-start(bf16[8,3,48,384]{3,2,1,0:T(8,128)(2,1)S(1)} %pad_maximum_fusion.5.refs_0_), channel_id=1, source_target_pairs={{0,2},{1,3},{2,0},{3,1},{4,6},{5,7},{6,4},{7,5},{8,10},{9,11},{10,... | collective-permute-start | bytes 2654216 | tf_op jit(solution)/shard_map/ppermute | solution.py:103
  43.4 22.4 %collective-permute-start.8 = (bf16[4,5,48,384]{3,2,1,0:T(8,128)(2,1)S(1)}, bf16[4,5,48,384]{3,2,1,0:T(8,128)(2,1)S(1)}, u32[]{:S(2)}, u32[]{:S(2)}) collective-permute-start(bf16[4,5,48,384]{3,2,1,0:T(8,128)(2,1)S(1)} %pad_maximum_fusion.7), channel_id=1, source_target_pairs={{0,4},{1,5},{2,6},{3,7},{4,0},{5,1},{6,2},{7,3},{8,12},{9,13},{10,... | collective-permute-start | bytes 2211848 | tf_op jit(solution)/shard_map/ppermute | solution.py:103
  55.7 31.8 %collective-permute-start.15 = (bf16[8,4,48,384]{3,2,1,0:T(8,128)(2,1)}, bf16[8,4,48,384]{3,2,1,0:T(8,128)(2,1)}, u32[]{:S(2)}, u32[]{:S(2)}) collective-permute-start(bf16[8,4,48,384]{3,2,1,0:T(8,128)(2,1)} %pad_maximum_fusion.3.refs_0_), channel_id=1, source_target_pairs={{0,2},{1,3},{2,0},{3,1},{4,6},{5,7},{6,4},{7,5},{8,10},{9,11},{10,... | collective-permute-start | bytes 3538952 | tf_op jit(solution)/shard_map/ppermute | solution.py:103
  57.2 21.1 %collective-permute-start.4 = (bf16[8,3,48,384]{3,2,1,0:T(8,128)(2,1)S(1)}, bf16[8,3,48,384]{3,2,1,0:T(8,128)(2,1)}, u32[]{:S(2)}, u32[]{:S(2)}) collective-permute-start(bf16[8,3,48,384]{3,2,1,0:T(8,128)(2,1)S(1)} %pad_maximum_fusion.5.refs_0_), channel_id=1, source_target_pairs={{0,1},{1,0},{2,3},{3,2},{4,5},{5,4},{6,7},{7,6},{8,9},{9,8},{10,11... | collective-permute-start | bytes 2654216 | tf_op jit(solution)/shard_map/ppermute | solution.py:103
  62.1 25.4 %collective-permute-start.5 = (bf16[8,3,48,384]{3,2,1,0:T(8,128)(2,1)S(1)}, bf16[8,3,48,384]{3,2,1,0:T(8,128)(2,1)}, u32[]{:S(2)}, u32[]{:S(2)}) collective-permute-start(bf16[8,3,48,384]{3,2,1,0:T(8,128)(2,1)S(1)} %collective-permute-done.3.refs_1_), channel_id=1, source_target_pairs={{0,1},{1,0},{2,3},{3,2},{4,5},{5,4},{6,7},{7,6},{8,9},{9,8},{10,11... | collective-permute-start | bytes 2654216 | tf_op jit(solution)/shard_map/ppermute | solution.py:103
  67.2 47.0 %collective-permute-start.9 = (bf16[8,5,48,384]{3,2,1,0:T(8,128)(2,1)}, bf16[8,5,48,384]{3,2,1,0:T(8,128)(2,1)}, u32[]{:S(2)}, u32[]{:S(2)}) collective-permute-start(bf16[8,5,48,384]{3,2,1,0:T(8,128)(2,1)} %pad_maximum_fusion.2), channel_id=1, source_target_pairs={{0,2},{1,3},{2,0},{3,1},{4,6},{5,7},{6,4},{7,5},{8,10},{9,11},{10,... | collective-permute-start | bytes 4423688 | tf_op jit(solution)/shard_map/ppermute | solution.py:103
  74.2 71.7 %collective-permute-start.16 = (bf16[8,4,48,384]{3,2,1,0:T(8,128)(2,1)}, bf16[8,4,48,384]{3,2,1,0:T(8,128)(2,1)}, u32[]{:S(2)}, u32[]{:S(2)}) collective-permute-start(bf16[8,4,48,384]{3,2,1,0:T(8,128)(2,1)} %pad_maximum_fusion.3.refs_0_), channel_id=1, source_target_pairs={{0,1},{1,0},{2,3},{3,2},{4,5},{5,4},{6,7},{7,6},{8,9},{9,8},{10,11... | collective-permute-start | bytes 3538952 | tf_op jit(solution)/shard_map/ppermute | solution.py:103
  78.3 59.3 %collective-permute-start.10 = (bf16[8,5,48,384]{3,2,1,0:T(8,128)(2,1)}, bf16[8,5,48,384]{3,2,1,0:T(8,128)(2,1)}, u32[]{:S(2)}, u32[]{:S(2)}) collective-permute-start(bf16[8,5,48,384]{3,2,1,0:T(8,128)(2,1)} %pad_maximum_fusion.2), channel_id=1, source_target_pairs={{0,1},{1,0},{2,3},{3,2},{4,5},{5,4},{6,7},{7,6},{8,9},{9,8},{10,11... | collective-permute-start | bytes 4423688 | tf_op jit(solution)/shard_map/ppermute | solution.py:103
  87.5 58.3 %collective-permute-start.17 = (bf16[8,4,48,384]{3,2,1,0:T(8,128)(2,1)}, bf16[8,4,48,384]{3,2,1,0:T(8,128)(2,1)}, u32[]{:S(2)}, u32[]{:S(2)}) collective-permute-start(bf16[8,4,48,384]{3,2,1,0:T(8,128)(2,1)} %collective-permute-done.15.refs_1_), channel_id=1, source_target_pairs={{0,1},{1,0},{2,3},{3,2},{4,5},{5,4},{6,7},{7,6},{8,9},{9,8},{10,11... | collective-permute-start | bytes 3538952 | tf_op jit(solution)/shard_map/ppermute | solution.py:103
  114.2 37.6 %collective-permute-start.11 = (bf16[8,5,48,384]{3,2,1,0:T(8,128)(2,1)}, bf16[8,5,48,384]{3,2,1,0:T(8,128)(2,1)}, u32[]{:S(2)}, u32[]{:S(2)}) collective-permute-start(bf16[8,5,48,384]{3,2,1,0:T(8,128)(2,1)} %collective-permute-done.9), channel_id=1, source_target_pairs={{0,1},{1,0},{2,3},{3,2},{4,5},{5,4},{6,7},{7,6},{8,9},{9,8},{10,11... | collective-permute-start | bytes 4423688 | tf_op jit(solution)/shard_map/ppermute | solution.py:103
  368.3 21.5 %collective-permute-start.37 = (f32[7680]{0:T(1024)S(1)}, f32[7680]{0:T(1024)S(1)}, u32[]{:S(2)}, u32[]{:S(2)}) collective-permute-start(f32[7680]{0:T(1024)S(1)} %constant_dynamic-update-slice_fusion.3), channel_id=1, source_target_pairs={{0,1},{1,0},{2,3},{3,2},{4,5},{5,4},{6,7},{7,6},{8,9},{9,8},{10,11... | collective-permute-start | bytes 92168 | tf_op jit(solution)/shard_map/ppermute | solution.py:103
  372.8 60.0 %collective-permute-start.30 = (bf16[8,5,96,384]{3,2,0,1:T(8,128)(2,1)}, bf16[8,5,96,384]{3,2,0,1:T(8,128)(2,1)}, u32[]{:S(2)}, u32[]{:S(2)}) collective-permute-start(bf16[8,5,96,384]{3,2,0,1:T(8,128)(2,1)} %fusion.43), channel_id=1, source_target_pairs={{0,1},{1,0},{2,3},{3,2},{4,5},{5,4},{6,7},{7,6},{8,9},{9,8},{10,11... | collective-permute-start | bytes 8847368 | tf_op jit(solution)/shard_map/ppermute | solution.py:103
  374.2 17.2 %collective-permute-start.18 = (bf16[8,3,96,384]{3,2,0,1:T(8,128)(2,1)}, bf16[8,3,96,384]{3,2,0,1:T(8,128)(2,1)S(1)}, u32[]{:S(2)}, u32[]{:S(2)}) collective-permute-start(bf16[8,3,96,384]{3,2,0,1:T(8,128)(2,1)} %pad_maximum_fusion.1), channel_id=1, source_target_pairs={{0,1},{1,0},{2,3},{3,2},{4,5},{5,4},{6,7},{7,6},{8,9},{9,8},{10,11... | collective-permute-start | bytes 5308424 | tf_op jit(solution)/shard_map/ppermute | solution.py:103
  384.4 30.2 %collective-permute-start.42 = (bf16[8,4,96,384]{3,2,0,1:T(8,128)(2,1)S(1)}, bf16[8,4,96,384]{3,2,0,1:T(8,128)(2,1)S(1)}, u32[]{:S(2)}, u32[]{:S(2)}) collective-permute-start(bf16[8,4,96,384]{3,2,0,1:T(8,128)(2,1)S(1)} %pad_maximum_fusion), channel_id=1, source_target_pairs={{0,1},{1,0},{2,3},{3,2},{4,5},{5,4},{6,7},{7,6},{8,9},{9,8},{10,11... | collective-permute-start | bytes 7077896 | tf_op jit(solution)/shard_map/ppermute | solution.py:103
  392.0 20.3 %collective-permute-start.19 = (bf16[8,3,48,384]{3,2,0,1:T(8,128)(2,1)S(1)}, bf16[8,3,48,384]{3,2,0,1:T(8,128)(2,1)S(1)}, u32[]{:S(2)}, u32[]{:S(2)}) collective-permute-start(bf16[8,3,48,384]{3,2,0,1:T(8,128)(2,1)S(1)} %broadcast_select_fusion.2), channel_id=1, source_target_pairs={{0,2},{1,3},{2,0},{3,1},{4,6},{5,7},{6,4},{7,5},{8,10},{9,11},{10,... | collective-permute-start | bytes 2654216 | tf_op jit(solution)/shard_map/ppermute | solution.py:103
  412.9 10.0 %collective-permute-start.20 = (bf16[4,3,48,384]{3,2,1,0:T(8,128)(2,1)S(1)}, bf16[4,3,48,384]{3,2,1,0:T(8,128)(2,1)S(1)}, u32[]{:S(2)}, u32[]{:S(2)}) collective-permute-start(bf16[4,3,48,384]{3,2,1,0:T(8,128)(2,1)S(1)} %select_bitcast_fusion.8), channel_id=1, source_target_pairs={{0,4},{1,5},{2,6},{3,7},{4,0},{5,1},{6,2},{7,3},{8,12},{9,13},{10,... | collective-permute-start | bytes 1327112 | tf_op jit(solution)/shard_map/ppermute | solution.py:103
  423.3 31.4 %collective-permute-start.43 = (bf16[8,4,48,384]{3,2,0,1:T(8,128)(2,1)S(1)}, bf16[8,4,48,384]{3,2,0,1:T(8,128)(2,1)S(1)}, u32[]{:S(2)}, u32[]{:S(2)}) collective-permute-start(bf16[8,4,48,384]{3,2,0,1:T(8,128)(2,1)S(1)} %broadcast_select_fusion.1), channel_id=1, source_target_pairs={{0,2},{1,3},{2,0},{3,1},{4,6},{5,7},{6,4},{7,5},{8,10},{9,11},{10,... | collective-permute-start | bytes 3538952 | tf_op jit(solution)/shard_map/ppermute | solution.py:103
  436.5 18.0 %collective-permute-start.23 = (bf16[3,48,384]{2,1,0:T(8,128)(2,1)S(1)}, bf16[3,48,384]{2,1,0:T(8,128)(2,1)S(1)}, u32[]{:S(2)}, u32[]{:S(2)}) collective-permute-start(bf16[3,48,384]{2,1,0:T(8,128)(2,1)S(1)} %fusion.63), channel_id=1, source_target_pairs={{0,2},{1,3},{2,0},{3,1},{4,6},{5,7},{6,4},{7,5},{8,10},{9,11},{10,... | collective-permute-start | bytes 331784 | tf_op jit(solution)/shard_map/ppermute | solution.py:103
  437.3 44.8 %collective-permute-start.31 = (bf16[8,5,48,384]{3,2,0,1:T(8,128)(2,1)S(1)}, bf16[8,5,48,384]{3,2,0,1:T(8,128)(2,1)S(1)}, u32[]{:S(2)}, u32[]{:S(2)}) collective-permute-start(bf16[8,5,48,384]{3,2,0,1:T(8,128)(2,1)S(1)} %broadcast_select_fusion), channel_id=1, source_target_pairs={{0,2},{1,3},{2,0},{3,1},{4,6},{5,7},{6,4},{7,5},{8,10},{9,11},{10,... | collective-permute-start | bytes 4423688 | tf_op jit(solution)/shard_map/ppermute | solution.py:103
  455.3 28.4 %collective-permute-start.44 = (bf16[4,4,48,384]{3,2,0,1:T(8,128)(2,1)S(1)}, bf16[4,4,48,384]{3,2,0,1:T(8,128)(2,1)S(1)}, u32[]{:S(2)}, u32[]{:S(2)}) collective-permute-start(bf16[4,4,48,384]{3,2,0,1:T(8,128)(2,1)S(1)} %fusion.30), channel_id=1, source_target_pairs={{0,4},{1,5},{2,6},{3,7},{4,0},{5,1},{6,2},{7,3},{8,12},{9,13},{10,... | collective-permute-start | bytes 1769480 | tf_op jit(solution)/shard_map/ppermute | solution.py:103
  483.1 14.6 %collective-permute-start.32 = (bf16[4,5,48,384]{3,2,1,0:T(8,128)(2,1)S(1)}, bf16[4,5,48,384]{3,2,1,0:T(8,128)(2,1)S(1)}, u32[]{:S(2)}, u32[]{:S(2)}) collective-permute-start(bf16[4,5,48,384]{3,2,1,0:T(8,128)(2,1)S(1)} %select_bitcast_fusion.7), channel_id=1, source_target_pairs={{0,4},{1,5},{2,6},{3,7},{4,0},{5,1},{6,2},{7,3},{8,12},{9,13},{10,... | collective-permute-start | bytes 2211848 | tf_op jit(solution)/shard_map/ppermute | solution.py:103
  484.0 15.5 %collective-permute-start.45 = (bf16[2,4,48,384]{3,2,1,0:T(8,128)(2,1)S(1)}, bf16[2,4,48,384]{3,2,1,0:T(8,128)(2,1)S(1)}, u32[]{:S(2)}, u32[]{:S(2)}) collective-permute-start(bf16[2,4,48,384]{3,2,1,0:T(8,128)(2,1)S(1)} %select_bitcast_fusion.9), channel_id=1, source_target_pairs={{0,8},{1,9},{2,10},{3,11},{4,12},{5,13},{6,14},{7,15},{8,0},{9,1},... | collective-permute-start | bytes 884744 | tf_op jit(solution)/shard_map/ppermute | solution.py:103
  498.0 10.0 %collective-permute-start.33 = (bf16[2,5,48,384]{3,2,1,0:T(8,128)(2,1)S(1)}, bf16[2,5,48,384]{3,2,1,0:T(8,128)(2,1)S(1)}, u32[]{:S(2)}, u32[]{:S(2)}) collective-permute-start(bf16[2,5,48,384]{3,2,1,0:T(8,128)(2,1)S(1)} %fusion.51), channel_id=1, source_target_pairs={{0,8},{1,9},{2,10},{3,11},{4,12},{5,13},{6,14},{7,15},{8,0},{9,1},... | collective-permute-start | bytes 1105928 | tf_op jit(solution)/shard_map/ppermute | solution.py:103
  499.6 11.3 %collective-permute-start.46 = (bf16[1,4,48,384]{3,2,1,0:T(8,128)(2,1)S(1)}, bf16[1,4,48,384]{3,2,1,0:T(8,128)(2,1)S(1)}, u32[]{:S(2)}, u32[]{:S(2)}) collective-permute-start(bf16[1,4,48,384]{3,2,1,0:T(8,128)(2,1)S(1)} %select_bitcast_fusion.11), channel_id=1, source_target_pairs={{0,16},{1,17},{2,18},{3,19},{4,20},{5,21},{6,22},{7,23},{8,24},{9,... | collective-permute-start | bytes 442376 | tf_op jit(solution)/shard_map/ppermute | solution.py:103
  (78 other events, 758.5 us)

commit v2 on v0

v2 whole, which is shorter than its diff:
```python
import functools
import math

import jax
import jax.numpy as jnp
from jax import lax
from jax.experimental import pallas as pl
from jax.experimental.pallas import tpu as pltpu
from jax.sharding import PartitionSpec as P

HEADS = 12
EPS = 1e-12
AXES = ("fsdp", "rep")
LANES = 128
NT = (((1,), (1,)), ((), ()))
NN = (((1,), (0,)), ((), ()))
LOW = jnp.bfloat16
WIDE = jnp.float32


def layer_norm(values, gain, shift):
    average = jnp.mean(values, axis=-1, keepdims=True)
    centred = values - average
    variance = jnp.mean(centred * centred, axis=-1, keepdims=True)
    return centred * lax.rsqrt(variance + EPS) * gain + shift


def attend_kernel(mixed_ref, seg_col_ref, seg_row_ref, *refs):
    context_ref, weights_ref, inverse_ref = refs[-3:]
    pos = mixed_ref.shape[0]
    head = mixed_ref.shape[1] // 6
    same = seg_col_ref[...] == seg_row_ref[...]
    values_t = mixed_ref[:, 4 * head : 6 * head].T
    ones = jnp.ones((16, pos), LOW)
    outs, inverses = [], []
    for h in range(2):
        queries = mixed_ref[:, h * head : (h + 1) * head] * LOW(1.0 / math.sqrt(head))
        keys = mixed_ref[:, (2 + h) * head : (3 + h) * head]
        scores = lax.dot_general(keys, queries, NT, preferred_element_type=WIDE)
        scores = jnp.where(same, scores, -jnp.inf)
        raised = jnp.exp(scores - jnp.max(scores, axis=0, keepdims=True)).astype(LOW)
        weights_ref[h] = raised
        extended = jnp.concatenate([values_t[h * head : (h + 1) * head], ones], axis=0)
        out = lax.dot_general(extended, raised, NN, preferred_element_type=WIDE)
        inverse = 1.0 / out[head : head + 1]
        outs.append(out[:head] * inverse)
        inverses.append(jnp.broadcast_to(inverse, (head, pos)))
    context_ref[...] = jnp.concatenate(outs, axis=0).T.astype(LOW)
    inverse_ref[...] = jnp.concatenate(inverses, axis=0).T


def attend_back_kernel(mixed_ref, weights_ref, context_ref, inverse_ref, grad_ref, *refs):
    out_ref, sum_ref = refs[-2:]
    head = mixed_ref.shape[1] // 6
    scale = LOW(1.0 / math.sqrt(head))
    grad = grad_ref[...].astype(WIDE) * inverse_ref[...]
    product = (grad * context_ref[...].astype(WIDE)).astype(LOW)
    grad_low = grad.astype(LOW)
    queries = mixed_ref[:, : 2 * head] * scale
    keys_t = (mixed_ref[:, 2 * head : 4 * head] * scale).T
    ones = jnp.ones((8, head), LOW)
    grad_q, grad_k, grad_v = [], [], []
    for h in range(2):
        cut = slice(h * head, (h + 1) * head)
        values = mixed_ref[:, (4 + h) * head : (5 + h) * head]
        inner = lax.dot_general(ones, product[:, cut], NT, preferred_element_type=WIDE)[0:1]
        raised = weights_ref[h]
        grad_attn = lax.dot_general(values, grad_low[:, cut], NT, preferred_element_type=WIDE)
        grad_scores = raised * (grad_attn - inner).astype(LOW)
        grad_k.append(lax.dot_general(grad_scores, queries[:, cut], NN, preferred_element_type=WIDE))
        grad_v.append(lax.dot_general(raised, grad_low[:, cut], NN, preferred_element_type=WIDE))
        grad_q.append(lax.dot_general(keys_t[cut], grad_scores, NN, preferred_element_type=WIDE))
    out = jnp.concatenate([jnp.concatenate(grad_q, axis=0).T] + grad_k + grad_v, axis=1).astype(LOW)
    out_ref[...] = out
    sum_ref[...] = jnp.broadcast_to(
        jnp.sum(out.astype(WIDE), axis=0, keepdims=True), sum_ref.shape
    )


class Chunk:
    def __init__(self, first, count, half):
        self.first, self.count, self.half = first, count, half
        self.pairs = [c * half + first + i for c in range(2) for i in range(count)]

    def block(self, place):
        return (place // self.count) * self.half + self.first + place % self.count


def attend(mixed, segments, chunk, context=None, behind=()):
    rows, pos, width = mixed.shape
    group = width // len(chunk.pairs)
    pair = group // 3
    count = len(chunk.pairs)
    total = 2 * chunk.half
    in_specs = [
        pl.BlockSpec((None, pos, group), lambda r, p: (r, 0, p)),
        pl.BlockSpec((None, pos, 1), lambda r, p: (r, 0, 0)),
        pl.BlockSpec((None, 1, pos), lambda r, p: (r, 0, 0)),
    ]
    operands = [mixed, segments[:, :, None], segments[:, None, :]]
    aliases = {}
    if context is not None:
        in_specs.append(pl.BlockSpec(memory_space=pl.ANY))
        operands.append(context)
        aliases = {3: 0}
    in_specs += [pl.BlockSpec(memory_space=pl.ANY)] * len(behind)
    operands += behind
    return pl.pallas_call(
        attend_kernel,
        grid=(rows, count),
        in_specs=in_specs,
        out_specs=[
            pl.BlockSpec((None, pos, pair), lambda r, p: (r, 0, chunk.block(p))),
            pl.BlockSpec((None, None, 2, pos, pos), lambda r, p: (r, p, 0, 0, 0)),
            pl.BlockSpec((None, pos, pair), lambda r, p: (r, 0, p)),
        ],
        out_shape=[
            jax.ShapeDtypeStruct((rows, pos, total * pair), LOW),
            jax.ShapeDtypeStruct((rows, count, 2, pos, pos), LOW),
            jax.ShapeDtypeStruct((rows, pos, count * pair), WIDE),
        ],
        input_output_aliases=aliases,
        cost_estimate=pl.CostEstimate(
            flops=rows * count * pos * pos * pair * 16,
            bytes_accessed=rows * count * pos * pos * 8,
            transcendentals=rows * count * pos * pos * 2,
        ),
        name="attend",
    )(*operands)


def attend_back(mixed, weights, context, inverse, grad, chunk, behind=()):
    rows, pos, width = mixed.shape
    count = len(chunk.pairs)
    group = width // count
    pair = group // 3
    natural = pl.BlockSpec((None, pos, pair), lambda r, p: (r, 0, chunk.block(p)))
    return pl.pallas_call(
        attend_back_kernel,
        grid=(rows, count),
        in_specs=[
            pl.BlockSpec((None, pos, group), lambda r, p: (r, 0, p)),
            pl.BlockSpec((None, None, 2, pos, pos), lambda r, p: (r, p, 0, 0, 0)),
            natural,
            pl.BlockSpec((None, pos, pair), lambda r, p: (r, 0, p)),
            natural,
        ]
        + [pl.BlockSpec(memory_space=pl.ANY)] * len(behind),
        out_specs=[
            pl.BlockSpec((None, pos, group), lambda r, p: (r, 0, p)),
            pl.BlockSpec((None, None, 8, group), lambda r, p: (r, p, 0, 0)),
        ],
        out_shape=[
            jax.ShapeDtypeStruct((rows, pos, count * group), LOW),
            jax.ShapeDtypeStruct((rows, count, 8, group), WIDE),
        ],
        cost_estimate=pl.CostEstimate(
            flops=rows * count * pos * pos * pair * 32,
            bytes_accessed=rows * count * pos * pos * 8,
            transcendentals=0,
        ),
        name="attend_back",
    )(mixed, weights, context, inverse, grad, *behind)


def expand_kernel(hidden_ref, weight_ref, bias_ref, active_ref, slope_ref, *, chunks):
    step = hidden_ref.shape[0] // chunks
    for i in range(chunks):
        cut = slice(i * step, (i + 1) * step)
        inner = lax.dot_general(hidden_ref[cut], weight_ref[...], NN, preferred_element_type=WIDE)
        inner = inner + bias_ref[...]
        share = 0.5 + 0.5 * lax.erf(inner * math.sqrt(0.5))
        active_ref[cut] = (inner * share).astype(LOW)
        density = jnp.exp(-0.5 * inner * inner) * (1.0 / math.sqrt(2.0 * math.pi))
        slope_ref[cut] = (share + inner * density).astype(LOW)


def expand_gelu(hidden, weight, bias):
    tokens, model_width = hidden.shape
    units = weight.shape[1]
    tile = 768
    return pl.pallas_call(
        functools.partial(expand_kernel, chunks=8),
        grid=(units // tile,),
        in_specs=[
            pl.BlockSpec((tokens, model_width), lambda j: (0, 0)),
            pl.BlockSpec((model_width, tile), lambda j: (0, j)),
            pl.BlockSpec((1, tile), lambda j: (0, j)),
        ],
        out_specs=[pl.BlockSpec((tokens, tile), lambda j: (0, j))] * 2,
        out_shape=[jax.ShapeDtypeStruct((tokens, units), LOW)] * 2,
        cost_estimate=pl.CostEstimate(
            flops=3 * tokens * model_width * units,
            bytes_accessed=2 * (tokens * units * 2 + model_width * units),
            transcendentals=2 * tokens * units,
        ),
        name="expand_gelu",
    )(hidden, weight, bias)


class Wires:
    def __init__(self, fsdp_count):
        self.fsdp_count = fsdp_count
        self.total = 4 * fsdp_count
        self.shard = lax.axis_index("fsdp")
        rep = lax.axis_index("rep")
        self.x = rep >> 1
        self.core = rep & 1
        self.meta = jnp.stack([self.shard, self.x, self.core]).astype(jnp.int32)

    def swap(self, value, mask):
        return lax.ppermute(value, AXES, [(i, i ^ mask) for i in range(self.total)])

    def own_half(self, low, high):
        return jnp.where(self.core == 1, high, low)

    def other_half(self, low, high):
        return jnp.where(self.core == 1, low, high)

    def own_rows(self, value, axis=0):
        half = value.shape[axis] // 2
        low = lax.slice_in_dim(value, 0, half, axis=axis)
        high = lax.slice_in_dim(value, half, 2 * half, axis=axis)
        return jnp.where(self.x == 1, high, low), jnp.where(self.x == 1, low, high)


    def steps(self):
        masks, mask = [], self.total // 2
        while mask >= 4:
            masks.append(mask)
            mask //= 2
        return masks

    def share(self, near):
        return near + [self.swap(v, 1) for v in near]


    def halve_steps(self, held):
        bit = 1
        while bit < self.fsdp_count:
            held = held.reshape((held.shape[0] // 2, 2) + held.shape[1:])
            flag = (self.shard & bit) != 0
            send = jnp.where(flag, held[:, 0], held[:, 1])
            keep = jnp.where(flag, held[:, 1], held[:, 0])
            held = add_low(keep, self.swap(send, 4 * bit))
            bit *= 2
            yield held if bit < self.fsdp_count else held[0]

    def x_steps(self, keep, got):
        held = add_low(keep, got)
        for held in self.halve_steps(held):
            yield held
        other = self.swap(held, 2)
        flag = self.x == 1
        yield jnp.concatenate([jnp.where(flag, other, held), jnp.where(flag, held, other)], axis=0)

    def all_steps(self, held):
        for held in self.halve_steps(held):
            yield held
        yield add_low(held, self.swap(held, 2))

    def reduce_vector(self, vector):
        mask = 1
        while mask < self.total:
            vector = vector + self.swap(vector, mask)
            mask *= 2
        return vector


def tie(*values):
    return lax.optimization_barrier(values)


def last(steps):
    for value in steps:
        pass
    return value


def row(vector):
    return vector.reshape(1, -1).astype(WIDE)


def add_low(first, second):
    return (first.astype(WIDE) + second.astype(WIDE)).astype(LOW)


def weight_copies(meta_ref, refs, out_ref, sem, parts, half_width):
    count = out_ref.shape[0]
    at = 0
    copies = []
    for width, start, by_x, offset in parts:
        for place in range(4 if by_x else 2):
            piece = refs[at]
            at += 1
            core = meta_ref[2] ^ (place // 2 if by_x else place)
            col = pl.multiple_of(core * half_width + offset, LANES)
            rows = piece.shape[1]
            row = pl.multiple_of((meta_ref[1] ^ (place & 1)) * rows, rows) if by_x else 0
            for j in range(count):
                copies.append(
                    pltpu.make_async_copy(
                        piece.at[j, :, pl.ds(start, width)],
                        out_ref.at[
                            meta_ref[0] ^ from_front(j, count), pl.ds(row, rows), pl.ds(col, width)
                        ],
                        sem,
                    )
                )
    return copies


def assemble_kernel(meta_ref, *refs, parts, half_width):
    copies = weight_copies(meta_ref, refs, refs[-2], refs[-1], parts, half_width)
    for copy in copies:
        copy.start()
    for copy in copies:
        copy.wait()


def project(inputs, weight_ref, query_ref, value_ref, out_ref, pairs):
    group = 3 * LANES
    step = 256
    for i, p in enumerate(pairs):
        cut = slice(i * group, (i + 1) * group)
        weight = weight_ref[..., cut].reshape(inputs.shape[1], group)
        bias = jnp.concatenate(
            [query_ref[p : p + 1], jnp.zeros((1, LANES), WIDE), value_ref[p : p + 1]], axis=1
        )
        for t in range(0, inputs.shape[0], step):
            out = lax.dot_general(inputs[t : t + step], weight, NN, preferred_element_type=WIDE)
            out_ref[t : t + step, cut] = (out + bias).astype(LOW)


def project_kernel(meta_ref, inputs_ref, query_ref, value_ref, *refs, parts, half_width, pairs):
    full_ref, out_ref, sem = refs[-3:]
    copies = weight_copies(meta_ref, refs, full_ref, sem, parts, half_width)
    for copy in copies:
        copy.start()
    for copy in copies:
        copy.wait()
    project(inputs_ref, full_ref, query_ref, value_ref, out_ref, pairs)


def project_whole_kernel(inputs_ref, query_ref, value_ref, full_ref, *refs, pairs):
    project(inputs_ref, full_ref, query_ref, value_ref, refs[-1], pairs)


def joint_project(wires, inputs, pieces, query_bias, value_bias, chunk, shard_rows, behind=()):
    tokens, model_width = inputs.shape
    half_width = chunk.count * 3 * LANES
    out_shape = jax.ShapeDtypeStruct((tokens, 2 * half_width), LOW)
    on_chip = pl.BlockSpec(memory_space=pltpu.VMEM)
    anywhere = pl.BlockSpec(memory_space=pl.ANY)
    cost = pl.CostEstimate(
        flops=4 * tokens * model_width * half_width,
        bytes_accessed=4 * half_width * (tokens + 3 * model_width),
        transcendentals=0,
    )
    if not isinstance(pieces, list):
        out = pl.pallas_call(
            functools.partial(project_whole_kernel, pairs=chunk.pairs),
            out_shape=out_shape,
            in_specs=[on_chip] * 4 + [anywhere] * len(behind),
            out_specs=on_chip,
            cost_estimate=cost,
            name="joint_project",
        )(inputs, query_bias, value_bias, pieces, *behind)
        return pieces, out
    full, out = pl.pallas_call(
        functools.partial(
            project_kernel,
            parts=[(half_width, 0, True, 0)],
            half_width=half_width,
            pairs=chunk.pairs,
        ),
        out_shape=[
            jax.ShapeDtypeStruct((wires.fsdp_count, shard_rows, 2 * half_width), LOW),
            out_shape,
        ],
        in_specs=[pl.BlockSpec(memory_space=pltpu.SMEM)]
        + [on_chip] * 3
        + [anywhere] * (len(pieces) + len(behind)),
        out_specs=[on_chip] * 2,
        scratch_shapes=[pltpu.SemaphoreType.DMA],
        cost_estimate=cost,
        name="joint_project",
    )(wires.meta, inputs, query_bias, value_bias, *pieces, *behind)
    return full.reshape(model_width, 2 * half_width), out


def pack_kernel(*refs, chunks, wide):
    *vector_refs, out_ref = refs
    sum_refs, vector_refs = vector_refs[: len(chunks)], vector_refs[len(chunks) :]
    out_ref[...] = jnp.zeros_like(out_ref)
    for ref, chunk in zip(sum_refs, chunks):
        for i, p in enumerate(chunk.pairs):
            total = ref[0, i, 0:1]
            for r in range(1, ref.shape[0]):
                total = total + ref[r, i, 0:1]
            out_ref[0:1, p * LANES : (p + 1) * LANES] = total[:, :LANES]
            out_ref[1:2, p * LANES : (p + 1) * LANES] = total[:, 2 * LANES :]
    row = 2
    for ref in vector_refs:
        for start in range(0, ref.shape[1], wide):
            out_ref[row : row + 1] = ref[:, start : start + wide]
            row += 1


def pack(sums, chunks, vectors, wide):
    rows = 2 + sum(v.shape[1] // wide for v in vectors)
    return pl.pallas_call(
        functools.partial(pack_kernel, chunks=chunks, wide=wide),
        out_shape=jax.ShapeDtypeStruct(((rows + 7) // 8 * 8, wide), WIDE),
        name="pack",
    )(*sums, *vectors)


def from_front(place, count):
    bits = count.bit_length() - 1
    return sum(((place >> b) & 1) << (bits - 1 - b) for b in range(bits))


def assemble(wires, shard_rows, half_width, parts):
    count = wires.fsdp_count
    operands, plan = [], []
    for pieces, width, start, by_x, offset in parts:
        plan.append((width, start, by_x, offset))
        operands += pieces
    shape = (count, shard_rows, 2 * half_width)
    full = pl.pallas_call(
        functools.partial(assemble_kernel, parts=plan, half_width=half_width),
        out_shape=jax.ShapeDtypeStruct(shape, LOW),
        in_specs=[pl.BlockSpec(memory_space=pltpu.SMEM)]
        + [pl.BlockSpec(memory_space=pl.ANY)] * len(operands),
        out_specs=pl.BlockSpec(memory_space=pltpu.VMEM),
        scratch_shapes=[pltpu.SemaphoreType.DMA],
        cost_estimate=pl.CostEstimate(
            flops=0, bytes_accessed=4 * math.prod(shape), transcendentals=0
        ),
        name="assemble",
    )(wires.meta, *operands)
    return full.reshape(count * shard_rows, 2 * half_width)


def pair_columns(array, pairs, model_width):
    return jnp.concatenate(
        [
            array[..., part * model_width + p * LANES : part * model_width + (p + 1) * LANES]
            for p in pairs
            for part in range(3)
        ],
        axis=-1,
    )


def natural_columns(pieces, chunks):
    where = {}
    for piece, chunk in zip(pieces, chunks):
        for i, p in enumerate(chunk.pairs):
            for part in range(3):
                place = (3 * i + part) * LANES
                where[(part, p)] = piece[..., place : place + LANES]
    return jnp.concatenate([where[key] for key in sorted(where)], axis=-1)


def body(
    fsdp_count,
    layer_input,
    segment_ids,
    joint_weight,
    query_bias,
    value_bias,
    close_weight,
    close_bias,
    first_gain,
    first_shift,
    expand_weight,
    expand_bias,
    shrink_weight,
    shrink_bias,
    second_gain,
    second_shift,
    cotangent,
):
    row_count, pos_count, model_width = layer_input.shape
    hidden_units = expand_bias.shape[0]
    tok_count = row_count * pos_count
    flat_input = layer_input.reshape(tok_count, model_width)
    wires = Wires(fsdp_count)
    half_pairs = model_width // LANES // 2
    small, large = Chunk(0, 1, half_pairs), Chunk(1, half_pairs - 1, half_pairs)
    chunks = (small, large)
    shard_rows = joint_weight.shape[0]

    joint_pieces = []
    for chunk in chunks:
        low, high = (
            pair_columns(joint_weight, chunk.pairs[c * chunk.count : (c + 1) * chunk.count], model_width)
            for c in range(2)
        )
        joint_pieces.append(wires.own_rows(wires.own_half(low, high))[0])
    unit = hidden_units // 4
    expand_half = wires.own_half(expand_weight[:, : 2 * unit], expand_weight[:, 2 * unit :])
    close_half = wires.own_half(
        close_weight[:, : model_width // 2], close_weight[:, model_width // 2 :]
    )
    plain_piece = jnp.concatenate([expand_half[:, :unit], close_half], axis=1)
    split_piece = wires.own_rows(expand_half[:, unit:])[0]
    shrink_piece = wires.own_half(
        shrink_weight[:, : model_width // 2], shrink_weight[:, model_width // 2 :]
    )
    aligned = shard_rows % 32 == 0
    query_rows = query_bias.astype(WIDE).reshape(-1, LANES)
    value_rows = value_bias.astype(WIDE).reshape(-1, LANES)
    half_model = model_width // 2
    behind = ((), (), ())
    if aligned:
        first, second = joint_pieces[0][None], joint_pieces[1][None]
        plain, split, shrink = plain_piece[None], split_piece[None], shrink_piece[None]
        *outer, inner = wires.steps()

        def join(held, got):
            return jnp.concatenate([held, got], axis=0)

        for mask in outer:
            got = wires.swap(first, mask)
            first = join(first, got)
        first, second = tie(first, second)
        got = wires.swap(first, inner)
        second_got = wires.swap(second, outer[0])
        got, second_got = tie(got, second_got)
        first, second = join(first, got), join(second, second_got)
        first_x = wires.swap(first, 2)
        for mask in outer[1:]:
            second = join(second, wires.swap(second, mask))
        first_x, second, plain = tie(first_x, second, plain)
        second_got = wires.swap(second, inner)
        for mask in outer:
            plain = join(plain, wires.swap(plain, mask))
        second = join(second, second_got)
        plain, second, split = tie(plain, second, split)
        second_x = wires.swap(second, 2)
        plain_got = wires.swap(plain, inner)
        for mask in outer:
            split = join(split, wires.swap(split, mask))
        split, shrink, plain_got = tie(split, shrink, plain_got)
        plain = join(plain, plain_got)
        split = join(split, wires.swap(split, inner))
        second_x, split = tie(second_x, split)
        split_x = wires.swap(split, 2)
        for mask in outer:
            shrink = join(shrink, wires.swap(shrink, mask))
        split, shrink = tie(split, shrink)
        shrink = join(shrink, wires.swap(shrink, inner))
        joint_shared = [wires.share([first, first_x]), wires.share([second, second_x])]
        split_shared = wires.share([split, split_x])
        plain_shared = wires.share([plain])
        shrink_shared = wires.share([shrink])
    else:
        joint_shared = [
            lax.all_gather(
                pair_columns(joint_weight, c.pairs, model_width), "fsdp", axis=0, tiled=True
            )
            for c in chunks
        ]

    joint_full, mixed, weights, inverse = [], [], [], []
    context = None
    for shared, chunk in zip(joint_shared, chunks):
        full, part = joint_project(
            wires, flat_input, shared, query_rows, value_rows, chunk, shard_rows
        )
        joint_full.append(full)
        mixed.append(part.reshape(row_count, pos_count, -1))
        context, w, inv = attend(mixed[-1], segment_ids, chunk, context)
        weights.append(w)
        inverse.append(inv)
    context_low = context.reshape(tok_count, model_width)

    if aligned:
        close_full = assemble(
            wires, shard_rows, half_model, [(plain_shared, half_model, unit, False, 0)]
        )
        expand_full = assemble(
            wires,
            shard_rows,
            hidden_units // 2,
            [(plain_shared, unit, 0, False, 0), (split_shared, unit, 0, True, unit)],
        )
        shrink_full = assemble(
            wires, shrink_weight.shape[0], half_model, [(shrink_shared, half_model, 0, False, 0)]
        )
    else:
        close_full, expand_full, shrink_full = (
            lax.all_gather(w, "fsdp", axis=0, tiled=True)
            for w in (close_weight, expand_weight, shrink_weight)
        )

    branch = jnp.dot(context_low, close_full, preferred_element_type=WIDE) + row(close_bias)
    first_sum = flat_input.astype(WIDE) + branch
    hidden, first_pull = jax.vjp(
        layer_norm, first_sum, row(first_gain), row(first_shift)
    )
    hidden_low = hidden.astype(LOW)
    active_low, slope = expand_gelu(hidden_low, expand_full, row(expand_bias))
    ffn_out = jnp.dot(active_low, shrink_full, preferred_element_type=WIDE) + row(shrink_bias)
    output, second_pull = jax.vjp(
        layer_norm, hidden + ffn_out, row(second_gain), row(second_shift)
    )
    layer_output = output.astype(LOW).reshape(row_count, pos_count, model_width)
    grad_second, second_gain_part, second_shift_part = second_pull(
        cotangent.reshape(tok_count, model_width).astype(WIDE)
    )
    grad_ffn = grad_second.astype(LOW)

    def outgoing(left, right):
        half = right.shape[1] // 2
        send = wires.other_half(right[:, :half], right[:, half:])
        return jnp.einsum("tf,td->fd", left, send, preferred_element_type=WIDE).astype(LOW)

    def staying(left, right, got):
        half = right.shape[1] // 2
        keep = wires.own_half(right[:, :half], right[:, half:])
        keep = jnp.einsum("tf,td->fd", left, keep, preferred_element_type=WIDE)
        held = (keep + got.astype(WIDE)).astype(LOW)
        return held.reshape(fsdp_count, held.shape[0] // fsdp_count, half)

    def both_halves(mine):
        other = wires.swap(mine, 1)
        return wires.own_half(mine, other), wires.own_half(other, mine)

    shrink_send = outgoing(active_low, grad_ffn)
    grad_ffn, shrink_send = tie(grad_ffn, shrink_send)
    shrink_got = wires.swap(shrink_send, 1)
    grad_active = jnp.einsum("td,fd->tf", grad_ffn, shrink_full, preferred_element_type=WIDE)
    grad_inner = (grad_active * slope.astype(WIDE)).astype(LOW)
    active_low, grad_inner = tie(active_low, grad_inner)
    shrink_held = staying(active_low, grad_ffn, shrink_got)
    hidden_low, shrink_held = tie(hidden_low, shrink_held)
    shrink_steps = wires.halve_steps(shrink_held)
    expand_send = outgoing(hidden_low, grad_inner)
    grad_inner, expand_send = tie(grad_inner, expand_send)
    expand_got = wires.swap(expand_send, 1)
    grad_hidden = grad_second + jnp.einsum(
        "tf,df->td", grad_inner, expand_full, preferred_element_type=WIDE
    )
    grad_first, first_gain_part, first_shift_part = first_pull(grad_hidden)
    grad_branch = grad_first.astype(LOW)
    hidden_low, grad_branch = tie(hidden_low, grad_branch)
    expand_held = staying(hidden_low, grad_inner, expand_got)
    context_low, expand_held = tie(context_low, expand_held)
    close_send = outgoing(context_low, grad_branch)
    grad_branch, close_send = tie(grad_branch, close_send)
    close_got = wires.swap(close_send, 1)
    grad_context = jnp.einsum(
        "te,de->td", grad_branch, close_full, preferred_element_type=WIDE
    ).astype(LOW)
    context_low, grad_context = tie(context_low, grad_context)
    close_held = staying(context_low, grad_branch, close_got)
    grad_context = grad_context.reshape(row_count, pos_count, model_width)
    second_keep, second_send = wires.own_rows(
        jnp.concatenate([expand_held, close_held], axis=2), axis=1
    )
    second_got = wires.swap(second_send, 2)

    shrink_now = next(shrink_steps)
    grad_mixed, bias_sums = {}, {}
    grad_mixed[1], bias_sums[1] = attend_back(
        mixed[1],
        weights[1],
        context,
        inverse[1],
        grad_context,
        chunks[1],
        [shrink_now, second_send],
    )
    grad_mixed[1] = grad_mixed[1].reshape(tok_count, -1)
    send = outgoing(flat_input, grad_mixed[1])
    flat_input, send = tie(flat_input, send)
    held = staying(flat_input, grad_mixed[1], wires.swap(send, 1))
    large_steps = wires.all_steps(held)
    shrink_now = next(shrink_steps)
    grad_mixed[0], bias_sums[0] = attend_back(
        mixed[0],
        weights[0],
        context,
        inverse[0],
        grad_context,
        chunks[0],
        [shrink_now, held],
    )
    grad_mixed[0] = grad_mixed[0].reshape(tok_count, -1)
    send = outgoing(flat_input, grad_mixed[0])
    flat_input, send = tie(flat_input, send)
    held = staying(flat_input, grad_mixed[0], wires.swap(send, 1))
    grad_mixed[0], grad_mixed[1], held = tie(grad_mixed[0], grad_mixed[1], held)
    small_steps = wires.all_steps(held)
    second_steps = wires.x_steps(second_keep, second_got)
    input_grad = (
        grad_first
        + jnp.einsum("te,de->td", grad_mixed[0], joint_full[0], preferred_element_type=WIDE)
        + jnp.einsum("te,de->td", grad_mixed[1], joint_full[1], preferred_element_type=WIDE)
    )
    for shrink_now in shrink_steps:
        pass
    shrink_mine = add_low(shrink_now, wires.swap(shrink_now, 2))
    second_mine, large_mine, small_mine = (last(v) for v in (second_steps, large_steps, small_steps))
    joint_mine = (small_mine, large_mine)

    def column_sum(value):
        return jnp.sum(value.astype(WIDE), axis=0, keepdims=True)

    packed = pack(
        [bias_sums[0], bias_sums[1]],
        chunks,
        [
            column_sum(grad_branch),
            first_gain_part,
            first_shift_part,
            column_sum(grad_ffn),
            second_gain_part,
            second_shift_part,
            column_sum(grad_inner),
        ],
        model_width,
    )
    summed = wires.reduce_vector(packed)
    (
        query_bias_grad,
        value_bias_grad,
        close_bias_grad,
        first_gain_grad,
        first_shift_grad,
        shrink_bias_grad,
        second_gain_grad,
        second_shift_grad,
    ) = (summed[i] for i in range(8))
    expand_bias_grad = summed[8 : 8 + hidden_units // model_width].reshape(hidden_units)

    shrink_grad = jnp.concatenate(both_halves(shrink_mine), axis=1).astype(WIDE)
    low, high = both_halves(second_mine)
    cut = hidden_units // 2
    expand_grad = jnp.concatenate([low[:, :cut], high[:, :cut]], axis=1).astype(WIDE)
    close_grad = jnp.concatenate([low[:, cut:], high[:, cut:]], axis=1).astype(WIDE)
    joint_grad = natural_columns(
        [jnp.concatenate(both_halves(joint_mine[i]), axis=1) for i in range(2)], chunks
    ).astype(WIDE)
    return (
        layer_output,
        input_grad.reshape(row_count, pos_count, model_width),
        joint_grad,
        query_bias_grad,
        value_bias_grad,
        close_grad,
        close_bias_grad,
        first_gain_grad,
        first_shift_grad,
        expand_grad,
        expand_bias_grad,
        shrink_grad,
        shrink_bias_grad,
        second_gain_grad,
        second_shift_grad,
    )


def solution(mesh):
    rows = P(("fsdp", "rep"), None, None)
    sharded = P("fsdp", None)
    copied = P()
    return jax.shard_map(
        functools.partial(body, mesh.shape["fsdp"]),
        mesh=mesh,
        in_specs=(
            rows,
            P(("fsdp", "rep"), None),
            sharded,
            copied,
            copied,
            sharded,
            copied,
            copied,
            copied,
            sharded,
            copied,
            sharded,
            copied,
            copied,
            copied,
            rows,
        ),
        out_specs=(
            rows,
            rows,
            sharded,
            copied,
            copied,
            sharded,
            copied,
            copied,
            copied,
            sharded,
            copied,
            sharded,
            copied,
            copied,
            copied,
        ),
        check_vma=False,
    )
```

time: 944 us -> 454 us (0.48)
  waiting for transfers between devices: 603 us -> 156 us
  matrix products: 173 us -> 70.7 us
  Pallas kernels: 0 us -> 84.3 us
  starting transfers between devices: 0.36 us -> 54.7 us
  blocking collectives: 43.5 us -> 0 us
  local copies, waits for them, and re-layouts: 48.9 us -> 29.7 us
  between operations: 14.5 us -> 2.04 us
    reduce_scatter x3 -> x0, waiting for transfers between devices: 325 us -> none  [the longest x1 163 us: body(): lax.psum_scatter(shrink_term, 'fsdp', scatter_dimension=0, tiled=True)]
    all_gather x4 -> x0, waiting for transfers between devices: 181 us -> none  [the longest x1 75.9 us: body(): lax.all_gather(expand_weight, 'fsdp', axis=0, tiled=True)]
    ppermute x0 -> x57, waiting for transfers between devices: none -> 156 us  [swap(): return lax.ppermute(value, AXES, [(i, i ^ mask) for i in range(self.total)])]
    dot_general x26 -> x17, matrix products: 173 us -> 70.7 us  [the longest x5 16.8 us: staying(): keep = jnp.einsum('tf,td->fd', left, keep, preferred_element_type=WIDE)]
    pallas_call x0 -> x11, Pallas kernels: none -> 84.3 us  [the longest x2 22.5 us: attend_back(): pl.pallas_call(attend_back_kernel, grid=(rows, count), in_specs=[pl.Block...]
    unnamed x10 -> x0, waiting for transfers between devices: 56.7 us -> none
    ppermute x0 -> x57, starting transfers between devices: none -> 54.7 us  [swap(): return lax.ppermute(value, AXES, [(i, i ^ mask) for i in range(self.total)])]
    psum x1 -> x0, blocking collectives: 43.5 us -> none  [body(): lax.psum((vector_terms[0], vector_terms[1], vector_terms[2], vector_terms...]
  transfers between devices with their start and end apart: 9 -> 57, of which waited for: 8 -> 33; matrix products, arithmetic and copies ran while one was open for 22% -> 22% of each run, Pallas kernels for 0% -> 18%
where the time goes in v2:
time: 454 us; the launch traced here: 448 us
  waiting for transfers between devices  156 us (34%)
  Pallas kernels  84.3 us (19%)
  matrix products  70.7 us (16%)
  starting transfers between devices  54.7 us (12%)
  other arithmetic  50.3 us (11%)
  local copies, waits for them, and re-layouts  29.7 us (7%)
    ppermute x57, waiting for transfers between devices, swap(): return lax.ppermute(value, AXES, [(i, i ^ mask) for i in range(self.total)])  156 us
    ppermute x57, starting transfers between devices, swap(): return lax.ppermute(value, AXES, [(i, i ^ mask) for i in range(self.total)])  54.7 us
    pallas_call x2, Pallas kernels, attend_back(): pl.pallas_call(attend_back_kernel, grid=(rows, count), in_specs=[pl.Block...  22.5 us
    pallas_call x2, Pallas kernels, attend(): pl.pallas_call(attend_kernel, grid=(rows, count), in_specs=in_specs, out_...  21.1 us
    dot_general x5, matrix products, staying(): keep = jnp.einsum('tf,td->fd', left, keep, preferred_element_type=WIDE)  16.8 us
    unnamed x123, local copies, waits for them, and re-layouts  16.6 us
    dot_general x5, matrix products, outgoing(): jnp.einsum('tf,td->fd', left, send, preferred_element_type=WIDE).astype(LOW)  15.9 us
    pallas_call x2, Pallas kernels, joint_project(): pl.pallas_call(functools.partial(project_kernel, parts=[(half_width, 0, T...  13.9 us
  transfers between devices with their start and end apart: 57, of which 33 were waited for; matrix products, arithmetic and copies ran while one was open for 22% of the time, Pallas kernels for 18%

profile of v2, /device:TPU:0, one launch (start us, length us, event | category | flops | bytes accessed | tf_op | source)
XLA Modules:
  0.0 447.9 jit_solution(6638501547143774654)
XLA Ops:
  27.2 6.2 %collective-permute-done.5 = bf16[2,48,768]{2,1,0:T(8,128)(2,1)S(1)} collective-permute-done((bf16[2,48,768]{2,1,0:T(8,128)(2,1)S(1)}, bf16[2,48,768]{2,1,0:T(8,128)(2,1)S(1)}, u32[]{:S(2)}, u32[]{:S(2)}) %collective-permute-start.5) | collective-permute-done | bytes 147488 | tf_op jit(solution)/shard_map/ppermute | solution.py:212
  35.3 7.0 %collective-permute-done.6 = bf16[1,96,1152]{2,1,0:T(8,128)(2,1)S(1)} collective-permute-done((bf16[1,96,1152]{2,1,0:T(8,128)(2,1)S(1)}, bf16[1,96,1152]{2,1,0:T(8,128)(2,1)S(1)}, u32[]{:S(2)}, u32[]{:S(2)}) %collective-permute-start.6) | collective-permute-done | bytes 221216 | tf_op jit(solution)/shard_map/ppermute | solution.py:212
  43.0 9.1 %collective-permute-done.8 = bf16[4,48,768]{2,1,0:T(8,128)(2,1)S(1)} collective-permute-done((bf16[4,48,768]{2,1,0:T(8,128)(2,1)S(1)}, bf16[4,48,768]{2,1,0:T(8,128)(2,1)S(1)}, u32[]{:S(2)}, u32[]{:S(2)}) %collective-permute-start.8) | collective-permute-done | bytes 294944 | tf_op jit(solution)/shard_map/ppermute | solution.py:212
  63.7 4.4 collective-permute-done.12
  72.8 5.5 %collective-permute-done.19 = bf16[1,384,384]{2,1,0:T(8,128)(2,1)S(1)} collective-permute-done((bf16[1,384,384]{2,1,0:T(8,128)(2,1)S(1)}, bf16[1,384,384]{2,1,0:T(8,128)(2,1)S(1)}, u32[]{:S(2)}, u32[]{:S(2)}) %collective-permute-start.19) | collective-permute-done | bytes 294944 | tf_op jit(solution)/shard_map/ppermute | solution.py:212
  81.9 4.5 %collective-permute-done.9.refs_1_ = bf16[8,48,768]{2,1,0:T(8,128)(2,1)S(1)} collective-permute-done((bf16[8,48,768]{2,1,0:T(8,128)(2,1)S(1)}, bf16[8,48,768]{2,1,0:T(8,128)(2,1)S(1)}, u32[]{:S(2)}, u32[]{:S(2)}) %collective-permute-start.9) | collective-permute-done | bytes 589856 | tf_op jit(solution)/shard_map/ppermute | solution.py:212
  102.4 5.6 %joint_project.3 = (bf16[8,96,768]{2,1,0:T(8,128)(2,1)}, bf16[1024,768]{1,0:T(8,128)(2,1)}) custom-call(s32[3]{0:T(128)} %pad_add_fusion.meta_ref, bf16[1024,768]{1,0:T(8,128)(2,1)} %bitcast.293, f32[6,128]{1,0:T(8,128)} %get-tuple-element.179.query_ref, f32[6,128]{1,0:T(8,128)} %get-tuple-element.178.value_ref, ...), custom_call_target="tpu_custom_call" | custom-call | flops 1207959552 | bytes 5111808 | tf_op jit(solution)/shard_map/joint_project/pallas_call | solution.py:370
  108.0 7.7 %attend.2 = (bf16[2,512,768]{2,1,0:T(8,128)(2,1)}, bf16[2,2,2,512,512]{4,3,2,1,0:T(8,128)(2,1)}, f32[2,512,256]{2,1,0:T(8,128)}) custom-call(bf16[2,512,768]{2,1,0:T(8,128)(2,1)} %bitcast.307, s32[2,512,1]{2,1,0:T(8,128)} %copy.66.seg_col_ref, s32[2,1,512]{2,1,0:T(1,128)} %broadcast_in_dim.54.seg_row_ref), custom_call_target="tpu_custom_call" | custom-call | flops 2147483648 | bytes 8388608 | tf_op jit(solution)/shard_map/attend/pallas_call | solution.py:108
  116.3 8.2 %joint_project.2 = (bf16[8,96,1536]{2,1,0:T(8,128)(2,1)}, bf16[1024,1536]{1,0:T(8,128)(2,1)}) custom-call(s32[3]{0:T(128)} %pad_add_fusion.meta_ref, bf16[1024,768]{1,0:T(8,128)(2,1)} %bitcast.294, f32[6,128]{1,0:T(8,128)} %get-tuple-element.179.query_ref, f32[6,128]{1,0:T(8,128)} %get-tuple-element.178.value_ref, bf16[8,48,768]{2,1,0:T(8,128)(2,1)} %copy-done.20, ...), custom_call_target="tpu_custom_call" | custom-call | flops 2415919104 | bytes 10223616 | tf_op jit(solution)/shard_map/joint_project/pallas_call | solution.py:370
  129.7 13.3 %attend.3 = (bf16[2,512,768]{2,1,0:T(8,128)(2,1)}, bf16[2,4,2,512,512]{4,3,2,1,0:T(8,128)(2,1)}, f32[2,512,512]{2,1,0:T(8,128)}) custom-call(bf16[2,512,1536]{2,1,0:T(8,128)(2,1)} %bitcast.301, s32[2,512,1]{2,1,0:T(8,128)} %copy.66.seg_col_ref, s32[2,1,512]{2,1,0:T(1,128)} %broadcast_in_dim.54.seg_row_ref, ...), custom_call_target="tpu_custom_call", output_to_operand_aliasing={{0}: (3, {})} | custom-call | flops 4294967296 | bytes 16777216 | tf_op jit(solution)/shard_map/attend/pallas_call | solution.py:108
  147.3 5.2 %assemble.4 = bf16[8,96,3072]{2,1,0:T(8,128)(2,1)} custom-call(s32[3]{0:T(128)} %pad_add_fusion.meta_ref, bf16[8,96,1152]{2,1,0:T(8,128)(2,1)} %copy-done.6, bf16[8,96,1152]{2,1,0:T(8,128)(2,1)} %copy-done.9, bf16[8,48,768]{2,1,0:T(8,128)(2,1)} %pad_maximum_fusion.4.refs_2_, bf16[8,48,768]{2,1,0:T(8,128)(2,1)} %collective-permute-done.21.refs_3_, ...), custom_call_target="tpu_custom_call" | custom-call | bytes 9437184 | tf_op jit(solution)/shard_map/assemble/pallas_call | solution.py:431
  158.5 11.8 %expand_gelu.1 = (bf16[1024,3072]{1,0:T(8,128)(2,1)}, bf16[1024,3072]{1,0:T(8,128)(2,1)}) custom-call(bf16[1024,768]{1,0:T(8,128)(2,1)} %fusion.15.hidden_ref, bf16[768,3072]{1,0:T(8,128)(2,1)} %bitcast.275, f32[1,3072]{1,0:T(1,128)} %bitcast.292), custom_call_target="tpu_custom_call" | custom-call | flops 7247757312 | bytes 17301504 | tf_op jit(solution)/shard_map/expand_gelu/pallas_call | solution.py:182
  170.3 5.3 %assemble.5 = bf16[8,384,768]{2,1,0:T(8,128)(2,1)} custom-call(s32[3]{0:T(128)} %pad_add_fusion.meta_ref, bf16[8,384,384]{2,1,0:T(8,128)(2,1)} %constant_dynamic-update-slice_fusion.16.refs_0_, bf16[8,384,384]{2,1,0:T(8,128)(2,1)} %collective-permute-done.25.refs_1_), custom_call_target="tpu_custom_call" | custom-call | bytes 9437184 | tf_op jit(solution)/shard_map/assemble/pallas_call | solution.py:431
  175.6 9.0 %fusion.97 = (f32[1024]{0:T(1024)S(1)}, f32[1024,768]{1,0:T(8,128)S(1)}) fusion(f32[768]{0:T(1024)S(1)} %copy-done.29, bf16[1024,3072]{1,0:T(8,128)(2,1)} %get-tuple-element.96, bf16[3072,768]{1,0:T(8,128)(2,1)} %bitcast.279, f32[768]{0:T(1024)S(1)} %convert_element_type.348, f32[768]{0:T(1024)S(1)} %convert_element_type.347, f32[1024]{0:T(1024)S(1)} %fusion.92, ...), kind=kOutput, calls=%fused_computation.249 | convolution fusion | flops 4837342208 | bytes 17323008 | tf_op jit(solution)/shard_map/dot_general | solution.py:607
  191.8 4.8 %convolution_convert_fusion = bf16[3072,384]{1,0:T(8,128)(2,1)} fusion(bf16[1024,3072]{1,0:T(8,128)(2,1)S(1)} %bitcast.319, bf16[1024,768]{1,0:T(8,128)(2,1)S(1)} %add_convert_fusion.4, pred[]{:T(512)S(6)} %eq.5), kind=kOutput, calls=%fused_computation.6 | convolution fusion | flops 2417491968 | bytes 10223617 | tf_op jit(solution)/shard_map/tf,td->fd/dot_general | solution.py:620
  197.7 10.4 %fusion.98 = f32[1024,3072]{1,0:T(8,128)} fusion(bf16[1024,768]{1,0:T(8,128)(2,1)} %copy-done.10, bf16[3072,768]{1,0:T(8,128)(2,1)} %bitcast.280), kind=kOutput, calls=%fused_computation.250 | convolution fusion | flops 4831838208 | bytes 18874368 | tf_op jit(solution)/shard_map/td,fd->tf/dot_general | solution.py:636
  208.2 11.3 %multiply_convert_fusion = bf16[1024,3072]{1,0:T(8,128)(2,1)} fusion(f32[1024,3072]{1,0:T(8,128)} %fusion.98, bf16[1024,3072]{1,0:T(8,128)(2,1)} %get-tuple-element.94), kind=kLoop, calls=%fused_computation.1 | loop fusion | flops 9437184 | bytes 25165824 | tf_op jit(solution)/shard_map/convert_element_type | solution.py:637
  219.5 7.5 %add_convert_fusion.1 = bf16[3072,384]{1,0:T(8,128)(2,1)S(1)} fusion(bf16[3072,384]{1,0:T(8,128)(2,1)} %collective-permute-done.26, bf16[1024,3072]{1,0:T(8,128)(2,1)} %get-tuple-element.96, bf16[1024,768]{1,0:T(8,128)(2,1)} %copy-done.10, pred[]{:T(512)S(6)} %eq.5), kind=kOutput, calls=%fused_computation.5 | convolution fusion | flops 2419851264 | bytes 12582913 | tf_op jit(solution)/shard_map/tf,td->fd/dot_general | solution.py:625
  227.1 4.3 convolution_convert_fusion.1
  233.7 6.4 %multiply_reduce_fusion = (f32[768]{0:T(1024)}, f32[1024]{0:T(1024)S(1)}, f32[768]{0:T(1024)}, f32[1024,768]{1,0:T(8,128)S(1)}) fusion(f32[1024,768]{1,0:T(8,128)S(1)} %get-tuple-element.174, f32[1024]{0:T(1024)S(1)} %fusion.92, f32[1024]{0:T(1024)S(1)} %broadcast_multiply_fusion.1, f32[768]{0:T(1024)S(1)} %convert_element_type.347, ...), kind=kOutput, calls=%fused_computation.16 | convolution fusion | flops 4839699456 | bytes 20472832 | tf_op jit(solution)/shard_map/tf,df->td/dot_general | solution.py:645
  240.0 21.3 %collective-permute-done.28 = bf16[4,384,384]{2,1,0:T(8,128)(2,1)} collective-permute-done((bf16[4,384,384]{2,1,0:T(8,128)(2,1)}, bf16[4,384,384]{2,1,0:T(8,128)(2,1)}, u32[]{:S(2)}, u32[]{:S(2)}) %collective-permute-start.28) | collective-permute-done | bytes 1179680 | tf_op jit(solution)/shard_map/ppermute | solution.py:212
  266.3 11.5 %collective-permute-done.29 = bf16[2,384,384]{2,1,0:T(8,128)(2,1)S(1)} collective-permute-done((bf16[2,384,384]{2,1,0:T(8,128)(2,1)S(1)}, bf16[2,384,384]{2,1,0:T(8,128)(2,1)S(1)}, u32[]{:S(2)}, u32[]{:S(2)}) %collective-permute-start.29) | collective-permute-done | bytes 589856 | tf_op jit(solution)/shard_map/ppermute | solution.py:212
  278.1 4.5 %add_convert_fusion = bf16[768,1536]{1,0:T(8,128)(2,1)S(1)} fusion(bf16[768,1536]{1,0:T(8,128)(2,1)} %collective-permute-done.27, bf16[1024,768]{1,0:T(8,128)(2,1)S(1)} %copy-done.17, bf16[1024,3072]{1,0:T(8,128)(2,1)S(1)} %copy-done, pred[]{:T(512)S(6)} %eq.5), kind=kOutput, calls=%fused_computation.4 | convolution fusion | flops 2421030912 | bytes 12582913 | tf_op jit(solution)/shard_map/tf,td->fd/dot_general | solution.py:625
  290.4 14.3 %attend_back.2 = (bf16[2,512,1536]{2,1,0:T(8,128)(2,1)}, f32[2,4,8,384]{3,2,1,0:T(8,128)}) custom-call(bf16[2,512,1536]{2,1,0:T(8,128)(2,1)} %bitcast.302, bf16[2,4,2,512,512]{4,3,2,1,0:T(8,128)(2,1)} %get-tuple-element.109.weights_ref, bf16[2,512,768]{2,1,0:T(8,128)(2,1)} %get-tuple-element.86.context_ref, f32[2,512,512]{2,1,0:T(8,128)} %get-tuple-element.110.inverse_ref, ...), custom_call_target="tpu_custom_call" | custom-call | flops 8589934592 | bytes 16777216 | tf_op jit(solution)/shard_map/attend_back/pallas_call | solution.py:138
  314.9 6.2 %collective-permute-done.55 = bf16[384,384]{1,0:T(8,128)(2,1)S(1)} collective-permute-done((bf16[384,384]{1,0:T(8,128)(2,1)S(1)}, bf16[384,384]{1,0:T(8,128)(2,1)S(1)}, u32[]{:S(2)}, u32[]{:S(2)}) %collective-permute-start.55) | collective-permute-done | bytes 294944 | tf_op jit(solution)/shard_map/ppermute | solution.py:212
  327.4 8.2 %attend_back.3 = (bf16[2,512,768]{2,1,0:T(8,128)(2,1)}, f32[2,2,8,384]{3,2,1,0:T(8,128)}) custom-call(bf16[2,512,768]{2,1,0:T(8,128)(2,1)} %bitcast.308, bf16[2,2,2,512,512]{4,3,2,1,0:T(8,128)(2,1)} %get-tuple-element.100.weights_ref, bf16[2,512,768]{2,1,0:T(8,128)(2,1)} %get-tuple-element.86.context_ref, f32[2,512,256]{2,1,0:T(8,128)} %get-tuple-element.101.inverse_ref, ...), custom_call_target="tpu_custom_call" | custom-call | flops 4294967296 | bytes 8388608 | tf_op jit(solution)/shard_map/attend_back/pallas_call | solution.py:138
  341.0 17.7 %collective-permute-done.44 = f32[16,768]{1,0:T(8,128)S(1)} collective-permute-done((f32[16,768]{1,0:T(8,128)S(1)}, f32[16,768]{1,0:T(8,128)S(1)}, u32[]{:S(2)}, u32[]{:S(2)}) %collective-permute-start.44) | collective-permute-done | bytes 49184 | tf_op jit(solution)/shard_map/ppermute | solution.py:212
  381.6 5.2 %collective-permute-done.38 = bf16[4,96,768]{2,1,0:T(8,128)(2,1)} collective-permute-done((bf16[4,96,768]{2,1,0:T(8,128)(2,1)}, bf16[4,96,768]{2,1,0:T(8,128)(2,1)}, u32[]{:S(2)}, u32[]{:S(2)}) %collective-permute-start.38) | collective-permute-done | bytes 589856 | tf_op jit(solution)/shard_map/ppermute | solution.py:212
  392.0 4.4 add_add_fusion.2
  396.4 9.7 %collective-permute-done.33 = bf16[4,96,384]{2,1,0:T(8,128)(2,1)S(1)} collective-permute-done((bf16[4,96,384]{2,1,0:T(8,128)(2,1)S(1)}, bf16[4,96,384]{2,1,0:T(8,128)(2,1)S(1)}, u32[]{:S(2)}, u32[]{:S(2)}) %collective-permute-start.33) | collective-permute-done | bytes 294944 | tf_op jit(solution)/shard_map/ppermute | solution.py:212
  430.6 7.4 %collective-permute-done.51 = bf16[1,48,1920]{2,1,0:T(8,128)(2,1)S(1)} collective-permute-done((bf16[1,48,1920]{2,1,0:T(8,128)(2,1)S(1)}, bf16[1,48,1920]{2,1,0:T(8,128)(2,1)S(1)}, u32[]{:S(2)}, u32[]{:S(2)}) %collective-permute-start.51) | collective-permute-done | bytes 184352 | tf_op jit(solution)/shard_map/ppermute | solution.py:212
  439.0 4.7 %collective-permute-done.52 = bf16[48,1920]{1,0:T(8,128)(2,1)S(1)} collective-permute-done((bf16[48,1920]{1,0:T(8,128)(2,1)S(1)}, bf16[48,1920]{1,0:T(8,128)(2,1)S(1)}, u32[]{:S(2)}, u32[]{:S(2)}) %collective-permute-start.52) | collective-permute-done | bytes 184352 | tf_op jit(solution)/shard_map/ppermute | solution.py:212
  (353 shorter events, 183.1 us)
Async XLA Ops:
  42.3 9.9 %collective-permute-start.7 = (bf16[2,96,1152]{2,1,0:T(8,128)(2,1)S(1)}, bf16[2,96,1152]{2,1,0:T(8,128)(2,1)S(1)}, u32[]{:S(2)}, u32[]{:S(2)}) collective-permute-start(bf16[2,96,1152]{2,1,0:T(8,128)(2,1)S(1)} %pad_maximum_fusion.6), channel_id=1, source_target_pairs={{0,8},{1,9},{2,10},{3,11},{4,12},{5,13},{6,14},{7,15},{8,0},{9,1},... | collective-permute-start | bytes 1327112 | tf_op jit(solution)/shard_map/ppermute | solution.py:212
  42.4 9.7 %collective-permute-start.8 = (bf16[4,48,768]{2,1,0:T(8,128)(2,1)S(1)}, bf16[4,48,768]{2,1,0:T(8,128)(2,1)S(1)}, u32[]{:S(2)}, u32[]{:S(2)}) collective-permute-start(bf16[4,48,768]{2,1,0:T(8,128)(2,1)S(1)} %pad_maximum_fusion.8), channel_id=1, source_target_pairs={{0,4},{1,5},{2,6},{3,7},{4,0},{5,1},{6,2},{7,3},{8,12},{9,13},{10,... | collective-permute-start | bytes 884744 | tf_op jit(solution)/shard_map/ppermute | solution.py:212
  52.3 15.8 %collective-permute-start.12 = (bf16[4,96,1152]{2,1,0:T(8,128)(2,1)S(1)}, bf16[4,96,1152]{2,1,0:T(8,128)(2,1)S(1)}, u32[]{:S(2)}, u32[]{:S(2)}) collective-permute-start(bf16[4,96,1152]{2,1,0:T(8,128)(2,1)S(1)} %pad_maximum_fusion.2), channel_id=1, source_target_pairs={{0,4},{1,5},{2,6},{3,7},{4,0},{5,1},{6,2},{7,3},{8,12},{9,13},{10,... | collective-permute-start | bytes 2654216 | tf_op jit(solution)/shard_map/ppermute | solution.py:212
  68.2 10.1 %collective-permute-start.19 = (bf16[1,384,384]{2,1,0:T(8,128)(2,1)S(1)}, bf16[1,384,384]{2,1,0:T(8,128)(2,1)S(1)}, u32[]{:S(2)}, u32[]{:S(2)}) collective-permute-start(bf16[1,384,384]{2,1,0:T(8,128)(2,1)S(1)} %select_bitcast_fusion.6), channel_id=1, source_target_pairs={{0,16},{1,17},{2,18},{3,19},{4,20},{5,21},{6,22},{7,23},{8,24},{9,... | collective-permute-start | bytes 884744 | tf_op jit(solution)/shard_map/ppermute | solution.py:212
  70.6 21.2 %collective-permute-start.16 = (bf16[8,48,384]{2,1,0:T(8,128)(2,1)}, bf16[8,48,384]{2,1,0:T(8,128)(2,1)}, u32[]{:S(2)}, u32[]{:S(2)}) collective-permute-start(bf16[8,48,384]{2,1,0:T(8,128)(2,1)} %constant_dynamic-update-slice_fusion.12.refs_0_), channel_id=1, source_target_pairs={{0,1},{1,0},{2,3},{3,2},{4,5},{5,4},{6,7},{7,6},{8,9},{9,8},{10,11... | collective-permute-start | bytes 884744 | tf_op jit(solution)/shard_map/ppermute | solution.py:212
  70.6 22.8 %collective-permute-start.17 = (bf16[8,48,384]{2,1,0:T(8,128)(2,1)}, bf16[8,48,384]{2,1,0:T(8,128)(2,1)}, u32[]{:S(2)}, u32[]{:S(2)}) collective-permute-start(bf16[8,48,384]{2,1,0:T(8,128)(2,1)} %collective-permute-done.4.refs_1_), channel_id=1, source_target_pairs={{0,1},{1,0},{2,3},{3,2},{4,5},{5,4},{6,7},{7,6},{8,9},{9,8},{10,11... | collective-permute-start | bytes 884744 | tf_op jit(solution)/shard_map/ppermute | solution.py:212
  71.1 15.2 %collective-permute-start.9 = (bf16[8,48,768]{2,1,0:T(8,128)(2,1)S(1)}, bf16[8,48,768]{2,1,0:T(8,128)(2,1)S(1)}, u32[]{:S(2)}, u32[]{:S(2)}) collective-permute-start(bf16[8,48,768]{2,1,0:T(8,128)(2,1)S(1)} %pad_maximum_fusion.3.refs_0_), channel_id=1, source_target_pairs={{0,2},{1,3},{2,0},{3,1},{4,6},{5,7},{6,4},{7,5},{8,10},{9,11},{10,... | collective-permute-start | bytes 1769480 | tf_op jit(solution)/shard_map/ppermute | solution.py:212
  78.4 10.9 %collective-permute-start.20 = (bf16[2,384,384]{2,1,0:T(8,128)(2,1)S(1)}, bf16[2,384,384]{2,1,0:T(8,128)(2,1)S(1)}, u32[]{:S(2)}, u32[]{:S(2)}) collective-permute-start(bf16[2,384,384]{2,1,0:T(8,128)(2,1)S(1)} %pad_maximum_fusion.5), channel_id=1, source_target_pairs={{0,8},{1,9},{2,10},{3,11},{4,12},{5,13},{6,14},{7,15},{8,0},{9,1},... | collective-permute-start | bytes 1769480 | tf_op jit(solution)/shard_map/ppermute | solution.py:212
  81.0 62.0 %collective-permute-start.18 = (bf16[8,96,1152]{2,1,0:T(8,128)(2,1)S(1)}, bf16[8,96,1152]{2,1,0:T(8,128)(2,1)S(1)}, u32[]{:S(2)}, u32[]{:S(2)}) collective-permute-start(bf16[8,96,1152]{2,1,0:T(8,128)(2,1)S(1)} %constant_dynamic-update-slice_fusion.14.refs_0_), channel_id=1, source_target_pairs={{0,1},{1,0},{2,3},{3,2},{4,5},{5,4},{6,7},{7,6},{8,9},{9,8},{10,11... | collective-permute-start | bytes 5308424 | tf_op jit(solution)/shard_map/ppermute | solution.py:212
  90.5 36.5 %collective-permute-start.24 = (bf16[4,384,384]{2,1,0:T(8,128)(2,1)}, bf16[4,384,384]{2,1,0:T(8,128)(2,1)}, u32[]{:S(2)}, u32[]{:S(2)}) collective-permute-start(bf16[4,384,384]{2,1,0:T(8,128)(2,1)} %pad_maximum_fusion.1), channel_id=1, source_target_pairs={{0,4},{1,5},{2,6},{3,7},{4,0},{5,1},{6,2},{7,3},{8,12},{9,13},{10,... | collective-permute-start | bytes 3538952 | tf_op jit(solution)/shard_map/ppermute | solution.py:212
  91.8 23.9 %collective-permute-start.14 = (bf16[8,48,768]{2,1,0:T(8,128)(2,1)}, bf16[8,48,768]{2,1,0:T(8,128)(2,1)}, u32[]{:S(2)}, u32[]{:S(2)}) collective-permute-start(bf16[8,48,768]{2,1,0:T(8,128)(2,1)} %copy-done.20), channel_id=1, source_target_pairs={{0,1},{1,0},{2,3},{3,2},{4,5},{5,4},{6,7},{7,6},{8,9},{9,8},{10,11... | collective-permute-start | bytes 1769480 | tf_op jit(solution)/shard_map/ppermute | solution.py:212
  91.8 24.2 %collective-permute-start.21 = (bf16[8,48,768]{2,1,0:T(8,128)(2,1)}, bf16[8,48,768]{2,1,0:T(8,128)(2,1)}, u32[]{:S(2)}, u32[]{:S(2)}) collective-permute-start(bf16[8,48,768]{2,1,0:T(8,128)(2,1)} %pad_maximum_fusion.4.refs_2_), channel_id=1, source_target_pairs={{0,2},{1,3},{2,0},{3,1},{4,6},{5,7},{6,4},{7,5},{8,10},{9,11},{10,... | collective-permute-start | bytes 1769480 | tf_op jit(solution)/shard_map/ppermute | solution.py:212
  93.4 22.9 %collective-permute-start.15 = (bf16[8,48,768]{2,1,0:T(8,128)(2,1)}, bf16[8,48,768]{2,1,0:T(8,128)(2,1)}, u32[]{:S(2)}, u32[]{:S(2)}) collective-permute-start(bf16[8,48,768]{2,1,0:T(8,128)(2,1)} %copy-done.35), channel_id=1, source_target_pairs={{0,1},{1,0},{2,3},{3,2},{4,5},{5,4},{6,7},{7,6},{8,9},{9,8},{10,11... | collective-permute-start | bytes 1769480 | tf_op jit(solution)/shard_map/ppermute | solution.py:212
  115.7 31.5 %collective-permute-start.22 = (bf16[8,48,768]{2,1,0:T(8,128)(2,1)}, bf16[8,48,768]{2,1,0:T(8,128)(2,1)}, u32[]{:S(2)}, u32[]{:S(2)}) collective-permute-start(bf16[8,48,768]{2,1,0:T(8,128)(2,1)} %pad_maximum_fusion.4.refs_2_), channel_id=1, source_target_pairs={{0,1},{1,0},{2,3},{3,2},{4,5},{5,4},{6,7},{7,6},{8,9},{9,8},{10,11... | collective-permute-start | bytes 1769480 | tf_op jit(solution)/shard_map/ppermute | solution.py:212
  116.0 31.3 %collective-permute-start.23 = (bf16[8,48,768]{2,1,0:T(8,128)(2,1)}, bf16[8,48,768]{2,1,0:T(8,128)(2,1)}, u32[]{:S(2)}, u32[]{:S(2)}) collective-permute-start(bf16[8,48,768]{2,1,0:T(8,128)(2,1)} %collective-permute-done.21.refs_3_), channel_id=1, source_target_pairs={{0,1},{1,0},{2,3},{3,2},{4,5},{5,4},{6,7},{7,6},{8,9},{9,8},{10,11... | collective-permute-start | bytes 1769480 | tf_op jit(solution)/shard_map/ppermute | solution.py:212
  129.4 40.9 %collective-permute-start.25 = (bf16[8,384,384]{2,1,0:T(8,128)(2,1)}, bf16[8,384,384]{2,1,0:T(8,128)(2,1)}, u32[]{:S(2)}, u32[]{:S(2)}) collective-permute-start(bf16[8,384,384]{2,1,0:T(8,128)(2,1)} %constant_dynamic-update-slice_fusion.16.refs_0_), channel_id=1, source_target_pairs={{0,1},{1,0},{2,3},{3,2},{4,5},{5,4},{6,7},{7,6},{8,9},{9,8},{10,11... | collective-permute-start | bytes 7077896 | tf_op jit(solution)/shard_map/ppermute | solution.py:212
  196.6 22.9 %collective-permute-start.26 = (bf16[3072,384]{1,0:T(8,128)(2,1)}, bf16[3072,384]{1,0:T(8,128)(2,1)}, u32[]{:S(2)}, u32[]{:S(2)}) collective-permute-start(bf16[3072,384]{1,0:T(8,128)(2,1)} %convolution_convert_fusion), channel_id=1, source_target_pairs={{0,1},{1,0},{2,3},{3,2},{4,5},{5,4},{6,7},{7,6},{8,9},{9,8},{10,11... | collective-permute-start | bytes 7077896 | tf_op jit(solution)/shard_map/ppermute | solution.py:212
  231.4 46.7 %collective-permute-start.27 = (bf16[768,1536]{1,0:T(8,128)(2,1)}, bf16[768,1536]{1,0:T(8,128)(2,1)}, u32[]{:S(2)}, u32[]{:S(2)}) collective-permute-start(bf16[768,1536]{1,0:T(8,128)(2,1)} %convolution_convert_fusion.1), channel_id=1, source_target_pairs={{0,1},{1,0},{2,3},{3,2},{4,5},{5,4},{6,7},{7,6},{8,9},{9,8},{10,11... | collective-permute-start | bytes 7077896 | tf_op jit(solution)/shard_map/ppermute | solution.py:212
  232.9 28.4 %collective-permute-start.28 = (bf16[4,384,384]{2,1,0:T(8,128)(2,1)}, bf16[4,384,384]{2,1,0:T(8,128)(2,1)}, u32[]{:S(2)}, u32[]{:S(2)}) collective-permute-start(bf16[4,384,384]{2,1,0:T(8,128)(2,1)} %select_bitcast_fusion), channel_id=1, source_target_pairs={{0,4},{1,5},{2,6},{3,7},{4,0},{5,1},{6,2},{7,3},{8,12},{9,13},{10,... | collective-permute-start | bytes 3538952 | tf_op jit(solution)/shard_map/ppermute | solution.py:212
  263.2 14.7 %collective-permute-start.29 = (bf16[2,384,384]{2,1,0:T(8,128)(2,1)S(1)}, bf16[2,384,384]{2,1,0:T(8,128)(2,1)S(1)}, u32[]{:S(2)}, u32[]{:S(2)}) collective-permute-start(bf16[2,384,384]{2,1,0:T(8,128)(2,1)S(1)} %select_bitcast_fusion.3), channel_id=1, source_target_pairs={{0,8},{1,9},{2,10},{3,11},{4,12},{5,13},{6,14},{7,15},{8,0},{9,1},... | collective-permute-start | bytes 1769480 | tf_op jit(solution)/shard_map/ppermute | solution.py:212
  283.8 27.9 %collective-permute-start.54 = (bf16[1,384,384]{2,1,0:T(8,128)(2,1)S(1)}, bf16[1,384,384]{2,1,0:T(8,128)(2,1)S(1)}, u32[]{:S(2)}, u32[]{:S(2)}) collective-permute-start(bf16[1,384,384]{2,1,0:T(8,128)(2,1)S(1)} %select_bitcast_fusion.4), channel_id=1, source_target_pairs={{0,16},{1,17},{2,18},{3,19},{4,20},{5,21},{6,22},{7,23},{8,24},{9,... | collective-permute-start | bytes 884744 | tf_op jit(solution)/shard_map/ppermute | solution.py:212
  308.8 15.5 %collective-permute-start.31 = (bf16[768,768]{0,1:T(8,128)(2,1)S(1)}, bf16[768,768]{0,1:T(8,128)(2,1)S(1)}, u32[]{:S(2)}, u32[]{:S(2)}) collective-permute-start(bf16[768,768]{0,1:T(8,128)(2,1)S(1)} %fusion.30), channel_id=1, source_target_pairs={{0,1},{1,0},{2,3},{3,2},{4,5},{5,4},{6,7},{7,6},{8,9},{9,8},{10,11... | collective-permute-start | bytes 3538952 | tf_op jit(solution)/shard_map/ppermute | solution.py:212
  311.8 9.3 %collective-permute-start.55 = (bf16[384,384]{1,0:T(8,128)(2,1)S(1)}, bf16[384,384]{1,0:T(8,128)(2,1)S(1)}, u32[]{:S(2)}, u32[]{:S(2)}) collective-permute-start(bf16[384,384]{1,0:T(8,128)(2,1)S(1)} %fusion.80), channel_id=1, source_target_pairs={{0,2},{1,3},{2,0},{3,1},{4,6},{5,7},{6,4},{7,5},{8,10},{9,11},{10,... | collective-permute-start | bytes 884744 | tf_op jit(solution)/shard_map/ppermute | solution.py:212
  321.9 18.0 %collective-permute-start.56 = (bf16[384,384]{1,0:T(8,128)(2,1)}, bf16[384,384]{1,0:T(8,128)(2,1)}, u32[]{:S(2)}, u32[]{:S(2)}) collective-permute-start(bf16[384,384]{1,0:T(8,128)(2,1)} %add_convert_fusion.9), channel_id=1, source_target_pairs={{0,1},{1,0},{2,3},{3,2},{4,5},{5,4},{6,7},{7,6},{8,9},{9,8},{10,11... | collective-permute-start | bytes 884744 | tf_op jit(solution)/shard_map/ppermute | solution.py:212
  322.7 52.3 %collective-permute-start.48 = (bf16[8,48,1920]{2,1,0:T(8,128)(2,1)}, bf16[8,48,1920]{2,1,0:T(8,128)(2,1)}, u32[]{:S(2)}, u32[]{:S(2)}) collective-permute-start(bf16[8,48,1920]{2,1,0:T(8,128)(2,1)} %broadcast_select_fusion.refs_1_), channel_id=1, source_target_pairs={{0,2},{1,3},{2,0},{3,1},{4,6},{5,7},{6,4},{7,5},{8,10},{9,11},{10,... | collective-permute-start | bytes 4423688 | tf_op jit(solution)/shard_map/ppermute | solution.py:212
  339.4 19.3 %collective-permute-start.44 = (f32[16,768]{1,0:T(8,128)S(1)}, f32[16,768]{1,0:T(8,128)S(1)}, u32[]{:S(2)}, u32[]{:S(2)}) collective-permute-start(f32[16,768]{1,0:T(8,128)S(1)} %add.175), channel_id=1, source_target_pairs={{0,2},{1,3},{2,0},{3,1},{4,6},{5,7},{6,4},{7,5},{8,10},{9,11},{10,... | collective-permute-start | bytes 147464 | tf_op jit(solution)/shard_map/ppermute | solution.py:212
  366.5 11.9 %collective-permute-start.32 = (bf16[768,384]{1,0:T(8,128)(2,1)}, bf16[768,384]{1,0:T(8,128)(2,1)}, u32[]{:S(2)}, u32[]{:S(2)}) collective-permute-start(bf16[768,384]{1,0:T(8,128)(2,1)} %convolution_convert_fusion.3), channel_id=1, source_target_pairs={{0,1},{1,0},{2,3},{3,2},{4,5},{5,4},{6,7},{7,6},{8,9},{9,8},{10,11... | collective-permute-start | bytes 1769480 | tf_op jit(solution)/shard_map/ppermute | solution.py:212
  370.3 16.5 %collective-permute-start.38 = (bf16[4,96,768]{2,1,0:T(8,128)(2,1)}, bf16[4,96,768]{2,1,0:T(8,128)(2,1)}, u32[]{:S(2)}, u32[]{:S(2)}) collective-permute-start(bf16[4,96,768]{2,1,0:T(8,128)(2,1)} %select_bitcast_fusion.2), channel_id=1, source_target_pairs={{0,4},{1,5},{2,6},{3,7},{4,0},{5,1},{6,2},{7,3},{8,12},{9,13},{10,... | collective-permute-start | bytes 1769480 | tf_op jit(solution)/shard_map/ppermute | solution.py:212
  377.3 41.7 %collective-permute-start.49 = (bf16[4,48,1920]{2,1,0:T(8,128)(2,1)S(1)}, bf16[4,48,1920]{2,1,0:T(8,128)(2,1)S(1)}, u32[]{:S(2)}, u32[]{:S(2)}) collective-permute-start(bf16[4,48,1920]{2,1,0:T(8,128)(2,1)S(1)} %select_bitcast_fusion.1), channel_id=1, source_target_pairs={{0,4},{1,5},{2,6},{3,7},{4,0},{5,1},{6,2},{7,3},{8,12},{9,13},{10,... | collective-permute-start | bytes 2211848 | tf_op jit(solution)/shard_map/ppermute | solution.py:212
  380.6 25.6 %collective-permute-start.33 = (bf16[4,96,384]{2,1,0:T(8,128)(2,1)S(1)}, bf16[4,96,384]{2,1,0:T(8,128)(2,1)S(1)}, u32[]{:S(2)}, u32[]{:S(2)}) collective-permute-start(bf16[4,96,384]{2,1,0:T(8,128)(2,1)S(1)} %fusion.78), channel_id=1, source_target_pairs={{0,4},{1,5},{2,6},{3,7},{4,0},{5,1},{6,2},{7,3},{8,12},{9,13},{10,... | collective-permute-start | bytes 884744 | tf_op jit(solution)/shard_map/ppermute | solution.py:212
  388.1 19.9 %collective-permute-start.39 = (bf16[2,96,768]{2,1,0:T(8,128)(2,1)S(1)}, bf16[2,96,768]{2,1,0:T(8,128)(2,1)S(1)}, u32[]{:S(2)}, u32[]{:S(2)}) collective-permute-start(bf16[2,96,768]{2,1,0:T(8,128)(2,1)S(1)} %select_bitcast_fusion.5), channel_id=1, source_target_pairs={{0,8},{1,9},{2,10},{3,11},{4,12},{5,13},{6,14},{7,15},{8,0},{9,1},... | collective-permute-start | bytes 884744 | tf_op jit(solution)/shard_map/ppermute | solution.py:212
  408.2 10.0 %collective-permute-start.40 = (bf16[1,96,768]{2,1,0:T(8,128)(2,1)S(1)}, bf16[1,96,768]{2,1,0:T(8,128)(2,1)S(1)}, u32[]{:S(2)}, u32[]{:S(2)}) collective-permute-start(bf16[1,96,768]{2,1,0:T(8,128)(2,1)S(1)} %select_bitcast_fusion.8), channel_id=1, source_target_pairs={{0,16},{1,17},{2,18},{3,19},{4,20},{5,21},{6,22},{7,23},{8,24},{9,... | collective-permute-start | bytes 442376 | tf_op jit(solution)/shard_map/ppermute | solution.py:212
  (74 other events, 594.4 us)

commit v3 on v2

--- a/solution.py
+++ b/solution.py
@@ -198,6 +198,47 @@
     )(hidden, weight, bias)
 
 
+def inner_grad_kernel(grad_ref, weight_ref, slope_ref, out_ref, sum_ref, *, chunks):
+    step = grad_ref.shape[0] // chunks
+    total = jnp.zeros((1, weight_ref.shape[0]), WIDE)
+    for i in range(chunks):
+        cut = slice(i * step, (i + 1) * step)
+        grad = lax.dot_general(grad_ref[cut], weight_ref[...], NT, preferred_element_type=WIDE)
+        grad = (grad * slope_ref[cut].astype(WIDE)).astype(LOW)
+        out_ref[cut] = grad
+        total = total + jnp.sum(grad.astype(WIDE), axis=0, keepdims=True)
+    sum_ref[...] = total
+
+
+def inner_grad(grad, weight, slope):
+    tokens, model_width = grad.shape
+    units = weight.shape[0]
+    tile = 768
+    return pl.pallas_call(
+        functools.partial(inner_grad_kernel, chunks=4),
+        grid=(units // tile,),
+        in_specs=[
+            pl.BlockSpec((tokens, model_width), lambda j: (0, 0)),
+            pl.BlockSpec((tile, model_width), lambda j: (j, 0)),
+            pl.BlockSpec((tokens, tile), lambda j: (0, j)),
+        ],
+        out_specs=[
+            pl.BlockSpec((tokens, tile), lambda j: (0, j)),
+            pl.BlockSpec((1, tile), lambda j: (0, j)),
+        ],
+        out_shape=[
+            jax.ShapeDtypeStruct((tokens, units), LOW),
+            jax.ShapeDtypeStruct((1, units), WIDE),
+        ],
+        cost_estimate=pl.CostEstimate(
+            flops=2 * tokens * model_width * units,
+            bytes_accessed=4 * tokens * units + 2 * model_width * units,
+            transcendentals=0,
+        ),
+        name="inner_grad",
+    )(grad, weight, slope)
+
+
 class Wires:
     def __init__(self, fsdp_count):
         self.fsdp_count = fsdp_count
@@ -223,41 +264,45 @@
         high = lax.slice_in_dim(value, half, 2 * half, axis=axis)
         return jnp.where(self.x == 1, high, low), jnp.where(self.x == 1, low, high)
 
-
-    def steps(self):
-        masks, mask = [], self.total // 2
-        while mask >= 4:
-            masks.append(mask)
-            mask //= 2
-        return masks
+    def near(self, value):
+        return [self.swap(value, 8 * k) for k in range(1, self.fsdp_count // 2)]
 
     def share(self, near):
         return near + [self.swap(v, 1) for v in near]
 
 
-    def halve_steps(self, held):
-        bit = 1
+    def y_halves(self, held):
+        held = held.reshape((held.shape[0] // 2, 2) + held.shape[1:])
+        flag = (self.shard & 1) != 0
+        return jnp.where(flag, held[:, 1], held[:, 0]), jnp.where(flag, held[:, 0], held[:, 1])
+
+    def z_block(self, held, k):
+        return lax.dynamic_index_in_dim(held, (self.shard >> 1) ^ k, 0, keepdims=False)
+
+    def z_sends(self, held):
+        if held.shape[0] > 4:
+            return [held]
+        return [self.z_block(held, k) for k in range(1, held.shape[0])]
+
+    def z_swap(self, sends):
+        if sends[0].ndim == 2:
+            return [self.swap(v, 8 * (k + 1)) for k, v in enumerate(sends)]
+        held, bit = sends[0], 2
         while bit < self.fsdp_count:
             held = held.reshape((held.shape[0] // 2, 2) + held.shape[1:])
             flag = (self.shard & bit) != 0
-            send = jnp.where(flag, held[:, 0], held[:, 1])
-            keep = jnp.where(flag, held[:, 1], held[:, 0])
-            held = add_low(keep, self.swap(send, 4 * bit))
+            got = self.swap(jnp.where(flag, held[:, 0], held[:, 1]), 4 * bit)
+            held = add_low(jnp.where(flag, held[:, 1], held[:, 0]), got)
             bit *= 2
-            yield held if bit < self.fsdp_count else held[0]
-
-    def x_steps(self, keep, got):
-        held = add_low(keep, got)
-        for held in self.halve_steps(held):
-            yield held
-        other = self.swap(held, 2)
-        flag = self.x == 1
-        yield jnp.concatenate([jnp.where(flag, other, held), jnp.where(flag, held, other)], axis=0)
-
-    def all_steps(self, held):
-        for held in self.halve_steps(held):
-            yield held
-        yield add_low(held, self.swap(held, 2))
+        return [held[0]]
+
+    def z_sum(self, held, got):
+        if held.shape[0] > 4:
+            return got[0]
+        return add_low(self.z_block(held, 0), *got)
+
+    def by_x(self, own, other):
+        return jnp.where(self.x == 1, other, own), jnp.where(self.x == 1, own, other)
 
     def reduce_vector(self, vector):
         mask = 1
@@ -271,38 +316,37 @@
     return lax.optimization_barrier(values)
 
 
-def last(steps):
-    for value in steps:
-        pass
-    return value
-
-
 def row(vector):
     return vector.reshape(1, -1).astype(WIDE)
 
 
-def add_low(first, second):
-    return (first.astype(WIDE) + second.astype(WIDE)).astype(LOW)
+def add_low(first, *others):
+    total = first.astype(WIDE)
+    for other in others:
+        total = total + other.astype(WIDE)
+    return total.astype(LOW)
 
 
 def weight_copies(meta_ref, refs, out_ref, sem, parts, half_width):
     count = out_ref.shape[0]
     at = 0
     copies = []
-    for width, start, by_x, offset in parts:
+    for width, start, by_x, offset, row in parts:
         for place in range(4 if by_x else 2):
             piece = refs[at]
             at += 1
             core = meta_ref[2] ^ (place // 2 if by_x else place)
-            col = pl.multiple_of(core * half_width + offset, LANES)
+            col = core * half_width + offset
+            if by_x:
+                col = col + (meta_ref[1] ^ (place & 1)) * width
+            col = pl.multiple_of(col, LANES)
             rows = piece.shape[1]
-            row = pl.multiple_of((meta_ref[1] ^ (place & 1)) * rows, rows) if by_x else 0
             for j in range(count):
                 copies.append(
                     pltpu.make_async_copy(
                         piece.at[j, :, pl.ds(start, width)],
                         out_ref.at[
-                            meta_ref[0] ^ from_front(j, count), pl.ds(row, rows), pl.ds(col, width)
+                            meta_ref[0] ^ relative(j, count), row : row + rows, pl.ds(col, width)
                         ],
                         sem,
                     )
@@ -370,7 +414,7 @@
     full, out = pl.pallas_call(
         functools.partial(
             project_kernel,
-            parts=[(half_width, 0, True, 0)],
+            parts=[(half_width, 0, False, 0, 0)],
             half_width=half_width,
             pairs=chunk.pairs,
         ),
@@ -416,16 +460,16 @@
     )(*sums, *vectors)
 
 
-def from_front(place, count):
-    bits = count.bit_length() - 1
-    return sum(((place >> b) & 1) << (bits - 1 - b) for b in range(bits))
+def relative(place, count):
+    half = count // 2
+    return (place % half) * 2 + place // half
 
 
 def assemble(wires, shard_rows, half_width, parts):
     count = wires.fsdp_count
     operands, plan = [], []
-    for pieces, width, start, by_x, offset in parts:
-        plan.append((width, start, by_x, offset))
+    for pieces, *where in parts:
+        plan.append(where)
         operands += pieces
     shape = (count, shard_rows, 2 * half_width)
     full = pl.pallas_call(
@@ -499,103 +543,104 @@
             pair_columns(joint_weight, chunk.pairs[c * chunk.count : (c + 1) * chunk.count], model_width)
             for c in range(2)
         )
-        joint_pieces.append(wires.own_rows(wires.own_half(low, high))[0])
-    unit = hidden_units // 4
-    expand_half = wires.own_half(expand_weight[:, : 2 * unit], expand_weight[:, 2 * unit :])
-    close_half = wires.own_half(
-        close_weight[:, : model_width // 2], close_weight[:, model_width // 2 :]
-    )
-    plain_piece = jnp.concatenate([expand_half[:, :unit], close_half], axis=1)
-    split_piece = wires.own_rows(expand_half[:, unit:])[0]
-    shrink_piece = wires.own_half(
-        shrink_weight[:, : model_width // 2], shrink_weight[:, model_width // 2 :]
-    )
-    aligned = shard_rows % 32 == 0
+        joint_pieces.append(wires.own_half(low, high))
+    half_model, half_hidden = model_width // 2, hidden_units // 2
+    unit = half_hidden // 3
+    expand_half = wires.own_half(expand_weight[:, :half_hidden], expand_weight[:, half_hidden:])
+    close_half = wires.own_half(close_weight[:, :half_model], close_weight[:, half_model:])
+    shrink_half = wires.own_half(shrink_weight[:, :half_model], shrink_weight[:, half_model:])
+    aligned = fsdp_count == 8 and shard_rows % 32 == 0
     query_rows = query_bias.astype(WIDE).reshape(-1, LANES)
     value_rows = value_bias.astype(WIDE).reshape(-1, LANES)
-    half_model = model_width // 2
-    behind = ((), (), ())
+
+    def join(*parts):
+        return jnp.concatenate(parts, axis=0)
+
+    def project_and_attend(place, shared, context):
+        full, part = joint_project(
+            wires, flat_input, shared, query_rows, value_rows, chunks[place], shard_rows
+        )
+        return full, part.reshape(row_count, pos_count, -1)
+
     if aligned:
         first, second = joint_pieces[0][None], joint_pieces[1][None]
-        plain, split, shrink = plain_piece[None], split_piece[None], shrink_piece[None]
-        *outer, inner = wires.steps()
-
-        def join(held, got):
-            return jnp.concatenate([held, got], axis=0)
-
-        for mask in outer:
-            got = wires.swap(first, mask)
-            first = join(first, got)
+        mixed_piece = jnp.concatenate([expand_half[:, :unit], close_half], axis=1)[None]
+        split = wires.by_x(expand_half[:, unit : 2 * unit], expand_half[:, 2 * unit :])[0][None]
+        shrink_rows = shrink_half.shape[0] // 2
+        top, bottom = shrink_half[None, :shrink_rows], shrink_half[None, shrink_rows:]
+        first_near = wires.near(first)
+        first = join(first, *first_near)
         first, second = tie(first, second)
-        got = wires.swap(first, inner)
-        second_got = wires.swap(second, outer[0])
-        got, second_got = tie(got, second_got)
-        first, second = join(first, got), join(second, second_got)
-        first_x = wires.swap(first, 2)
-        for mask in outer[1:]:
-            second = join(second, wires.swap(second, mask))
-        first_x, second, plain = tie(first_x, second, plain)
-        second_got = wires.swap(second, inner)
-        for mask in outer:
-            plain = join(plain, wires.swap(plain, mask))
-        second = join(second, second_got)
-        plain, second, split = tie(plain, second, split)
-        second_x = wires.swap(second, 2)
-        plain_got = wires.swap(plain, inner)
-        for mask in outer:
-            split = join(split, wires.swap(split, mask))
-        split, shrink, plain_got = tie(split, shrink, plain_got)
-        plain = join(plain, plain_got)
-        split = join(split, wires.swap(split, inner))
-        second_x, split = tie(second_x, split)
+        first_y = wires.swap(first, 4)
+        second_near = wires.near(second)
+        first = join(first, first_y)
+        first_core = wires.swap(first, 1)
+        first_core, split, second, *second_near = tie(first_core, split, second, *second_near)
+        second = join(second, *second_near)
+        second_y = wires.swap(second, 4)
+        split_near = wires.near(split)
+        full, part = project_and_attend(0, [first, first_core], None)
+        joint_full, mixed = [full], [part]
+        mixed[0], mixed_piece = tie(mixed[0], mixed_piece)
+        piece_near = wires.near(mixed_piece)
+        context, w, inv = attend(mixed[0], segment_ids, chunks[0])
+        weights, inverse = [w], [inv]
+        context, second, second_y, split, *split_near = tie(
+            context, second, second_y, split, *split_near
+        )
+        second = join(second, second_y)
+        second_core = wires.swap(second, 1)
+        split = join(split, *split_near)
+        split_y = wires.swap(split, 4)
+        full, part = project_and_attend(1, [second, second_core], context)
+        joint_full.append(full)
+        part, split, split_y, mixed_piece, top, *piece_near = tie(
+            part, split, split_y, mixed_piece, top, *piece_near
+        )
+        mixed.append(part)
+        split = join(split, split_y)
         split_x = wires.swap(split, 2)
-        for mask in outer:
-            shrink = join(shrink, wires.swap(shrink, mask))
-        split, shrink = tie(split, shrink)
-        shrink = join(shrink, wires.swap(shrink, inner))
-        joint_shared = [wires.share([first, first_x]), wires.share([second, second_x])]
-        split_shared = wires.share([split, split_x])
-        plain_shared = wires.share([plain])
-        shrink_shared = wires.share([shrink])
-    else:
-        joint_shared = [
-            lax.all_gather(
-                pair_columns(joint_weight, c.pairs, model_width), "fsdp", axis=0, tiled=True
-            )
-            for c in chunks
-        ]
-
-    joint_full, mixed, weights, inverse = [], [], [], []
-    context = None
-    for shared, chunk in zip(joint_shared, chunks):
-        full, part = joint_project(
-            wires, flat_input, shared, query_rows, value_rows, chunk, shard_rows
-        )
-        joint_full.append(full)
-        mixed.append(part.reshape(row_count, pos_count, -1))
-        context, w, inv = attend(mixed[-1], segment_ids, chunk, context)
+        mixed_piece = join(mixed_piece, *piece_near)
+        piece_y = wires.swap(mixed_piece, 4)
+        top_near = wires.near(top)
+        context, w, inv = attend(mixed[1], segment_ids, chunks[1], context)
         weights.append(w)
         inverse.append(inv)
-    context_low = context.reshape(tok_count, model_width)
-
-    if aligned:
+        context, split, split_x, mixed_piece, piece_y, top, bottom, *top_near = tie(
+            context, split, split_x, mixed_piece, piece_y, top, bottom, *top_near
+        )
+        plain_shared = wires.share([join(mixed_piece, piece_y)])
+        split_shared = wires.share([split, split_x])
+        top = join(top, *top_near)
+        top_y = wires.swap(top, 4)
+        bottom_near = wires.near(bottom)
         close_full = assemble(
-            wires, shard_rows, half_model, [(plain_shared, half_model, unit, False, 0)]
+            wires, shard_rows, half_model, [(plain_shared, half_model, unit, False, 0, 0)]
         )
         expand_full = assemble(
             wires,
             shard_rows,
-            hidden_units // 2,
-            [(plain_shared, unit, 0, False, 0), (split_shared, unit, 0, True, unit)],
-        )
-        shrink_full = assemble(
-            wires, shrink_weight.shape[0], half_model, [(shrink_shared, half_model, 0, False, 0)]
+            half_hidden,
+            [(plain_shared, unit, 0, False, 0, 0), (split_shared, unit, 0, True, unit, 0)],
         )
     else:
+        joint_full, mixed, weights, inverse = [], [], [], []
+        context = None
+        for place, chunk in enumerate(chunks):
+            shared = lax.all_gather(
+                pair_columns(joint_weight, chunk.pairs, model_width), "fsdp", axis=0, tiled=True
+            )
+            full, part = project_and_attend(place, shared, context)
+            joint_full.append(full)
+            mixed.append(part)
+            context, w, inv = attend(part, segment_ids, chunk, context)
+            weights.append(w)
+            inverse.append(inv)
         close_full, expand_full, shrink_full = (
             lax.all_gather(w, "fsdp", axis=0, tiled=True)
             for w in (close_weight, expand_weight, shrink_weight)
         )
+    context_low = context.reshape(tok_count, model_width)
 
     branch = jnp.dot(context_low, close_full, preferred_element_type=WIDE) + row(close_bias)
     first_sum = flat_input.astype(WIDE) + branch
@@ -604,6 +649,23 @@
     )
     hidden_low = hidden.astype(LOW)
     active_low, slope = expand_gelu(hidden_low, expand_full, row(expand_bias))
+    if aligned:
+        active_low, top, top_y, bottom, *bottom_near = tie(
+            active_low, top, top_y, bottom, *bottom_near
+        )
+        bottom = join(bottom, *bottom_near)
+        bottom_y = wires.swap(bottom, 4)
+        top_shared = wires.share([join(top, top_y)])
+        bottom_shared = wires.share([join(bottom, bottom_y)])
+        shrink_full = assemble(
+            wires,
+            shrink_weight.shape[0],
+            half_model,
+            [
+                (top_shared, half_model, 0, False, 0, 0),
+                (bottom_shared, half_model, 0, False, 0, shrink_rows),
+            ],
+        )
     ffn_out = jnp.dot(active_low, shrink_full, preferred_element_type=WIDE) + row(shrink_bias)
     output, second_pull = jax.vjp(
         layer_norm, hidden + ffn_out, row(second_gain), row(second_shift)
@@ -633,12 +695,11 @@
     shrink_send = outgoing(active_low, grad_ffn)
     grad_ffn, shrink_send = tie(grad_ffn, shrink_send)
     shrink_got = wires.swap(shrink_send, 1)
-    grad_active = jnp.einsum("td,fd->tf", grad_ffn, shrink_full, preferred_element_type=WIDE)
-    grad_inner = (grad_active * slope.astype(WIDE)).astype(LOW)
-    active_low, grad_inner = tie(active_low, grad_inner)
-    shrink_held = staying(active_low, grad_ffn, shrink_got)
-    hidden_low, shrink_held = tie(hidden_low, shrink_held)
-    shrink_steps = wires.halve_steps(shrink_held)
+    grad_inner, inner_sum = inner_grad(grad_ffn, shrink_full, slope)
+    active_low, grad_inner, shrink_got = tie(active_low, grad_inner, shrink_got)
+    shrink_keep, shrink_send = wires.y_halves(staying(active_low, grad_ffn, shrink_got))
+    hidden_low, shrink_keep, shrink_send = tie(hidden_low, shrink_keep, shrink_send)
+    shrink_got = wires.swap(shrink_send, 4)
     expand_send = outgoing(hidden_low, grad_inner)
     grad_inner, expand_send = tie(grad_inner, expand_send)
     expand_got = wires.swap(expand_send, 1)
@@ -647,66 +708,101 @@
     )
     grad_first, first_gain_part, first_shift_part = first_pull(grad_hidden)
     grad_branch = grad_first.astype(LOW)
-    hidden_low, grad_branch = tie(hidden_low, grad_branch)
+    hidden_low, grad_branch, expand_got = tie(hidden_low, grad_branch, expand_got)
     expand_held = staying(hidden_low, grad_inner, expand_got)
-    context_low, expand_held = tie(context_low, expand_held)
+    expand_keep, expand_send = wires.by_x(
+        expand_held[..., : half_hidden // 2], expand_held[..., half_hidden // 2 :]
+    )
+    context_low, expand_keep, expand_send = tie(context_low, expand_keep, expand_send)
+    expand_got = wires.swap(expand_send, 2)
     close_send = outgoing(context_low, grad_branch)
     grad_branch, close_send = tie(grad_branch, close_send)
     close_got = wires.swap(close_send, 1)
     grad_context = jnp.einsum(
         "te,de->td", grad_branch, close_full, preferred_element_type=WIDE
     ).astype(LOW)
-    context_low, grad_context = tie(context_low, grad_context)
+    context_low, grad_context, close_got = tie(context_low, grad_context, close_got)
     close_held = staying(context_low, grad_branch, close_got)
     grad_context = grad_context.reshape(row_count, pos_count, model_width)
-    second_keep, second_send = wires.own_rows(
-        jnp.concatenate([expand_held, close_held], axis=2), axis=1
-    )
-    second_got = wires.swap(second_send, 2)
-
-    shrink_now = next(shrink_steps)
+    grad_context, close_held, shrink_keep, shrink_got = tie(
+        grad_context, close_held, shrink_keep, shrink_got
+    )
+    shrink_held = add_low(shrink_keep, shrink_got)
+    grad_context, shrink_held, *shrink_sends = tie(
+        grad_context, shrink_held, *wires.z_sends(shrink_held)
+    )
+    shrink_got = wires.z_swap(shrink_sends)
+
     grad_mixed, bias_sums = {}, {}
     grad_mixed[1], bias_sums[1] = attend_back(
-        mixed[1],
-        weights[1],
-        context,
-        inverse[1],
-        grad_context,
-        chunks[1],
-        [shrink_now, second_send],
+        mixed[1], weights[1], context, inverse[1], grad_context, chunks[1]
     )
     grad_mixed[1] = grad_mixed[1].reshape(tok_count, -1)
-    send = outgoing(flat_input, grad_mixed[1])
-    flat_input, send = tie(flat_input, send)
-    held = staying(flat_input, grad_mixed[1], wires.swap(send, 1))
-    large_steps = wires.all_steps(held)
-    shrink_now = next(shrink_steps)
+    large_send = outgoing(flat_input, grad_mixed[1])
+    grad_mixed[1], large_send, expand_keep, expand_got = tie(
+        grad_mixed[1], large_send, expand_keep, expand_got
+    )
+    large_got = wires.swap(large_send, 1)
+    second_keep, second_send = wires.y_halves(
+        jnp.concatenate([add_low(expand_keep, expand_got), close_held], axis=2)
+    )
+    flat_input, second_keep, second_send, large_got = tie(
+        flat_input, second_keep, second_send, large_got
+    )
+    second_got = wires.swap(second_send, 4)
+    large_keep, large_send = wires.own_rows(staying(flat_input, grad_mixed[1], large_got), axis=1)
+    grad_context, large_keep, large_send, shrink_held, *shrink_got = tie(
+        grad_context, large_keep, large_send, shrink_held, *shrink_got
+    )
+    large_got = wires.swap(large_send, 2)
+    shrink_mine = wires.z_sum(shrink_held, shrink_got)
     grad_mixed[0], bias_sums[0] = attend_back(
-        mixed[0],
-        weights[0],
-        context,
-        inverse[0],
-        grad_context,
-        chunks[0],
-        [shrink_now, held],
+        mixed[0], weights[0], context, inverse[0], grad_context, chunks[0]
     )
     grad_mixed[0] = grad_mixed[0].reshape(tok_count, -1)
-    send = outgoing(flat_input, grad_mixed[0])
-    flat_input, send = tie(flat_input, send)
-    held = staying(flat_input, grad_mixed[0], wires.swap(send, 1))
-    grad_mixed[0], grad_mixed[1], held = tie(grad_mixed[0], grad_mixed[1], held)
-    small_steps = wires.all_steps(held)
-    second_steps = wires.x_steps(second_keep, second_got)
+    small_send = outgoing(flat_input, grad_mixed[0])
+    grad_mixed[0], small_send, large_keep, large_got, second_keep, second_got = tie(
+        grad_mixed[0], small_send, large_keep, large_got, second_keep, second_got
+    )
+    small_got = wires.swap(small_send, 1)
+    large_keep, large_send = wires.y_halves(add_low(large_keep, large_got))
+    second_held = add_low(second_keep, second_got)
+    flat_input, small_got, large_keep, large_send, second_held, *second_sends = tie(
+        flat_input, small_got, large_keep, large_send, second_held, *wires.z_sends(second_held)
+    )
+    large_got = wires.swap(large_send, 4)
+    second_got = wires.z_swap(second_sends)
+    small_keep, small_send = wires.own_rows(staying(flat_input, grad_mixed[0], small_got), axis=1)
+    grad_mixed[0], grad_mixed[1], small_keep, small_send = tie(
+        grad_mixed[0], grad_mixed[1], small_keep, small_send
+    )
+    small_got = wires.swap(small_send, 2)
     input_grad = (
         grad_first
         + jnp.einsum("te,de->td", grad_mixed[0], joint_full[0], preferred_element_type=WIDE)
         + jnp.einsum("te,de->td", grad_mixed[1], joint_full[1], preferred_element_type=WIDE)
     )
-    for shrink_now in shrink_steps:
-        pass
-    shrink_mine = add_low(shrink_now, wires.swap(shrink_now, 2))
-    second_mine, large_mine, small_mine = (last(v) for v in (second_steps, large_steps, small_steps))
-    joint_mine = (small_mine, large_mine)
+    input_grad, small_keep, small_got, large_keep, large_got = tie(
+        input_grad, small_keep, small_got, large_keep, large_got
+    )
+    small_keep, small_send = wires.y_halves(add_low(small_keep, small_got))
+    small_got = wires.swap(small_send, 4)
+    large_held = add_low(large_keep, large_got)
+    joint_held = jnp.concatenate([add_low(small_keep, small_got), large_held], axis=2)
+    joint_mine = wires.z_sum(joint_held, wires.z_swap(wires.z_sends(joint_held)))
+    second_mine = wires.z_sum(second_held, second_got)
+
+    shrink_mine = add_low(shrink_mine, wires.swap(shrink_mine, 2))
+    second_other = wires.swap(second_mine, 2)
+    quarter = half_hidden // 2
+    second_mine = jnp.concatenate(
+        [
+            *wires.by_x(second_mine[:, :quarter], second_other[:, :quarter]),
+            add_low(second_mine[:, quarter:], second_other[:, quarter:]),
+        ],
+        axis=1,
+    )
+    joint_mine = jnp.concatenate(wires.by_x(joint_mine, wires.swap(joint_mine, 2)), axis=0)
 
     def column_sum(value):
         return jnp.sum(value.astype(WIDE), axis=0, keepdims=True)
@@ -721,7 +817,7 @@
             column_sum(grad_ffn),
             second_gain_part,
             second_shift_part,
-            column_sum(grad_inner),
+            inner_sum,
         ],
         model_width,
     )
@@ -743,8 +839,14 @@
     cut = hidden_units // 2
     expand_grad = jnp.concatenate([low[:, :cut], high[:, :cut]], axis=1).astype(WIDE)
     close_grad = jnp.concatenate([low[:, cut:], high[:, cut:]], axis=1).astype(WIDE)
+    low, high = both_halves(joint_mine)
+    cut = small.count * 3 * LANES
     joint_grad = natural_columns(
-        [jnp.concatenate(both_halves(joint_mine[i]), axis=1) for i in range(2)], chunks
+        [
+            jnp.concatenate([low[:, :cut], high[:, :cut]], axis=1),
+            jnp.concatenate([low[:, cut:], high[:, cut:]], axis=1),
+        ],
+        chunks,
     ).astype(WIDE)
     return (
         layer_output,

time: 454 us -> 382 us (0.84)
  waiting for transfers between devices: 156 us -> 74.2 us
  other arithmetic: 50.3 us -> 27.6 us
  starting transfers between devices: 54.7 us -> 73.1 us
  Pallas kernels: 84.3 us -> 95.9 us
  local copies, waits for them, and re-layouts: 29.7 us -> 39.8 us
  matrix products: 70.7 us -> 64.2 us
    ppermute x57 -> x64, waiting for transfers between devices: 156 us -> 74.2 us  [swap(): return lax.ppermute(value, AXES, [(i, i ^ mask) for i in range(self.total)])]
    ppermute x57 -> x64, starting transfers between devices: 54.7 us -> 73.1 us  [swap(): return lax.ppermute(value, AXES, [(i, i ^ mask) for i in range(self.total)])]
    convert_element_type x11 -> x13, other arithmetic: 19 us -> 6.24 us  [the longest x12 5.27 us: add_low(): return total.astype(LOW)]
    pallas_call x2 -> x3, Pallas kernels: 13.9 us -> 24.9 us  [the longest x2 14 us: joint_project(): pl.pallas_call(functools.partial(project_kernel, parts=[(half_width, 0, F...]
    dot_general x1 -> x0, matrix products: 10.4 us -> none  [body(): jnp.einsum('td,fd->tf', grad_ffn, shrink_full, preferred_element_type=WIDE)]
    unnamed x123 -> x149, local copies, waits for them, and re-layouts: 16.6 us -> 25 us
  transfers between devices with their start and end apart: 57 -> 64, of which waited for: 33 -> 21; matrix products, arithmetic and copies ran while one was open for 22% -> 21% of each run, Pallas kernels for 18% -> 24%
where the time goes in v3:
time: 382 us; the launch traced here: 377 us
  Pallas kernels  95.9 us (25%)
  waiting for transfers between devices  74.2 us (19%)
  starting transfers between devices  73.1 us (19%)
  matrix products  64.2 us (17%)
  local copies, waits for them, and re-layouts  39.8 us (10%)
  other arithmetic  27.6 us (7%)
    ppermute x64, waiting for transfers between devices, swap(): return lax.ppermute(value, AXES, [(i, i ^ mask) for i in range(self.total)])  74.2 us
    ppermute x64, starting transfers between devices, swap(): return lax.ppermute(value, AXES, [(i, i ^ mask) for i in range(self.total)])  73.1 us
    unnamed x149, local copies, waits for them, and re-layouts  25 us
    pallas_call x2, Pallas kernels, attend_back(): pl.pallas_call(attend_back_kernel, grid=(rows, count), in_specs=[pl.Block...  22.6 us
    pallas_call x2, Pallas kernels, attend(): pl.pallas_call(attend_kernel, grid=(rows, count), in_specs=in_specs, out_...  21.2 us
    dot_general x5, matrix products, staying(): keep = jnp.einsum('tf,td->fd', left, keep, preferred_element_type=WIDE)  18.6 us
    dot_general x5, matrix products, outgoing(): jnp.einsum('tf,td->fd', left, send, preferred_element_type=WIDE).astype(LOW)  16.4 us
    pallas_call x2, Pallas kernels, joint_project(): pl.pallas_call(functools.partial(project_kernel, parts=[(half_width, 0, F...  14 us
  transfers between devices with their start and end apart: 64, of which 21 were waited for; matrix products, arithmetic and copies ran while one was open for 21% of the time, Pallas kernels for 24%

profile of v3, /device:TPU:0, one launch (start us, length us, event | category | flops | bytes accessed | tf_op | source)
XLA Modules:
  0.0 377.1 jit_solution(10371051143755528264)
XLA Ops:
  15.3 5.4 %collective-permute-done.3 = bf16[4,96,384]{2,1,0:T(8,128)(2,1)S(1)} collective-permute-done((bf16[4,96,384]{2,1,0:T(8,128)(2,1)S(1)}, bf16[4,96,384]{2,1,0:T(8,128)(2,1)S(1)}, u32[]{:S(2)}, u32[]{:S(2)}) %collective-permute-start.3) | collective-permute-done | bytes 294944 | tf_op jit(solution)/shard_map/ppermute | solution.py:253
  25.4 4.8 %collective-permute-done.5 = bf16[1,96,768]{2,1,0:T(8,128)(2,1)S(1)} collective-permute-done((bf16[1,96,768]{2,1,0:T(8,128)(2,1)S(1)}, bf16[1,96,768]{2,1,0:T(8,128)(2,1)S(1)}, u32[]{:S(2)}, u32[]{:S(2)}) %collective-permute-start.5) | collective-permute-done | bytes 147488 | tf_op jit(solution)/shard_map/ppermute | solution.py:253
  30.2 6.0 %collective-permute-done.6 = bf16[1,96,768]{2,1,0:T(8,128)(2,1)S(1)} collective-permute-done((bf16[1,96,768]{2,1,0:T(8,128)(2,1)S(1)}, bf16[1,96,768]{2,1,0:T(8,128)(2,1)S(1)}, u32[]{:S(2)}, u32[]{:S(2)}) %collective-permute-start.6) | collective-permute-done | bytes 147488 | tf_op jit(solution)/shard_map/ppermute | solution.py:253
  40.7 4.4 %collective-permute-start.10 = (bf16[1,96,512]{2,1,0:T(8,128)(2,1)S(1)}, bf16[1,96,512]{2,1,0:T(8,128)(2,1)S(1)}, u32[]{:S(2)}, u32[]{:S(2)}) collective-permute-start(bf16[1,96,512]{2,1,0:T(8,128)(2,1)S(1)} %get-tuple-element.157), channel_id=1, source_target_pairs={{0,16},{1,17},{2,18},{3,19},{4,20},{5,21},{6,22},{7,23},{8,24},{9,... | collective-permute-start | bytes 294920 | tf_op jit(solution)/shard_map/ppermute | solution.py:253
  46.0 5.7 %joint_project.2 = (bf16[8,96,768]{2,1,0:T(8,128)(2,1)}, bf16[1024,768]{1,0:T(8,128)(2,1)}) custom-call(s32[3]{0:T(128)} %pad_add_fusion.meta_ref, bf16[1024,768]{1,0:T(8,128)(2,1)} %bitcast.231, f32[6,128]{1,0:T(8,128)} %get-tuple-element.344.query_ref, f32[6,128]{1,0:T(8,128)} %get-tuple-element.343.value_ref, bf16[8,96,384]{2,1,0:T(8,128)(2,1)} %copy-done.22, ...), custom_call_target="tpu_custom_call" | custom-call | flops 1207959552 | bytes 5111808 | tf_op jit(solution)/shard_map/joint_project/pallas_call | solution.py:414
  51.7 7.8 %attend.2 = (bf16[2,512,768]{2,1,0:T(8,128)(2,1)}, bf16[2,2,2,512,512]{4,3,2,1,0:T(8,128)(2,1)}, f32[2,512,256]{2,1,0:T(8,128)}) custom-call(bf16[2,512,768]{2,1,0:T(8,128)(2,1)} %bitcast.245, s32[2,512,1]{2,1,0:T(8,128)} %copy.33.seg_col_ref, s32[2,1,512]{2,1,0:T(1,128)} %broadcast_in_dim.47.seg_row_ref), custom_call_target="tpu_custom_call" | custom-call | flops 2147483648 | bytes 8388608 | tf_op jit(solution)/shard_map/attend/pallas_call | solution.py:108
  66.4 8.2 %joint_project.3 = (bf16[8,96,1536]{2,1,0:T(8,128)(2,1)}, bf16[1024,1536]{1,0:T(8,128)(2,1)}) custom-call(s32[3]{0:T(128)} %pad_add_fusion.meta_ref, bf16[1024,768]{1,0:T(8,128)(2,1)} %bitcast.232, f32[6,128]{1,0:T(8,128)} %get-tuple-element.344.query_ref, f32[6,128]{1,0:T(8,128)} %get-tuple-element.343.value_ref, bf16[8,96,768]{2,1,0:T(8,128)(2,1)} %copy-done.21, ...), custom_call_target="tpu_custom_call" | custom-call | flops 2415919104 | bytes 10223616 | tf_op jit(solution)/shard_map/joint_project/pallas_call | solution.py:414
  74.6 4.3 %collective-permute-done.15 = bf16[1,96,896]{2,1,0:T(8,128)(2,1)S(1)} collective-permute-done((bf16[1,96,896]{2,1,0:T(8,128)(2,1)S(1)}, bf16[1,96,896]{2,1,0:T(8,128)(2,1)S(1)}, u32[]{:S(2)}, u32[]{:S(2)}) %collective-permute-start.15) | collective-permute-done | bytes 172064 | tf_op jit(solution)/shard_map/ppermute | solution.py:253
  89.0 13.4 %attend.3 = (bf16[2,512,768]{2,1,0:T(8,128)(2,1)}, bf16[2,4,2,512,512]{4,3,2,1,0:T(8,128)(2,1)}, f32[2,512,512]{2,1,0:T(8,128)}) custom-call(bf16[2,512,1536]{2,1,0:T(8,128)(2,1)} %bitcast.238, s32[2,512,1]{2,1,0:T(8,128)} %copy.33.seg_col_ref, s32[2,1,512]{2,1,0:T(1,128)} %broadcast_in_dim.47.seg_row_ref, ...), custom_call_target="tpu_custom_call", output_to_operand_aliasing={{0}: (3, {})} | custom-call | flops 4294967296 | bytes 16777216 | tf_op jit(solution)/shard_map/attend/pallas_call | solution.py:108
  117.0 3.8 fusion.75
  123.5 5.2 %assemble.4 = bf16[8,96,3072]{2,1,0:T(8,128)(2,1)} custom-call(s32[3]{0:T(128)} %pad_add_fusion.meta_ref, bf16[8,96,896]{2,1,0:T(8,128)(2,1)} %copy-done.5, bf16[8,96,896]{2,1,0:T(8,128)(2,1)} %copy-done.8, bf16[8,96,512]{2,1,0:T(8,128)(2,1)} %constant_dynamic-update-slice_fusion.24.refs_2_, bf16[8,96,512]{2,1,0:T(8,128)(2,1)} %copy-done.16, ...), custom_call_target="tpu_custom_call" | custom-call | bytes 9437184 | tf_op jit(solution)/shard_map/assemble/pallas_call | solution.py:475
  128.7 12.1 %expand_gelu.1 = (bf16[1024,3072]{1,0:T(8,128)(2,1)}, bf16[1024,3072]{1,0:T(8,128)(2,1)}) custom-call(bf16[1024,768]{1,0:T(8,128)(2,1)} %fusion.12.hidden_ref, bf16[768,3072]{1,0:T(8,128)(2,1)} %bitcast.214, f32[1,3072]{1,0:T(1,128)} %bitcast.230), custom_call_target="tpu_custom_call" | custom-call | flops 7247757312 | bytes 17301504 | tf_op jit(solution)/shard_map/expand_gelu/pallas_call | solution.py:182
  148.8 8.7 %collective-permute-done.30 = bf16[4,192,384]{2,1,0:T(8,128)(2,1)S(1)} collective-permute-done((bf16[4,192,384]{2,1,0:T(8,128)(2,1)S(1)}, bf16[4,192,384]{2,1,0:T(8,128)(2,1)S(1)}, u32[]{:S(2)}, u32[]{:S(2)}) %collective-permute-start.30) | collective-permute-done | bytes 589856 | tf_op jit(solution)/shard_map/ppermute | solution.py:253
  160.6 5.3 %assemble.5 = bf16[8,384,768]{2,1,0:T(8,128)(2,1)} custom-call(s32[3]{0:T(128)} %pad_add_fusion.meta_ref, bf16[8,192,384]{2,1,0:T(8,128)(2,1)} %copy-done.9, bf16[8,192,384]{2,1,0:T(8,128)(2,1)} %copy-done.13, bf16[8,192,384]{2,1,0:T(8,128)(2,1)} %copy-done.12, bf16[8,192,384]{2,1,0:T(8,128)(2,1)} %collective-permute-done.31.refs_3_), custom_call_target="tpu_custom_call" | custom-call | bytes 9437184 | tf_op jit(solution)/shard_map/assemble/pallas_call | solution.py:475
  166.0 8.8 %fusion.76 = (f32[1024]{0:T(1024)S(1)}, f32[1024,768]{1,0:T(8,128)S(1)}) fusion(f32[768]{0:T(1024)S(1)} %convert_element_type.269, bf16[1024,3072]{1,0:T(8,128)(2,1)} %get-tuple-element.195, bf16[3072,768]{1,0:T(8,128)(2,1)} %bitcast.218, f32[768]{0:T(1024)S(1)} %convert_element_type.265, f32[768]{0:T(1024)S(1)} %convert_element_type.264, ...), kind=kOutput, calls=%fused_computation.262 | convolution fusion | flops 4837342208 | bytes 17323008 | tf_op jit(solution)/shard_map/dot_general | solution.py:669
  182.0 4.8 %convolution_convert_fusion = bf16[3072,384]{1,0:T(8,128)(2,1)} fusion(bf16[1024,3072]{1,0:T(8,128)(2,1)S(1)} %bitcast.257, bf16[1024,768]{1,0:T(8,128)(2,1)S(1)} %add_convert_fusion.4.grad_ref, pred[]{:T(512)S(6)} %eq.4), kind=kOutput, calls=%fused_computation.4 | convolution fusion | flops 2417491968 | bytes 10223617 | tf_op jit(solution)/shard_map/tf,td->fd/dot_general | solution.py:682
  189.3 11.0 %inner_grad.1 = (bf16[1024,3072]{1,0:T(8,128)(2,1)}, f32[1,3072]{1,0:T(1,128)}) custom-call(bf16[1024,768]{1,0:T(8,128)(2,1)} %copy-done.6, bf16[3072,768]{1,0:T(8,128)(2,1)} %bitcast.219, bf16[1024,3072]{1,0:T(8,128)(2,1)} %get-tuple-element.191.slope_ref), custom_call_target="tpu_custom_call" | custom-call | flops 4831838208 | bytes 17301504 | tf_op jit(solution)/shard_map/inner_grad/pallas_call | solution.py:217
  200.2 7.5 %add_convert_fusion.1 = bf16[3072,384]{1,0:T(8,128)(2,1)S(1)} fusion(bf16[3072,384]{1,0:T(8,128)(2,1)} %collective-permute-done.32, bf16[1024,3072]{1,0:T(8,128)(2,1)} %get-tuple-element.195, bf16[1024,768]{1,0:T(8,128)(2,1)} %copy-done.6, pred[]{:T(512)S(6)} %eq.4), kind=kOutput, calls=%fused_computation.3 | convolution fusion | flops 2419851264 | bytes 12582913 | tf_op jit(solution)/shard_map/tf,td->fd/dot_general | solution.py:687
  211.6 8.3 %multiply_reduce_fusion = (f32[768]{0:T(1024)S(1)}, f32[1024]{0:T(1024)S(1)}, f32[768]{0:T(1024)S(1)}, f32[1024,768]{1,0:T(8,128)S(1)}) fusion(f32[1024,768]{1,0:T(8,128)S(1)} %get-tuple-element.339, f32[1024]{0:T(1024)S(1)} %fusion.70, f32[1024]{0:T(1024)S(1)} %broadcast_multiply_fusion.1, f32[768]{0:T(1024)S(1)} %convert_element_type.264, ...), kind=kOutput, calls=%fused_computation.14 | convolution fusion | flops 4839699456 | bytes 20472832 | tf_op jit(solution)/shard_map/tf,df->td/dot_general | solution.py:706
  224.8 5.6 %add_convert_fusion = bf16[768,1536]{1,0:T(8,128)(2,1)S(1)} fusion(bf16[768,1536]{1,0:T(8,128)(2,1)S(1)} %collective-permute-done.33, bf16[1024,768]{1,0:T(8,128)(2,1)S(1)} %copy-done.11, bf16[1024,3072]{1,0:T(8,128)(2,1)} %get-tuple-element.198, pred[]{:T(512)S(6)} %eq.4), kind=kOutput, calls=%fused_computation.2 | convolution fusion | flops 2421030912 | bytes 12582913 | tf_op jit(solution)/shard_map/tf,td->fd/dot_general | solution.py:687
  241.6 6.3 %collective-permute-done.35 = bf16[4,384,384]{2,1,0:T(8,128)(2,1)S(1)} collective-permute-done((bf16[4,384,384]{2,1,0:T(8,128)(2,1)S(1)}, bf16[4,384,384]{2,1,0:T(8,128)(2,1)S(1)}, u32[]{:S(2)}, u32[]{:S(2)}) %collective-permute-start.35) | collective-permute-done | bytes 1179680 | tf_op jit(solution)/shard_map/ppermute | solution.py:253
  253.6 14.3 %attend_back.2 = (bf16[2,512,1536]{2,1,0:T(8,128)(2,1)}, f32[2,4,8,384]{3,2,1,0:T(8,128)}) custom-call(bf16[2,512,1536]{2,1,0:T(8,128)(2,1)} %bitcast.239, bf16[2,4,2,512,512]{4,3,2,1,0:T(8,128)(2,1)} %get-tuple-element.217.weights_ref, bf16[2,512,768]{2,1,0:T(8,128)(2,1)} %get-tuple-element.172.context_ref, f32[2,512,512]{2,1,0:T(8,128)} %get-tuple-element.218.inverse_ref, ...), custom_call_target="tpu_custom_call" | custom-call | flops 8589934592 | bytes 16777216 | tf_op jit(solution)/shard_map/attend_back/pallas_call | solution.py:138
  267.9 3.9 %fusion.24 = bf16[768,768]{0,1:T(8,128)(2,1)S(1)} fusion(bf16[1024,768]{1,0:T(8,128)(2,1)} %bitcast.234, bf16[1024,1536]{1,0:T(8,128)(2,1)} %bitcast.240, pred[]{:T(512)S(6)} %eq.4), kind=kOutput, calls=%fused_computation.53 | convolution fusion | flops 1209335808 | bytes 5898241 | tf_op jit(solution)/shard_map/tf,td->fd/dot_general | solution.py:682
  283.6 8.3 %attend_back.3 = (bf16[2,512,768]{2,1,0:T(8,128)(2,1)}, f32[2,2,8,384]{3,2,1,0:T(8,128)}) custom-call(bf16[2,512,768]{2,1,0:T(8,128)(2,1)} %bitcast.246, bf16[2,2,2,512,512]{4,3,2,1,0:T(8,128)(2,1)} %get-tuple-element.199.weights_ref, bf16[2,512,768]{2,1,0:T(8,128)(2,1)} %get-tuple-element.172.context_ref, f32[2,512,256]{2,1,0:T(8,128)} %get-tuple-element.200.inverse_ref, ...), custom_call_target="tpu_custom_call" | custom-call | flops 4294967296 | bytes 8388608 | tf_op jit(solution)/shard_map/attend_back/pallas_call | solution.py:138
  310.2 3.7 convolution_convert_fusion.3
  317.5 7.2 %collective-permute-done.42 = bf16[4,96,1152]{2,1,0:T(8,128)(2,1)S(1)} collective-permute-done((bf16[4,96,1152]{2,1,0:T(8,128)(2,1)S(1)}, bf16[4,96,1152]{2,1,0:T(8,128)(2,1)S(1)}, u32[]{:S(2)}, u32[]{:S(2)}) %collective-permute-start.42) | collective-permute-done | bytes 884768 | tf_op jit(solution)/shard_map/ppermute | solution.py:253
  337.9 4.3 %add_add_fusion.2 = f32[1024,768]{1,0:T(8,128)} fusion(f32[1024,768]{1,0:T(8,128)S(1)} %fusion.77, f32[1024,768]{1,0:T(8,128)S(1)} %copy-done.2, bf16[1024,1536]{1,0:T(8,128)(2,1)S(1)} %bitcast.242, bf16[768,1536]{1,0:T(8,128)(2,1)S(1)} %bitcast.244, f32[1024]{0:T(1024)S(1)} %negate_multiply_fusion), kind=kOutput, calls=%fused_computation.16 | convolution fusion | flops 2418278400 | bytes 14946304 | tf_op jit(solution)/shard_map/te,de->td/dot_general | solution.py:783
  342.3 4.9 %collective-permute-done.58 = bf16[96,1152]{1,0:T(8,128)(2,1)S(1)} collective-permute-done((bf16[96,1152]{1,0:T(8,128)(2,1)S(1)}, bf16[96,1152]{1,0:T(8,128)(2,1)S(1)}, u32[]{:S(2)}, u32[]{:S(2)}) %collective-permute-start.58) | collective-permute-done | bytes 221216 | tf_op jit(solution)/shard_map/ppermute | solution.py:253
  349.7 3.6 collective-permute-done.60
  353.4 5.1 %collective-permute-start.47 = (bf16[48,1152]{1,0:T(8,128)(2,1)S(1)}, bf16[48,1152]{1,0:T(8,128)(2,1)S(1)}, u32[]{:S(2)}, u32[]{:S(2)}) collective-permute-start(bf16[48,1152]{1,0:T(8,128)(2,1)S(1)} %get-tuple-element.311), channel_id=1, source_target_pairs={{0,8},{1,9},{2,10},{3,11},{4,12},{5,13},{6,14},{7,15},{8,0},{9,1},... | collective-permute-start | bytes 331784 | tf_op jit(solution)/shard_map/ppermute | solution.py:253
  362.3 6.1 %collective-permute-done.48 = bf16[48,1152]{1,0:T(8,128)(2,1)S(1)} collective-permute-done((bf16[48,1152]{1,0:T(8,128)(2,1)S(1)}, bf16[48,1152]{1,0:T(8,128)(2,1)S(1)}, u32[]{:S(2)}, u32[]{:S(2)}) %collective-permute-start.48) | collective-permute-done | bytes 110624 | tf_op jit(solution)/shard_map/ppermute | solution.py:253
  369.2 4.1 %collective-permute-done.50 = bf16[48,1152]{1,0:T(8,128)(2,1)S(1)} collective-permute-done((bf16[48,1152]{1,0:T(8,128)(2,1)S(1)}, bf16[48,1152]{1,0:T(8,128)(2,1)S(1)}, u32[]{:S(2)}, u32[]{:S(2)}) %collective-permute-start.50) | collective-permute-done | bytes 110624 | tf_op jit(solution)/shard_map/ppermute | solution.py:253
  (383 shorter events, 161.7 us)
Async XLA Ops:
  20.7 15.5 %collective-permute-start.4 = (bf16[8,96,384]{2,1,0:T(8,128)(2,1)S(1)}, bf16[8,96,384]{2,1,0:T(8,128)(2,1)S(1)}, u32[]{:S(2)}, u32[]{:S(2)}) collective-permute-start(bf16[8,96,384]{2,1,0:T(8,128)(2,1)S(1)} %constant_dynamic-update-slice_fusion.12.refs_0_), channel_id=1, source_target_pairs={{0,1},{1,0},{2,3},{3,2},{4,5},{5,4},{6,7},{7,6},{8,9},{9,8},{10,11... | collective-permute-start | bytes 1769480 | tf_op jit(solution)/shard_map/ppermute | solution.py:253
  22.2 14.0 %collective-permute-start.6 = (bf16[1,96,768]{2,1,0:T(8,128)(2,1)S(1)}, bf16[1,96,768]{2,1,0:T(8,128)(2,1)S(1)}, u32[]{:S(2)}, u32[]{:S(2)}) collective-permute-start(bf16[1,96,768]{2,1,0:T(8,128)(2,1)S(1)} %broadcast_select_fusion.14), channel_id=1, source_target_pairs={{0,16},{1,17},{2,18},{3,19},{4,20},{5,21},{6,22},{7,23},{8,24},{9,... | collective-permute-start | bytes 442376 | tf_op jit(solution)/shard_map/ppermute | solution.py:253
  36.3 23.3 %collective-permute-start.8 = (bf16[4,96,768]{2,1,0:T(8,128)(2,1)S(1)}, bf16[4,96,768]{2,1,0:T(8,128)(2,1)S(1)}, u32[]{:S(2)}, u32[]{:S(2)}) collective-permute-start(bf16[4,96,768]{2,1,0:T(8,128)(2,1)S(1)} %constant_dynamic-update-slice_fusion.14), channel_id=1, source_target_pairs={{0,4},{1,5},{2,6},{3,7},{4,0},{5,1},{6,2},{7,3},{8,12},{9,13},{10,... | collective-permute-start | bytes 1769480 | tf_op jit(solution)/shard_map/ppermute | solution.py:253
  40.7 18.9 %collective-permute-start.10 = (bf16[1,96,512]{2,1,0:T(8,128)(2,1)S(1)}, bf16[1,96,512]{2,1,0:T(8,128)(2,1)S(1)}, u32[]{:S(2)}, u32[]{:S(2)}) collective-permute-start(bf16[1,96,512]{2,1,0:T(8,128)(2,1)S(1)} %get-tuple-element.157), channel_id=1, source_target_pairs={{0,16},{1,17},{2,18},{3,19},{4,20},{5,21},{6,22},{7,23},{8,24},{9,... | collective-permute-start | bytes 294920 | tf_op jit(solution)/shard_map/ppermute | solution.py:253
  45.1 14.4 %collective-permute-start.11 = (bf16[1,96,512]{2,1,0:T(8,128)(2,1)S(1)}, bf16[1,96,512]{2,1,0:T(8,128)(2,1)S(1)}, u32[]{:S(2)}, u32[]{:S(2)}) collective-permute-start(bf16[1,96,512]{2,1,0:T(8,128)(2,1)S(1)} %get-tuple-element.157), channel_id=1, source_target_pairs={{0,24},{1,25},{2,26},{3,27},{4,28},{5,29},{6,30},{7,31},{8,16},{9,... | collective-permute-start | bytes 294920 | tf_op jit(solution)/shard_map/ppermute | solution.py:253
  46.0 13.6 %collective-permute-start.9 = (bf16[1,96,512]{2,1,0:T(8,128)(2,1)S(1)}, bf16[1,96,512]{2,1,0:T(8,128)(2,1)S(1)}, u32[]{:S(2)}, u32[]{:S(2)}) collective-permute-start(bf16[1,96,512]{2,1,0:T(8,128)(2,1)S(1)} %get-tuple-element.157), channel_id=1, source_target_pairs={{0,8},{1,9},{2,10},{3,11},{4,12},{5,13},{6,14},{7,15},{8,0},{9,1},... | collective-permute-start | bytes 294920 | tf_op jit(solution)/shard_map/ppermute | solution.py:253
  60.7 18.2 %collective-permute-start.13 = (bf16[4,96,512]{2,1,0:T(8,128)(2,1)S(1)}, bf16[4,96,512]{2,1,0:T(8,128)(2,1)S(1)}, u32[]{:S(2)}, u32[]{:S(2)}) collective-permute-start(bf16[4,96,512]{2,1,0:T(8,128)(2,1)S(1)} %constant_dynamic-update-slice_fusion.20), channel_id=1, source_target_pairs={{0,4},{1,5},{2,6},{3,7},{4,0},{5,1},{6,2},{7,3},{8,12},{9,13},{10,... | collective-permute-start | bytes 1179656 | tf_op jit(solution)/shard_map/ppermute | solution.py:253
  63.4 15.5 %collective-permute-start.15 = (bf16[1,96,896]{2,1,0:T(8,128)(2,1)S(1)}, bf16[1,96,896]{2,1,0:T(8,128)(2,1)S(1)}, u32[]{:S(2)}, u32[]{:S(2)}) collective-permute-start(bf16[1,96,896]{2,1,0:T(8,128)(2,1)S(1)} %maximum_bitcast_fusion), channel_id=1, source_target_pairs={{0,16},{1,17},{2,18},{3,19},{4,20},{5,21},{6,22},{7,23},{8,24},{9,... | collective-permute-start | bytes 516104 | tf_op jit(solution)/shard_map/ppermute | solution.py:253
  65.0 13.9 %collective-permute-start.16 = (bf16[1,96,896]{2,1,0:T(8,128)(2,1)S(1)}, bf16[1,96,896]{2,1,0:T(8,128)(2,1)S(1)}, u32[]{:S(2)}, u32[]{:S(2)}) collective-permute-start(bf16[1,96,896]{2,1,0:T(8,128)(2,1)S(1)} %maximum_bitcast_fusion), channel_id=1, source_target_pairs={{0,24},{1,25},{2,26},{3,27},{4,28},{5,29},{6,30},{7,31},{8,16},{9,... | collective-permute-start | bytes 516104 | tf_op jit(solution)/shard_map/ppermute | solution.py:253
  80.5 21.9 %collective-permute-start.17 = (bf16[8,96,512]{2,1,0:T(8,128)(2,1)}, bf16[8,96,512]{2,1,0:T(8,128)(2,1)S(1)}, u32[]{:S(2)}, u32[]{:S(2)}) collective-permute-start(bf16[8,96,512]{2,1,0:T(8,128)(2,1)} %constant_dynamic-update-slice_fusion.24.refs_2_), channel_id=1, source_target_pairs={{0,2},{1,3},{2,0},{3,1},{4,6},{5,7},{6,4},{7,5},{8,10},{9,11},{10,... | collective-permute-start | bytes 2359304 | tf_op jit(solution)/shard_map/ppermute | solution.py:253
  82.1 20.4 %collective-permute-start.18 = (bf16[4,96,896]{2,1,0:T(8,128)(2,1)S(1)}, bf16[4,96,896]{2,1,0:T(8,128)(2,1)S(1)}, u32[]{:S(2)}, u32[]{:S(2)}) collective-permute-start(bf16[4,96,896]{2,1,0:T(8,128)(2,1)S(1)} %constant_dynamic-update-slice_fusion.26), channel_id=1, source_target_pairs={{0,4},{1,5},{2,6},{3,7},{4,0},{5,1},{6,2},{7,3},{8,12},{9,13},{10,... | collective-permute-start | bytes 2064392 | tf_op jit(solution)/shard_map/ppermute | solution.py:253
  83.7 18.7 %collective-permute-start.19 = (bf16[1,192,384]{2,1,0:T(8,128)(2,1)S(1)}, bf16[1,192,384]{2,1,0:T(8,128)(2,1)S(1)}, u32[]{:S(2)}, u32[]{:S(2)}) collective-permute-start(bf16[1,192,384]{2,1,0:T(8,128)(2,1)S(1)} %get-tuple-element.178), channel_id=1, source_target_pairs={{0,8},{1,9},{2,10},{3,11},{4,12},{5,13},{6,14},{7,15},{8,0},{9,1},... | collective-permute-start | bytes 442376 | tf_op jit(solution)/shard_map/ppermute | solution.py:253
  86.1 16.3 %collective-permute-start.20 = (bf16[1,192,384]{2,1,0:T(8,128)(2,1)S(1)}, bf16[1,192,384]{2,1,0:T(8,128)(2,1)S(1)}, u32[]{:S(2)}, u32[]{:S(2)}) collective-permute-start(bf16[1,192,384]{2,1,0:T(8,128)(2,1)S(1)} %get-tuple-element.178), channel_id=1, source_target_pairs={{0,16},{1,17},{2,18},{3,19},{4,20},{5,21},{6,22},{7,23},{8,24},{9,... | collective-permute-start | bytes 442376 | tf_op jit(solution)/shard_map/ppermute | solution.py:253
  87.5 14.9 %collective-permute-start.21 = (bf16[1,192,384]{2,1,0:T(8,128)(2,1)S(1)}, bf16[1,192,384]{2,1,0:T(8,128)(2,1)S(1)}, u32[]{:S(2)}, u32[]{:S(2)}) collective-permute-start(bf16[1,192,384]{2,1,0:T(8,128)(2,1)S(1)} %get-tuple-element.178), channel_id=1, source_target_pairs={{0,24},{1,25},{2,26},{3,27},{4,28},{5,29},{6,30},{7,31},{8,16},{9,... | collective-permute-start | bytes 442376 | tf_op jit(solution)/shard_map/ppermute | solution.py:253
  105.7 35.1 %collective-permute-start.26 = (bf16[1,192,384]{2,1,0:T(8,128)(2,1)S(1)}, bf16[1,192,384]{2,1,0:T(8,128)(2,1)S(1)}, u32[]{:S(2)}, u32[]{:S(2)}) collective-permute-start(bf16[1,192,384]{2,1,0:T(8,128)(2,1)S(1)} %get-tuple-element.186), channel_id=1, source_target_pairs={{0,8},{1,9},{2,10},{3,11},{4,12},{5,13},{6,14},{7,15},{8,0},{9,1},... | collective-permute-start | bytes 442376 | tf_op jit(solution)/shard_map/ppermute | solution.py:253
  106.3 34.5 %collective-permute-start.27 = (bf16[1,192,384]{2,1,0:T(8,128)(2,1)S(1)}, bf16[1,192,384]{2,1,0:T(8,128)(2,1)}, u32[]{:S(2)}, u32[]{:S(2)}) collective-permute-start(bf16[1,192,384]{2,1,0:T(8,128)(2,1)S(1)} %get-tuple-element.186), channel_id=1, source_target_pairs={{0,16},{1,17},{2,18},{3,19},{4,20},{5,21},{6,22},{7,23},{8,24},{9,... | collective-permute-start | bytes 442376 | tf_op jit(solution)/shard_map/ppermute | solution.py:253
  108.7 32.2 %collective-permute-start.28 = (bf16[1,192,384]{2,1,0:T(8,128)(2,1)S(1)}, bf16[1,192,384]{2,1,0:T(8,128)(2,1)}, u32[]{:S(2)}, u32[]{:S(2)}) collective-permute-start(bf16[1,192,384]{2,1,0:T(8,128)(2,1)S(1)} %get-tuple-element.186), channel_id=1, source_target_pairs={{0,24},{1,25},{2,26},{3,27},{4,28},{5,29},{6,30},{7,31},{8,16},{9,... | collective-permute-start | bytes 442376 | tf_op jit(solution)/shard_map/ppermute | solution.py:253
  123.0 17.8 %collective-permute-start.25 = (bf16[4,192,384]{2,1,0:T(8,128)(2,1)}, bf16[4,192,384]{2,1,0:T(8,128)(2,1)}, u32[]{:S(2)}, u32[]{:S(2)}) collective-permute-start(bf16[4,192,384]{2,1,0:T(8,128)(2,1)} %constant_dynamic-update-slice_fusion.32), channel_id=1, source_target_pairs={{0,4},{1,5},{2,6},{3,7},{4,0},{5,1},{6,2},{7,3},{8,12},{9,13},{10,... | collective-permute-start | bytes 1769480 | tf_op jit(solution)/shard_map/ppermute | solution.py:253
  142.0 15.5 %collective-permute-start.30 = (bf16[4,192,384]{2,1,0:T(8,128)(2,1)S(1)}, bf16[4,192,384]{2,1,0:T(8,128)(2,1)S(1)}, u32[]{:S(2)}, u32[]{:S(2)}) collective-permute-start(bf16[4,192,384]{2,1,0:T(8,128)(2,1)S(1)} %pad_maximum_fusion.1), channel_id=1, source_target_pairs={{0,4},{1,5},{2,6},{3,7},{4,0},{5,1},{6,2},{7,3},{8,12},{9,13},{10,... | collective-permute-start | bytes 1769480 | tf_op jit(solution)/shard_map/ppermute | solution.py:253
  211.1 13.7 %collective-permute-start.33 = (bf16[768,1536]{1,0:T(8,128)(2,1)S(1)}, bf16[768,1536]{1,0:T(8,128)(2,1)S(1)}, u32[]{:S(2)}, u32[]{:S(2)}) collective-permute-start(bf16[768,1536]{1,0:T(8,128)(2,1)S(1)} %convolution_convert_fusion.1), channel_id=1, source_target_pairs={{0,1},{1,0},{2,3},{3,2},{4,5},{5,4},{6,7},{7,6},{8,9},{9,8},{10,11... | collective-permute-start | bytes 7077896 | tf_op jit(solution)/shard_map/ppermute | solution.py:253
  219.9 28.1 %collective-permute-start.35 = (bf16[4,384,384]{2,1,0:T(8,128)(2,1)S(1)}, bf16[4,384,384]{2,1,0:T(8,128)(2,1)S(1)}, u32[]{:S(2)}, u32[]{:S(2)}) collective-permute-start(bf16[4,384,384]{2,1,0:T(8,128)(2,1)S(1)} %get-tuple-element.212), channel_id=1, source_target_pairs={{0,4},{1,5},{2,6},{3,7},{4,0},{5,1},{6,2},{7,3},{8,12},{9,13},{10,... | collective-permute-start | bytes 3538952 | tf_op jit(solution)/shard_map/ppermute | solution.py:253
  235.8 36.0 %collective-permute-start.36 = (bf16[8,96,768]{2,1,0:T(8,128)(2,1)S(1)}, bf16[8,96,768]{2,1,0:T(8,128)(2,1)}, u32[]{:S(2)}, u32[]{:S(2)}) collective-permute-start(bf16[8,96,768]{2,1,0:T(8,128)(2,1)S(1)} %get-tuple-element.221), channel_id=1, source_target_pairs={{0,2},{1,3},{2,0},{3,1},{4,6},{5,7},{6,4},{7,5},{8,10},{9,11},{10,... | collective-permute-start | bytes 3538952 | tf_op jit(solution)/shard_map/ppermute | solution.py:253
  249.2 32.5 %collective-permute-start.38 = (bf16[384,384]{1,0:T(8,128)(2,1)}, bf16[384,384]{1,0:T(8,128)(2,1)}, u32[]{:S(2)}, u32[]{:S(2)}) collective-permute-start(bf16[384,384]{1,0:T(8,128)(2,1)} %get-tuple-element.230), channel_id=1, source_target_pairs={{0,8},{1,9},{2,10},{3,11},{4,12},{5,13},{6,14},{7,15},{8,0},{9,1},... | collective-permute-start | bytes 884744 | tf_op jit(solution)/shard_map/ppermute | solution.py:253
  249.2 32.5 %collective-permute-start.39 = (bf16[384,384]{1,0:T(8,128)(2,1)}, bf16[384,384]{1,0:T(8,128)(2,1)}, u32[]{:S(2)}, u32[]{:S(2)}) collective-permute-start(bf16[384,384]{1,0:T(8,128)(2,1)} %get-tuple-element.231), channel_id=1, source_target_pairs={{0,16},{1,17},{2,18},{3,19},{4,20},{5,21},{6,22},{7,23},{8,24},{9,... | collective-permute-start | bytes 884744 | tf_op jit(solution)/shard_map/ppermute | solution.py:253
  252.2 29.6 %collective-permute-start.40 = (bf16[384,384]{1,0:T(8,128)(2,1)}, bf16[384,384]{1,0:T(8,128)(2,1)}, u32[]{:S(2)}, u32[]{:S(2)}) collective-permute-start(bf16[384,384]{1,0:T(8,128)(2,1)} %get-tuple-element.232), channel_id=1, source_target_pairs={{0,24},{1,25},{2,26},{3,27},{4,28},{5,29},{6,30},{7,31},{8,16},{9,... | collective-permute-start | bytes 884744 | tf_op jit(solution)/shard_map/ppermute | solution.py:253
  283.0 27.0 %collective-permute-start.62 = (bf16[384,384]{1,0:T(8,128)(2,1)S(1)}, bf16[384,384]{1,0:T(8,128)(2,1)S(1)}, u32[]{:S(2)}, u32[]{:S(2)}) collective-permute-start(bf16[384,384]{1,0:T(8,128)(2,1)S(1)} %fusion.51), channel_id=1, source_target_pairs={{0,2},{1,3},{2,0},{3,1},{4,6},{5,7},{6,4},{7,5},{8,10},{9,11},{10,... | collective-permute-start | bytes 884744 | tf_op jit(solution)/shard_map/ppermute | solution.py:253
  305.6 19.1 %collective-permute-start.42 = (bf16[4,96,1152]{2,1,0:T(8,128)(2,1)S(1)}, bf16[4,96,1152]{2,1,0:T(8,128)(2,1)S(1)}, u32[]{:S(2)}, u32[]{:S(2)}) collective-permute-start(bf16[4,96,1152]{2,1,0:T(8,128)(2,1)S(1)} %copy-done.15), channel_id=1, source_target_pairs={{0,4},{1,5},{2,6},{3,7},{4,0},{5,1},{6,2},{7,3},{8,12},{9,13},{10,... | collective-permute-start | bytes 2654216 | tf_op jit(solution)/shard_map/ppermute | solution.py:253
  326.8 15.5 %collective-permute-start.57 = (bf16[96,1152]{1,0:T(8,128)(2,1)S(1)}, bf16[96,1152]{1,0:T(8,128)(2,1)S(1)}, u32[]{:S(2)}, u32[]{:S(2)}) collective-permute-start(bf16[96,1152]{1,0:T(8,128)(2,1)S(1)} %get-tuple-element.264), channel_id=1, source_target_pairs={{0,8},{1,9},{2,10},{3,11},{4,12},{5,13},{6,14},{7,15},{8,0},{9,1},... | collective-permute-start | bytes 663560 | tf_op jit(solution)/shard_map/ppermute | solution.py:253
  328.4 18.7 %collective-permute-start.58 = (bf16[96,1152]{1,0:T(8,128)(2,1)S(1)}, bf16[96,1152]{1,0:T(8,128)(2,1)S(1)}, u32[]{:S(2)}, u32[]{:S(2)}) collective-permute-start(bf16[96,1152]{1,0:T(8,128)(2,1)S(1)} %get-tuple-element.265), channel_id=1, source_target_pairs={{0,16},{1,17},{2,18},{3,19},{4,20},{5,21},{6,22},{7,23},{8,24},{9,... | collective-permute-start | bytes 663560 | tf_op jit(solution)/shard_map/ppermute | solution.py:253
  329.7 17.5 %collective-permute-start.59 = (bf16[96,1152]{1,0:T(8,128)(2,1)S(1)}, bf16[96,1152]{1,0:T(8,128)(2,1)S(1)}, u32[]{:S(2)}, u32[]{:S(2)}) collective-permute-start(bf16[96,1152]{1,0:T(8,128)(2,1)S(1)} %get-tuple-element.266), channel_id=1, source_target_pairs={{0,24},{1,25},{2,26},{3,27},{4,28},{5,29},{6,30},{7,31},{8,16},{9,... | collective-permute-start | bytes 663560 | tf_op jit(solution)/shard_map/ppermute | solution.py:253
  332.3 15.6 %collective-permute-start.44 = (bf16[8,48,384]{2,1,0:T(8,128)(2,1)S(1)}, bf16[8,48,384]{2,1,0:T(8,128)(2,1)S(1)}, u32[]{:S(2)}, u32[]{:S(2)}) collective-permute-start(bf16[8,48,384]{2,1,0:T(8,128)(2,1)S(1)} %get-tuple-element.252), channel_id=1, source_target_pairs={{0,2},{1,3},{2,0},{3,1},{4,6},{5,7},{6,4},{7,5},{8,10},{9,11},{10,... | collective-permute-start | bytes 884744 | tf_op jit(solution)/shard_map/ppermute | solution.py:253
  332.9 15.0 %collective-permute-start.45 = (bf16[4,48,768]{2,1,0:T(8,128)(2,1)S(1)}, bf16[4,48,768]{2,1,0:T(8,128)(2,1)S(1)}, u32[]{:S(2)}, u32[]{:S(2)}) collective-permute-start(bf16[4,48,768]{2,1,0:T(8,128)(2,1)S(1)} %fusion.55), channel_id=1, source_target_pairs={{0,4},{1,5},{2,6},{3,7},{4,0},{5,1},{6,2},{7,3},{8,12},{9,13},{10,... | collective-permute-start | bytes 884744 | tf_op jit(solution)/shard_map/ppermute | solution.py:253
  (85 other events, 619.0 us)
